TPU v7x, 128 devices: a whole 4x4x4 slice. The times are simulated.
128 devices in a mesh: section: 4 (over x_hi, core), dom: 32 (over z, y, x_lo).
Axes of the slice: x: 4 (x_hi: 2, x_lo: 2; x = x_hi * 2 + x_lo), y: 4, z: 4, core: 2. Of those that a mesh axis runs over, the one named last changes fastest.
Arguments:
- initial_features: bfloat16 [49152, 384], P('dom'), may hold values from -16 to 16
- layer_weights: bfloat16 [8, 384, 384], P('section'), may hold values from -0.3125 to 0.3125
- adjacency_tiles: bfloat16 [384, 24, 128, 128], P('dom'), may hold values from -0.15625 to 0.15625
- tile_columns: int32 [384, 24], P('dom'), may hold values from 0 to 107, as said below
- send_blocks: int32 [32, 3, 32], P('dom'), may hold values from -1 to 3, as said below
- stale_imports: bfloat16 [8, 32, 64, 128, 384], P('section', 'dom'), may hold values from 0 to 1.5
Outputs:
- final_features: bfloat16 [49152, 384], P('dom', 'section')
Inputs may be any that keep to these rules, and one draw needn't show every extreme that they name: send_blocks[q, h, p] is -1 when q equals p, else -1 or a block index of 0 to 3 within row group h. `tile_columns`: for a tile of partition p's local block r: a value j < 12 names p's own block j with j // 4 <= r // 4; a value 12 + h*32 + q names an import slot with send_blocks[q, h, p] >= 0.
All inputs are finite; a program needn't handle non-finite values.
Results may differ from a plain program's by a relative error of at most 0.011.
Values may be sent and summed in bfloat16 or wider, within the bound.
A program may use at most 256 MiB of HBM per device.

v0:
```python
import jax
import jax.numpy as jnp
from jax import lax
from jax.sharding import PartitionSpec as P

alpha_mix = 0.1
lambda_decay = 0.5


def shifted(value, axis, steps):
    count = lax.axis_size(axis)
    initial, last = (max(0, -steps), min(count, count - steps))
    return lax.ppermute(value, axis, [(source, source + steps) for source in range(initial, last)])


def broadcast(value, axis, source):
    kept = jnp.where(lax.axis_index(axis) == source, value, 0).astype(value.dtype)
    return lax.psum(kept, axis)


def gather_rows(table, columns, tile_rows):
    picked = table[columns]
    flat = picked.reshape(picked.shape[0], picked.shape[1] * picked.shape[2], picked.shape[3])
    return jnp.einsum("rim,rmd->rid", tile_rows, flat, preferred_element_type=jnp.float32)


def finish(summed, initial_rows, weight, beta_layer):
    mixed = ((1.0 - alpha_mix) * summed + alpha_mix * initial_rows.astype(jnp.float32)).astype(
        jnp.bfloat16
    )
    product = jnp.einsum("rid,de->rie", mixed, weight, preferred_element_type=jnp.float32)
    return jax.nn.relu(
        (1.0 - beta_layer) * mixed.astype(jnp.float32) + beta_layer * product
    ).astype(jnp.bfloat16)


def per_device(
    initial_features, layer_weights, adjacency_tiles, tile_columns, send_blocks, stale_imports
):
    segment_index = lax.axis_index("section")
    segment_count = lax.axis_size("section")
    part_count = lax.axis_size("dom")
    blocks_dev = adjacency_tiles.shape[0]
    fanout = adjacency_tiles.shape[1]
    block = adjacency_tiles.shape[2]
    width = initial_features.shape[1]
    groups = send_blocks.shape[1]
    group_blocks = blocks_dev // groups
    depth = layer_weights.shape[0]
    tile_rows_all = adjacency_tiles.transpose(0, 2, 1, 3).reshape(blocks_dev, block, fanout * block)
    initial_blocks = initial_features.reshape(blocks_dev, block, width)
    send_row = send_blocks[0]
    block_ids = jnp.arange(group_blocks, dtype=jnp.int32)
    turns = groups + segment_count - 1

    def turn(position, carry):
        inbox, owned, imported, results = carry
        group_index = position - segment_index
        active = (group_index >= 0) & (group_index < groups)
        current = jnp.clip(group_index, 0, groups - 1)
        first_row = current * group_blocks
        initial_rows = lax.dynamic_slice_in_dim(initial_blocks, first_row, group_blocks, 0)
        columns = lax.dynamic_slice_in_dim(tile_columns, first_row, group_blocks, 0)
        tile_rows = lax.dynamic_slice_in_dim(tile_rows_all, first_row, group_blocks, 0)
        features = jnp.where(segment_index == 0, initial_rows, inbox)
        picks = send_row[current]
        selector = (picks[:, None] == block_ids[None, :]).astype(jnp.bfloat16)
        owned_next = []
        imported_next = []
        for sublayer in range(depth):
            weight = layer_weights[sublayer]
            beta_layer = jnp.log(
                lambda_decay / (depth * segment_index + sublayer + 1).astype(jnp.float32) + 1.0
            )
            own_table = owned[sublayer]
            kept_rows = lax.dynamic_slice_in_dim(own_table, first_row, group_blocks, 0)
            own_table = lax.dynamic_update_slice_in_dim(
                own_table, jnp.where(active, features, kept_rows), first_row, 0
            )
            stale_table = imported[sublayer]
            outgoing = jnp.einsum(
                "eb,bid->eid", selector, features, preferred_element_type=jnp.float32
            ).astype(jnp.bfloat16)
            received = lax.all_to_all(outgoing, "dom", split_axis=0, concat_axis=0, tiled=True)
            kept_slots = lax.dynamic_slice_in_dim(stale_table, current * part_count, part_count, 0)
            stale_table = lax.dynamic_update_slice_in_dim(
                stale_table, jnp.where(active, received, kept_slots), current * part_count, 0
            )
            table = jnp.concatenate([own_table, stale_table], 0)
            features = lax.cond(
                active,
                lambda: finish(
                    gather_rows(table, columns, tile_rows), initial_rows, weight, beta_layer
                ),
                lambda: features,
            )
            owned_next.append(own_table)
            imported_next.append(stale_table)
        kept_out = lax.dynamic_slice_in_dim(results, first_row, group_blocks, 0)
        results = lax.dynamic_update_slice_in_dim(
            results, jnp.where(active, features, kept_out), first_row, 0
        )
        inbox = shifted(features, "section", 1)
        return (inbox, jnp.stack(owned_next), jnp.stack(imported_next), results)

    start_carry = (
        jnp.zeros((group_blocks, block, width), jnp.bfloat16),
        jnp.zeros((depth, blocks_dev, block, width), jnp.bfloat16),
        jnp.concatenate(
            [jnp.zeros((depth, part_count, block, width), jnp.bfloat16), stale_imports[:, 0]], 1
        ),
        jnp.zeros((blocks_dev, block, width), jnp.bfloat16),
    )
    final_carry = lax.fori_loop(0, turns, turn, start_carry)
    finished = final_carry[3].reshape(blocks_dev * block, width)
    column_count = width // segment_count
    whole = broadcast(finished, "section", segment_count - 1)
    return lax.dynamic_slice_in_dim(whole, segment_index * column_count, column_count, 1)


def solution(mesh):
    return jax.shard_map(
        per_device,
        mesh=mesh,
        in_specs=(
            P("dom", None),
            P("section", None, None),
            P("dom", None, None, None),
            P("dom", None),
            P("dom", None, None),
            P("section", "dom", None, None, None),
        ),
        out_specs=P("dom", "section"),
        check_vma=False,
    )
```

profile of v0, /device:TPU:1, one launch (start us, length us, event | category | flops | bytes accessed | tf_op | source)
XLA Modules:
  0.0 1157.4 jit_solution(420370258129279811)
XLA Ops:
  16.3 14.5 %concatenate.21 = bf16[2,96,128,384]{3,2,1,0:T(8,128)(2,1)} pad(bf16[2,64,128,384]{3,2,1,0:T(8,128)(2,1)} %bitcast.104, bf16[]{:T(256)} %constant.147.clone.1), padding=0_0x32_0x0_0x0_0 | pad | bytes 31457282 | tf_op jit(solution)/shard_map/concatenate | solution.py:109
  33.2 1064.2 %while.22 = (s32[]{:T(128)}, bf16[4,128,384]{1,2,0:T(8,128)(2,1)}, bf16[2,12,128,384]{3,2,1,0:T(8,128)(2,1)S(1)}, bf16[2,96,128,384]{3,2,1,0:T(8,128)(2,1)}, bf1...) while((s32[]{:T(128)}, bf16[4,128,384]{1,2,0:T(8,128)(2,1)}, ...), condition=%wide.region_5.6_spmd.clone, body=%wide.region_0.5_spmd.clone.sunk | while | flops 2775714560 | bytes 348601984 | solution.py:114
  62.8 19.6 %fusion.51 = (bf16[1,96,128,384]{3,2,1,0:T(8,128)(2,1)}, bf16[96,128,384]{2,1,0:T(8,128)(2,1)}, bf16[96,128,384]{2,1,0:T(8,128)(2,1)}, bf16[1,96,128,384]{3,2,1,0:T(8,128)(2,1)}) fusion(bf16[2,96,128,384]{3,2,1,0:T(8,128)(2,1)} %get-tuple-element.597), kind=kLoop, calls=%fused_computation.64.clone.1 | loop fusion | bytes 56623104 | tf_op jit(solution)/shard_map/while/body/eval_jaxpr/slice | solution.py:80
  82.3 17.5 %all-to-all-done = bf16[32,128,384]{2,1,0:T(8,128)(2,1)S(1)} async-done(((bf16[32,128,384]{2,1,0:T(8,128)(2,1)}), bf16[32,128,384]{2,1,0:T(8,128)(2,1)S(1)}, u32[]{:S(2)}, u32[]{:S(2)}) %all-to-all-start) | async-done | bytes 3145760 | tf_op jit(solution)/shard_map/while/body/eval_jaxpr/all_to_all | solution.py:84
  104.6 10.8 pad_maximum_fusion.8
  159.1 10.8 pad_maximum_fusion.9
  169.9 15.6 %collective-permute-start = (bf16[4,128,384]{1,2,0:T(8,128)(2,1)S(1)}, bf16[4,128,384]{1,2,0:T(8,128)(2,1)}, u32[]{:S(2)}, u32[]{:S(2)}) collective-permute-start(bf16[4,128,384]{1,2,0:T(8,128)(2,1)S(1)} %get-tuple-element.639), channel_id=1, source_target_pairs={{0,32},{32,64},{64,96},{1,33},{33,65},{65,97},{2,34},{34,66},{66,9... | collective-permute-start | bytes 1179656 | tf_op jit(solution)/shard_map/while/body/eval_jaxpr/ppermute | solution.py:13
  185.5 16.8 %pad_maximum_fusion.11 = bf16[2,96,128,384]{3,2,1,0:T(8,128)(2,1)} fusion(bf16[1,96,128,384]{3,2,1,0:T(8,128)(2,1)} %bitcast.98, bf16[1,96,128,384]{3,2,1,0:T(8,128)(2,1)} %bitcast.99), kind=kLoop, calls=%fused_computation.27.clone.1 | loop fusion | flops 9437184 | bytes 37748736 | tf_op jit(solution)/shard_map/while/body/eval_jaxpr/stack | solution.py:104
  203.4 14.5 %collective-permute-done = bf16[4,128,384]{1,2,0:T(8,128)(2,1)} collective-permute-done((bf16[4,128,384]{1,2,0:T(8,128)(2,1)S(1)}, bf16[4,128,384]{1,2,0:T(8,128)(2,1)}, u32[]{:S(2)}, u32[]{:S(2)}) %collective-permute-start) | collective-permute-done | bytes 393248 | tf_op jit(solution)/shard_map/while/body/eval_jaxpr/ppermute | solution.py:13
  242.4 19.6 %fusion.51 = (bf16[1,96,128,384]{3,2,1,0:T(8,128)(2,1)}, bf16[96,128,384]{2,1,0:T(8,128)(2,1)}, bf16[96,128,384]{2,1,0:T(8,128)(2,1)}, bf16[1,96,128,384]{3,2,1,0:T(8,128)(2,1)}) fusion(bf16[2,96,128,384]{3,2,1,0:T(8,128)(2,1)} %get-tuple-element.597), kind=kLoop, calls=%fused_computation.64.clone.1 | loop fusion | bytes 56623104 | tf_op jit(solution)/shard_map/while/body/eval_jaxpr/slice | solution.py:80
  266.7 10.8 pad_maximum_fusion.8
  277.5 21.4 %conditional.6 = (bf16[4,128,384]{1,2,0:T(8,128)(2,1)S(1)}) conditional(s32[]{:T(128)} %convert_element_type.95, bf16[4,128,384]{1,2,0:T(8,128)(2,1)S(1)} %get-tuple-element.563, (f32[]{:T(128)}, s32[4,24]{1,0:T(4,128)S(1)}, bf16[108,128,384]{2,1,0:T(8,128)(2,1)}, bf16[4,128,3072]{2,1,0:T(8,128)(2,1)S(1)}, bf16[4,128,384]{1,2,0:T(8,128)(2,1)}, ...), branch_computations={%region_1.1_spmd, %region_2.2_spmd} | conditional | flops 1361118464 | bytes 35298100 | solution.py:90
  277.6 11.9 %gather_fusion = bf16[96,128,384]{2,1,0:T(8,128)(2,1)} fusion(bf16[108,128,384]{2,1,0:T(8,128)(2,1)} %get-tuple-element.334, s32[1024]{0:T(1024)S(1)} %pad_clamp_fusion), kind=kCustom, calls=%fused_computation | custom fusion | bytes 18874752 | tf_op jit(solution)/shard_map/while/body/eval_jaxpr/cond/branch_1_fun/gather | solution.py:22
  325.1 11.7 %all-to-all-done.1 = bf16[32,128,384]{2,1,0:T(8,128)(2,1)S(1)} async-done(((bf16[32,128,384]{2,1,0:T(8,128)(2,1)}), bf16[32,128,384]{2,1,0:T(8,128)(2,1)S(1)}, u32[]{:S(2)}, u32[]{:S(2)}) %all-to-all-start.1) | async-done | bytes 3145760 | tf_op jit(solution)/shard_map/while/body/eval_jaxpr/all_to_all | solution.py:84
  341.5 10.8 pad_maximum_fusion.9
  352.3 21.5 %conditional.7 = (bf16[4,128,384]{1,2,0:T(8,128)(2,1)S(1)}) conditional(s32[]{:T(128)} %convert_element_type.95, bf16[4,128,384]{1,2,0:T(8,128)(2,1)S(1)} %get-tuple-element.638, (f32[]{:T(128)}, s32[4,24]{1,0:T(4,128)S(1)}, bf16[108,128,384]{2,1,0:T(8,128)(2,1)}, bf16[4,128,3072]{2,1,0:T(8,128)(2,1)S(1)}, bf16[4,128,384]{1,2,0:T(8,128)(2,1)}, ...), branch_computations={%region_3.3_spmd, %region_4.4_spmd} | conditional | flops 1361118464 | bytes 35298100 | solution.py:90
  352.4 12.0 %gather_fusion.1 = bf16[96,128,384]{2,1,0:T(8,128)(2,1)} fusion(bf16[108,128,384]{2,1,0:T(8,128)(2,1)} %get-tuple-element.340, s32[1024]{0:T(1024)S(1)} %pad_clamp_fusion.1), kind=kCustom, calls=%fused_computation.1 | custom fusion | bytes 18874752 | tf_op jit(solution)/shard_map/while/body/eval_jaxpr/cond/branch_1_fun/gather | solution.py:22
  375.7 16.8 %pad_maximum_fusion.11 = bf16[2,96,128,384]{3,2,1,0:T(8,128)(2,1)} fusion(bf16[1,96,128,384]{3,2,1,0:T(8,128)(2,1)} %bitcast.98, bf16[1,96,128,384]{3,2,1,0:T(8,128)(2,1)} %bitcast.99), kind=kLoop, calls=%fused_computation.27.clone.1 | loop fusion | flops 9437184 | bytes 37748736 | tf_op jit(solution)/shard_map/while/body/eval_jaxpr/stack | solution.py:104
  420.9 19.6 %fusion.51 = (bf16[1,96,128,384]{3,2,1,0:T(8,128)(2,1)}, bf16[96,128,384]{2,1,0:T(8,128)(2,1)}, bf16[96,128,384]{2,1,0:T(8,128)(2,1)}, bf16[1,96,128,384]{3,2,1,0:T(8,128)(2,1)}) fusion(bf16[2,96,128,384]{3,2,1,0:T(8,128)(2,1)} %get-tuple-element.597), kind=kLoop, calls=%fused_computation.64.clone.1 | loop fusion | bytes 56623104 | tf_op jit(solution)/shard_map/while/body/eval_jaxpr/slice | solution.py:80
  445.2 10.8 pad_maximum_fusion.8
  456.0 21.4 %conditional.6 = (bf16[4,128,384]{1,2,0:T(8,128)(2,1)S(1)}) conditional(s32[]{:T(128)} %convert_element_type.95, bf16[4,128,384]{1,2,0:T(8,128)(2,1)S(1)} %get-tuple-element.563, (f32[]{:T(128)}, s32[4,24]{1,0:T(4,128)S(1)}, bf16[108,128,384]{2,1,0:T(8,128)(2,1)}, bf16[4,128,3072]{2,1,0:T(8,128)(2,1)S(1)}, bf16[4,128,384]{1,2,0:T(8,128)(2,1)}, ...), branch_computations={%region_1.1_spmd, %region_2.2_spmd} | conditional | flops 1361118464 | bytes 35298100 | solution.py:90
  456.1 11.9 %gather_fusion = bf16[96,128,384]{2,1,0:T(8,128)(2,1)} fusion(bf16[108,128,384]{2,1,0:T(8,128)(2,1)} %get-tuple-element.334, s32[1024]{0:T(1024)S(1)} %pad_clamp_fusion), kind=kCustom, calls=%fused_computation | custom fusion | bytes 18874752 | tf_op jit(solution)/shard_map/while/body/eval_jaxpr/cond/branch_1_fun/gather | solution.py:22
  503.5 11.9 %all-to-all-done.1 = bf16[32,128,384]{2,1,0:T(8,128)(2,1)S(1)} async-done(((bf16[32,128,384]{2,1,0:T(8,128)(2,1)}), bf16[32,128,384]{2,1,0:T(8,128)(2,1)S(1)}, u32[]{:S(2)}, u32[]{:S(2)}) %all-to-all-start.1) | async-done | bytes 3145760 | tf_op jit(solution)/shard_map/while/body/eval_jaxpr/all_to_all | solution.py:84
  520.2 10.8 pad_maximum_fusion.9
  531.0 21.5 %conditional.7 = (bf16[4,128,384]{1,2,0:T(8,128)(2,1)S(1)}) conditional(s32[]{:T(128)} %convert_element_type.95, bf16[4,128,384]{1,2,0:T(8,128)(2,1)S(1)} %get-tuple-element.638, (f32[]{:T(128)}, s32[4,24]{1,0:T(4,128)S(1)}, bf16[108,128,384]{2,1,0:T(8,128)(2,1)}, bf16[4,128,3072]{2,1,0:T(8,128)(2,1)S(1)}, bf16[4,128,384]{1,2,0:T(8,128)(2,1)}, ...), branch_computations={%region_3.3_spmd, %region_4.4_spmd} | conditional | flops 1361118464 | bytes 35298100 | solution.py:90
  531.1 12.0 %gather_fusion.1 = bf16[96,128,384]{2,1,0:T(8,128)(2,1)} fusion(bf16[108,128,384]{2,1,0:T(8,128)(2,1)} %get-tuple-element.340, s32[1024]{0:T(1024)S(1)} %pad_clamp_fusion.1), kind=kCustom, calls=%fused_computation.1 | custom fusion | bytes 18874752 | tf_op jit(solution)/shard_map/while/body/eval_jaxpr/cond/branch_1_fun/gather | solution.py:22
  554.5 16.8 %pad_maximum_fusion.11 = bf16[2,96,128,384]{3,2,1,0:T(8,128)(2,1)} fusion(bf16[1,96,128,384]{3,2,1,0:T(8,128)(2,1)} %bitcast.98, bf16[1,96,128,384]{3,2,1,0:T(8,128)(2,1)} %bitcast.99), kind=kLoop, calls=%fused_computation.27.clone.1 | loop fusion | flops 9437184 | bytes 37748736 | tf_op jit(solution)/shard_map/while/body/eval_jaxpr/stack | solution.py:104
  599.5 19.6 %fusion.51 = (bf16[1,96,128,384]{3,2,1,0:T(8,128)(2,1)}, bf16[96,128,384]{2,1,0:T(8,128)(2,1)}, bf16[96,128,384]{2,1,0:T(8,128)(2,1)}, bf16[1,96,128,384]{3,2,1,0:T(8,128)(2,1)}) fusion(bf16[2,96,128,384]{3,2,1,0:T(8,128)(2,1)} %get-tuple-element.597), kind=kLoop, calls=%fused_computation.64.clone.1 | loop fusion | bytes 56623104 | tf_op jit(solution)/shard_map/while/body/eval_jaxpr/slice | solution.py:80
  623.8 10.8 pad_maximum_fusion.8
  634.6 21.4 %conditional.6 = (bf16[4,128,384]{1,2,0:T(8,128)(2,1)S(1)}) conditional(s32[]{:T(128)} %convert_element_type.95, bf16[4,128,384]{1,2,0:T(8,128)(2,1)S(1)} %get-tuple-element.563, (f32[]{:T(128)}, s32[4,24]{1,0:T(4,128)S(1)}, bf16[108,128,384]{2,1,0:T(8,128)(2,1)}, bf16[4,128,3072]{2,1,0:T(8,128)(2,1)S(1)}, bf16[4,128,384]{1,2,0:T(8,128)(2,1)}, ...), branch_computations={%region_1.1_spmd, %region_2.2_spmd} | conditional | flops 1361118464 | bytes 35298100 | solution.py:90
  634.7 11.9 %gather_fusion = bf16[96,128,384]{2,1,0:T(8,128)(2,1)} fusion(bf16[108,128,384]{2,1,0:T(8,128)(2,1)} %get-tuple-element.334, s32[1024]{0:T(1024)S(1)} %pad_clamp_fusion), kind=kCustom, calls=%fused_computation | custom fusion | bytes 18874752 | tf_op jit(solution)/shard_map/while/body/eval_jaxpr/cond/branch_1_fun/gather | solution.py:22
  682.2 23.4 %all-to-all-done.1 = bf16[32,128,384]{2,1,0:T(8,128)(2,1)S(1)} async-done(((bf16[32,128,384]{2,1,0:T(8,128)(2,1)}), bf16[32,128,384]{2,1,0:T(8,128)(2,1)S(1)}, u32[]{:S(2)}, u32[]{:S(2)}) %all-to-all-start.1) | async-done | bytes 3145760 | tf_op jit(solution)/shard_map/while/body/eval_jaxpr/all_to_all | solution.py:84
  710.4 10.8 pad_maximum_fusion.9
  721.2 21.5 %conditional.7 = (bf16[4,128,384]{1,2,0:T(8,128)(2,1)S(1)}) conditional(s32[]{:T(128)} %convert_element_type.95, bf16[4,128,384]{1,2,0:T(8,128)(2,1)S(1)} %get-tuple-element.638, (f32[]{:T(128)}, s32[4,24]{1,0:T(4,128)S(1)}, bf16[108,128,384]{2,1,0:T(8,128)(2,1)}, bf16[4,128,3072]{2,1,0:T(8,128)(2,1)S(1)}, bf16[4,128,384]{1,2,0:T(8,128)(2,1)}, ...), branch_computations={%region_3.3_spmd, %region_4.4_spmd} | conditional | flops 1361118464 | bytes 35298100 | solution.py:90
  721.3 12.0 %gather_fusion.1 = bf16[96,128,384]{2,1,0:T(8,128)(2,1)} fusion(bf16[108,128,384]{2,1,0:T(8,128)(2,1)} %get-tuple-element.340, s32[1024]{0:T(1024)S(1)} %pad_clamp_fusion.1), kind=kCustom, calls=%fused_computation.1 | custom fusion | bytes 18874752 | tf_op jit(solution)/shard_map/while/body/eval_jaxpr/cond/branch_1_fun/gather | solution.py:22
  744.7 16.8 %pad_maximum_fusion.11 = bf16[2,96,128,384]{3,2,1,0:T(8,128)(2,1)} fusion(bf16[1,96,128,384]{3,2,1,0:T(8,128)(2,1)} %bitcast.98, bf16[1,96,128,384]{3,2,1,0:T(8,128)(2,1)} %bitcast.99), kind=kLoop, calls=%fused_computation.27.clone.1 | loop fusion | flops 9437184 | bytes 37748736 | tf_op jit(solution)/shard_map/while/body/eval_jaxpr/stack | solution.py:104
  787.9 19.6 %fusion.51 = (bf16[1,96,128,384]{3,2,1,0:T(8,128)(2,1)}, bf16[96,128,384]{2,1,0:T(8,128)(2,1)}, bf16[96,128,384]{2,1,0:T(8,128)(2,1)}, bf16[1,96,128,384]{3,2,1,0:T(8,128)(2,1)}) fusion(bf16[2,96,128,384]{3,2,1,0:T(8,128)(2,1)} %get-tuple-element.597), kind=kLoop, calls=%fused_computation.64.clone.1 | loop fusion | bytes 56623104 | tf_op jit(solution)/shard_map/while/body/eval_jaxpr/slice | solution.py:80
  807.5 15.6 %all-to-all-done = bf16[32,128,384]{2,1,0:T(8,128)(2,1)S(1)} async-done(((bf16[32,128,384]{2,1,0:T(8,128)(2,1)}), bf16[32,128,384]{2,1,0:T(8,128)(2,1)S(1)}, u32[]{:S(2)}, u32[]{:S(2)}) %all-to-all-start) | async-done | bytes 3145760 | tf_op jit(solution)/shard_map/while/body/eval_jaxpr/all_to_all | solution.py:84
  827.8 10.8 pad_maximum_fusion.8
  864.8 26.8 %all-to-all-done.1 = bf16[32,128,384]{2,1,0:T(8,128)(2,1)S(1)} async-done(((bf16[32,128,384]{2,1,0:T(8,128)(2,1)}), bf16[32,128,384]{2,1,0:T(8,128)(2,1)S(1)}, u32[]{:S(2)}, u32[]{:S(2)}) %all-to-all-start.1) | async-done | bytes 3145760 | tf_op jit(solution)/shard_map/while/body/eval_jaxpr/all_to_all | solution.py:84
  896.5 10.8 pad_maximum_fusion.9
  913.9 16.8 %pad_maximum_fusion.11 = bf16[2,96,128,384]{3,2,1,0:T(8,128)(2,1)} fusion(bf16[1,96,128,384]{3,2,1,0:T(8,128)(2,1)} %bitcast.98, bf16[1,96,128,384]{3,2,1,0:T(8,128)(2,1)} %bitcast.99), kind=kLoop, calls=%fused_computation.27.clone.1 | loop fusion | flops 9437184 | bytes 37748736 | tf_op jit(solution)/shard_map/while/body/eval_jaxpr/stack | solution.py:104
  955.7 19.6 %fusion.51 = (bf16[1,96,128,384]{3,2,1,0:T(8,128)(2,1)}, bf16[96,128,384]{2,1,0:T(8,128)(2,1)}, bf16[96,128,384]{2,1,0:T(8,128)(2,1)}, bf16[1,96,128,384]{3,2,1,0:T(8,128)(2,1)}) fusion(bf16[2,96,128,384]{3,2,1,0:T(8,128)(2,1)} %get-tuple-element.597), kind=kLoop, calls=%fused_computation.64.clone.1 | loop fusion | bytes 56623104 | tf_op jit(solution)/shard_map/while/body/eval_jaxpr/slice | solution.py:80
  975.3 14.1 %all-to-all-done = bf16[32,128,384]{2,1,0:T(8,128)(2,1)S(1)} async-done(((bf16[32,128,384]{2,1,0:T(8,128)(2,1)}), bf16[32,128,384]{2,1,0:T(8,128)(2,1)S(1)}, u32[]{:S(2)}, u32[]{:S(2)}) %all-to-all-start) | async-done | bytes 3145760 | tf_op jit(solution)/shard_map/while/body/eval_jaxpr/all_to_all | solution.py:84
  1030.9 31.0 %all-to-all-done.1 = bf16[32,128,384]{2,1,0:T(8,128)(2,1)S(1)} async-done(((bf16[32,128,384]{2,1,0:T(8,128)(2,1)}), bf16[32,128,384]{2,1,0:T(8,128)(2,1)S(1)}, u32[]{:S(2)}, u32[]{:S(2)}) %all-to-all-start.1) | async-done | bytes 3145760 | tf_op jit(solution)/shard_map/while/body/eval_jaxpr/all_to_all | solution.py:84
  1066.8 10.8 pad_maximum_fusion.9
  1079.5 16.8 %pad_maximum_fusion.11 = bf16[2,96,128,384]{3,2,1,0:T(8,128)(2,1)} fusion(bf16[1,96,128,384]{3,2,1,0:T(8,128)(2,1)} %bitcast.98, bf16[1,96,128,384]{3,2,1,0:T(8,128)(2,1)} %bitcast.99), kind=kLoop, calls=%fused_computation.27.clone.1 | loop fusion | flops 9437184 | bytes 37748736 | tf_op jit(solution)/shard_map/while/body/eval_jaxpr/stack | solution.py:104
  1098.6 49.7 %all-reduce.3.cloned.1.call-done = bf16[1536,384]{1,0:T(8,128)(2,1)} async-done(((bf16[1536,384]{1,0:T(8,128)(2,1)}), bf16[1536,384]{1,0:T(8,128)(2,1)}) %all-reduce.3.cloned.1.call-update) | async-done | bytes 1179664 | tf_op jit(solution)/shard_map/psum | solution.py:18
  (343 shorter events, 488.0 us)
Async XLA Ops:
  6.5 1141.8 %all-reduce.3.cloned.1.call-start = ((), (), s32[]{:S(2)}) async-start(), calls=%async_computation.2 | async-start | bytes 2359296 | tf_op jit(solution)/shard_map/psum | solution.py:18
  44.8 55.0 %all-to-all-start = ((bf16[32,128,384]{2,1,0:T(8,128)(2,1)}), bf16[32,128,384]{2,1,0:T(8,128)(2,1)S(1)}, u32[]{:S(2)}, u32[]{:S(2)}) async-start(bf16[32,128,384]{2,1,0:T(8,128)(2,1)} %copy.95), calls=%async_computation | async-start | bytes 6291456 | tf_op jit(solution)/shard_map/while/body/eval_jaxpr/all_to_all | solution.py:84
  104.6 10.8 copy-start.3
  119.4 34.9 %all-to-all-start.1 = ((bf16[32,128,384]{2,1,0:T(8,128)(2,1)}), bf16[32,128,384]{2,1,0:T(8,128)(2,1)S(1)}, u32[]{:S(2)}, u32[]{:S(2)}) async-start(bf16[32,128,384]{2,1,0:T(8,128)(2,1)} %copy.98), calls=%async_computation.1 | async-start | bytes 6291456 | tf_op jit(solution)/shard_map/while/body/eval_jaxpr/all_to_all | solution.py:84
  159.1 10.8 copy-start.4
  169.9 48.0 %collective-permute-start = (bf16[4,128,384]{1,2,0:T(8,128)(2,1)S(1)}, bf16[4,128,384]{1,2,0:T(8,128)(2,1)}, u32[]{:S(2)}, u32[]{:S(2)}) collective-permute-start(bf16[4,128,384]{1,2,0:T(8,128)(2,1)S(1)} %get-tuple-element.639), channel_id=1, source_target_pairs={{0,32},{32,64},{64,96},{1,33},{33,65},{65,97},{2,34},{34,66},{66,9... | collective-permute-start | bytes 1179656 | tf_op jit(solution)/shard_map/while/body/eval_jaxpr/ppermute | solution.py:13
  185.5 16.8 %copy-start.8 = (bf16[4,128,384]{1,2,0:T(8,128)(2,1)S(1)}, bf16[4,128,384]{1,2,0:T(8,128)(2,1)}, u32[]{:S(2)}) copy-start(bf16[4,128,384]{1,2,0:T(8,128)(2,1)} %copy.101) | copy-start | bytes 1179652 | tf_op jit(solution)/shard_map/while
  185.5 32.4 %copy-start.2 = (bf16[2,12,128,384]{3,2,1,0:T(8,128)(2,1)S(1)}, bf16[2,12,128,384]{3,2,1,0:T(8,128)(2,1)}, u32[]{:S(2)}) copy-start(bf16[2,12,128,384]{3,2,1,0:T(8,128)(2,1)} %pad_maximum_fusion.10) | copy-start | bytes 7077892 | tf_op jit(solution)/shard_map/while
  229.5 32.5 %all-to-all-start = ((bf16[32,128,384]{2,1,0:T(8,128)(2,1)}), bf16[32,128,384]{2,1,0:T(8,128)(2,1)S(1)}, u32[]{:S(2)}, u32[]{:S(2)}) async-start(bf16[32,128,384]{2,1,0:T(8,128)(2,1)} %copy.95), calls=%async_computation | async-start | bytes 6291456 | tf_op jit(solution)/shard_map/while/body/eval_jaxpr/all_to_all | solution.py:84
  266.7 10.8 copy-start.3
  277.6 11.9 %copy-start.6 = (bf16[4,128,384]{1,2,0:T(8,128)(2,1)S(1)}, bf16[4,128,384]{1,2,0:T(8,128)(2,1)}, u32[]{:S(2)}) copy-start(bf16[4,128,384]{1,2,0:T(8,128)(2,1)} %get-tuple-element.337) | copy-start | bytes 1179652 | tf_op jit(solution)/shard_map/while/body/eval_jaxpr/cond
  302.9 33.8 %all-to-all-start.1 = ((bf16[32,128,384]{2,1,0:T(8,128)(2,1)}), bf16[32,128,384]{2,1,0:T(8,128)(2,1)S(1)}, u32[]{:S(2)}, u32[]{:S(2)}) async-start(bf16[32,128,384]{2,1,0:T(8,128)(2,1)} %copy.98), calls=%async_computation.1 | async-start | bytes 6291456 | tf_op jit(solution)/shard_map/while/body/eval_jaxpr/all_to_all | solution.py:84
  341.5 10.8 copy-start.4
  352.4 12.0 %copy-start.7 = (bf16[4,128,384]{1,2,0:T(8,128)(2,1)S(1)}, bf16[4,128,384]{1,2,0:T(8,128)(2,1)}, u32[]{:S(2)}) copy-start(bf16[4,128,384]{1,2,0:T(8,128)(2,1)} %get-tuple-element.343) | copy-start | bytes 1179652 | tf_op jit(solution)/shard_map/while/body/eval_jaxpr/cond
  373.8 23.2 %collective-permute-start = (bf16[4,128,384]{1,2,0:T(8,128)(2,1)S(1)}, bf16[4,128,384]{1,2,0:T(8,128)(2,1)}, u32[]{:S(2)}, u32[]{:S(2)}) collective-permute-start(bf16[4,128,384]{1,2,0:T(8,128)(2,1)S(1)} %get-tuple-element.639), channel_id=1, source_target_pairs={{0,32},{32,64},{64,96},{1,33},{33,65},{65,97},{2,34},{34,66},{66,9... | collective-permute-start | bytes 1179656 | tf_op jit(solution)/shard_map/while/body/eval_jaxpr/ppermute | solution.py:13
  375.7 16.8 %copy-start.8 = (bf16[4,128,384]{1,2,0:T(8,128)(2,1)S(1)}, bf16[4,128,384]{1,2,0:T(8,128)(2,1)}, u32[]{:S(2)}) copy-start(bf16[4,128,384]{1,2,0:T(8,128)(2,1)} %copy.101) | copy-start | bytes 1179652 | tf_op jit(solution)/shard_map/while
  375.7 21.3 %copy-start.2 = (bf16[2,12,128,384]{3,2,1,0:T(8,128)(2,1)S(1)}, bf16[2,12,128,384]{3,2,1,0:T(8,128)(2,1)}, u32[]{:S(2)}) copy-start(bf16[2,12,128,384]{3,2,1,0:T(8,128)(2,1)} %pad_maximum_fusion.10) | copy-start | bytes 7077892 | tf_op jit(solution)/shard_map/while
  408.6 31.8 %all-to-all-start = ((bf16[32,128,384]{2,1,0:T(8,128)(2,1)}), bf16[32,128,384]{2,1,0:T(8,128)(2,1)S(1)}, u32[]{:S(2)}, u32[]{:S(2)}) async-start(bf16[32,128,384]{2,1,0:T(8,128)(2,1)} %copy.95), calls=%async_computation | async-start | bytes 6291456 | tf_op jit(solution)/shard_map/while/body/eval_jaxpr/all_to_all | solution.py:84
  445.2 10.8 copy-start.3
  456.1 11.9 %copy-start.6 = (bf16[4,128,384]{1,2,0:T(8,128)(2,1)S(1)}, bf16[4,128,384]{1,2,0:T(8,128)(2,1)}, u32[]{:S(2)}) copy-start(bf16[4,128,384]{1,2,0:T(8,128)(2,1)} %get-tuple-element.337) | copy-start | bytes 1179652 | tf_op jit(solution)/shard_map/while/body/eval_jaxpr/cond
  481.5 34.0 %all-to-all-start.1 = ((bf16[32,128,384]{2,1,0:T(8,128)(2,1)}), bf16[32,128,384]{2,1,0:T(8,128)(2,1)S(1)}, u32[]{:S(2)}, u32[]{:S(2)}) async-start(bf16[32,128,384]{2,1,0:T(8,128)(2,1)} %copy.98), calls=%async_computation.1 | async-start | bytes 6291456 | tf_op jit(solution)/shard_map/while/body/eval_jaxpr/all_to_all | solution.py:84
  520.2 10.8 copy-start.4
  531.1 12.0 %copy-start.7 = (bf16[4,128,384]{1,2,0:T(8,128)(2,1)S(1)}, bf16[4,128,384]{1,2,0:T(8,128)(2,1)}, u32[]{:S(2)}) copy-start(bf16[4,128,384]{1,2,0:T(8,128)(2,1)} %get-tuple-element.343) | copy-start | bytes 1179652 | tf_op jit(solution)/shard_map/while/body/eval_jaxpr/cond
  552.5 23.1 %collective-permute-start = (bf16[4,128,384]{1,2,0:T(8,128)(2,1)S(1)}, bf16[4,128,384]{1,2,0:T(8,128)(2,1)}, u32[]{:S(2)}, u32[]{:S(2)}) collective-permute-start(bf16[4,128,384]{1,2,0:T(8,128)(2,1)S(1)} %get-tuple-element.639), channel_id=1, source_target_pairs={{0,32},{32,64},{64,96},{1,33},{33,65},{65,97},{2,34},{34,66},{66,9... | collective-permute-start | bytes 1179656 | tf_op jit(solution)/shard_map/while/body/eval_jaxpr/ppermute | solution.py:13
  554.5 16.8 %copy-start.8 = (bf16[4,128,384]{1,2,0:T(8,128)(2,1)S(1)}, bf16[4,128,384]{1,2,0:T(8,128)(2,1)}, u32[]{:S(2)}) copy-start(bf16[4,128,384]{1,2,0:T(8,128)(2,1)} %copy.101) | copy-start | bytes 1179652 | tf_op jit(solution)/shard_map/while
  554.5 21.2 %copy-start.2 = (bf16[2,12,128,384]{3,2,1,0:T(8,128)(2,1)S(1)}, bf16[2,12,128,384]{3,2,1,0:T(8,128)(2,1)}, u32[]{:S(2)}) copy-start(bf16[2,12,128,384]{3,2,1,0:T(8,128)(2,1)} %pad_maximum_fusion.10) | copy-start | bytes 7077892 | tf_op jit(solution)/shard_map/while
  587.3 31.8 %all-to-all-start = ((bf16[32,128,384]{2,1,0:T(8,128)(2,1)}), bf16[32,128,384]{2,1,0:T(8,128)(2,1)S(1)}, u32[]{:S(2)}, u32[]{:S(2)}) async-start(bf16[32,128,384]{2,1,0:T(8,128)(2,1)} %copy.95), calls=%async_computation | async-start | bytes 6291456 | tf_op jit(solution)/shard_map/while/body/eval_jaxpr/all_to_all | solution.py:84
  623.8 10.8 copy-start.3
  634.7 11.9 %copy-start.6 = (bf16[4,128,384]{1,2,0:T(8,128)(2,1)S(1)}, bf16[4,128,384]{1,2,0:T(8,128)(2,1)}, u32[]{:S(2)}) copy-start(bf16[4,128,384]{1,2,0:T(8,128)(2,1)} %get-tuple-element.337) | copy-start | bytes 1179652 | tf_op jit(solution)/shard_map/while/body/eval_jaxpr/cond
  660.1 45.5 %all-to-all-start.1 = ((bf16[32,128,384]{2,1,0:T(8,128)(2,1)}), bf16[32,128,384]{2,1,0:T(8,128)(2,1)S(1)}, u32[]{:S(2)}, u32[]{:S(2)}) async-start(bf16[32,128,384]{2,1,0:T(8,128)(2,1)} %copy.98), calls=%async_computation.1 | async-start | bytes 6291456 | tf_op jit(solution)/shard_map/while/body/eval_jaxpr/all_to_all | solution.py:84
  710.4 10.8 copy-start.4
  721.3 12.0 %copy-start.7 = (bf16[4,128,384]{1,2,0:T(8,128)(2,1)S(1)}, bf16[4,128,384]{1,2,0:T(8,128)(2,1)}, u32[]{:S(2)}) copy-start(bf16[4,128,384]{1,2,0:T(8,128)(2,1)} %get-tuple-element.343) | copy-start | bytes 1179652 | tf_op jit(solution)/shard_map/while/body/eval_jaxpr/cond
  742.7 19.9 %collective-permute-start = (bf16[4,128,384]{1,2,0:T(8,128)(2,1)S(1)}, bf16[4,128,384]{1,2,0:T(8,128)(2,1)}, u32[]{:S(2)}, u32[]{:S(2)}) collective-permute-start(bf16[4,128,384]{1,2,0:T(8,128)(2,1)S(1)} %get-tuple-element.639), channel_id=1, source_target_pairs={{0,32},{32,64},{64,96},{1,33},{33,65},{65,97},{2,34},{34,66},{66,9... | collective-permute-start | bytes 1179656 | tf_op jit(solution)/shard_map/while/body/eval_jaxpr/ppermute | solution.py:13
  744.7 16.8 %copy-start.8 = (bf16[4,128,384]{1,2,0:T(8,128)(2,1)S(1)}, bf16[4,128,384]{1,2,0:T(8,128)(2,1)}, u32[]{:S(2)}) copy-start(bf16[4,128,384]{1,2,0:T(8,128)(2,1)} %copy.101) | copy-start | bytes 1179652 | tf_op jit(solution)/shard_map/while
  744.7 17.9 %copy-start.2 = (bf16[2,12,128,384]{3,2,1,0:T(8,128)(2,1)S(1)}, bf16[2,12,128,384]{3,2,1,0:T(8,128)(2,1)}, u32[]{:S(2)}) copy-start(bf16[2,12,128,384]{3,2,1,0:T(8,128)(2,1)} %pad_maximum_fusion.10) | copy-start | bytes 7077892 | tf_op jit(solution)/shard_map/while
  774.2 48.8 %all-to-all-start = ((bf16[32,128,384]{2,1,0:T(8,128)(2,1)}), bf16[32,128,384]{2,1,0:T(8,128)(2,1)S(1)}, u32[]{:S(2)}, u32[]{:S(2)}) async-start(bf16[32,128,384]{2,1,0:T(8,128)(2,1)} %copy.95), calls=%async_computation | async-start | bytes 6291456 | tf_op jit(solution)/shard_map/while/body/eval_jaxpr/all_to_all | solution.py:84
  827.8 10.8 copy-start.3
  842.7 49.0 %all-to-all-start.1 = ((bf16[32,128,384]{2,1,0:T(8,128)(2,1)}), bf16[32,128,384]{2,1,0:T(8,128)(2,1)S(1)}, u32[]{:S(2)}, u32[]{:S(2)}) async-start(bf16[32,128,384]{2,1,0:T(8,128)(2,1)} %copy.98), calls=%async_computation.1 | async-start | bytes 6291456 | tf_op jit(solution)/shard_map/while/body/eval_jaxpr/all_to_all | solution.py:84
  896.5 10.8 copy-start.4
  907.3 24.5 %collective-permute-start = (bf16[4,128,384]{1,2,0:T(8,128)(2,1)S(1)}, bf16[4,128,384]{1,2,0:T(8,128)(2,1)}, u32[]{:S(2)}, u32[]{:S(2)}) collective-permute-start(bf16[4,128,384]{1,2,0:T(8,128)(2,1)S(1)} %get-tuple-element.639), channel_id=1, source_target_pairs={{0,32},{32,64},{64,96},{1,33},{33,65},{65,97},{2,34},{34,66},{66,9... | collective-permute-start | bytes 1179656 | tf_op jit(solution)/shard_map/while/body/eval_jaxpr/ppermute | solution.py:13
  913.9 16.8 %copy-start.8 = (bf16[4,128,384]{1,2,0:T(8,128)(2,1)S(1)}, bf16[4,128,384]{1,2,0:T(8,128)(2,1)}, u32[]{:S(2)}) copy-start(bf16[4,128,384]{1,2,0:T(8,128)(2,1)} %copy.101) | copy-start | bytes 1179652 | tf_op jit(solution)/shard_map/while
  913.9 17.9 %copy-start.2 = (bf16[2,12,128,384]{3,2,1,0:T(8,128)(2,1)S(1)}, bf16[2,12,128,384]{3,2,1,0:T(8,128)(2,1)}, u32[]{:S(2)}) copy-start(bf16[2,12,128,384]{3,2,1,0:T(8,128)(2,1)} %pad_maximum_fusion.10) | copy-start | bytes 7077892 | tf_op jit(solution)/shard_map/while
  943.4 46.0 %all-to-all-start = ((bf16[32,128,384]{2,1,0:T(8,128)(2,1)}), bf16[32,128,384]{2,1,0:T(8,128)(2,1)S(1)}, u32[]{:S(2)}, u32[]{:S(2)}) async-start(bf16[32,128,384]{2,1,0:T(8,128)(2,1)} %copy.95), calls=%async_computation | async-start | bytes 6291456 | tf_op jit(solution)/shard_map/while/body/eval_jaxpr/all_to_all | solution.py:84
  994.2 10.8 copy-start.3
  1009.0 52.9 %all-to-all-start.1 = ((bf16[32,128,384]{2,1,0:T(8,128)(2,1)}), bf16[32,128,384]{2,1,0:T(8,128)(2,1)S(1)}, u32[]{:S(2)}, u32[]{:S(2)}) async-start(bf16[32,128,384]{2,1,0:T(8,128)(2,1)} %copy.98), calls=%async_computation.1 | async-start | bytes 6291456 | tf_op jit(solution)/shard_map/while/body/eval_jaxpr/all_to_all | solution.py:84
  1077.6 19.9 %collective-permute-start = (bf16[4,128,384]{1,2,0:T(8,128)(2,1)S(1)}, bf16[4,128,384]{1,2,0:T(8,128)(2,1)}, u32[]{:S(2)}, u32[]{:S(2)}) collective-permute-start(bf16[4,128,384]{1,2,0:T(8,128)(2,1)S(1)} %get-tuple-element.639), channel_id=1, source_target_pairs={{0,32},{32,64},{64,96},{1,33},{33,65},{65,97},{2,34},{34,66},{66,9... | collective-permute-start | bytes 1179656 | tf_op jit(solution)/shard_map/while/body/eval_jaxpr/ppermute | solution.py:13
  1079.5 16.8 %copy-start.8 = (bf16[4,128,384]{1,2,0:T(8,128)(2,1)S(1)}, bf16[4,128,384]{1,2,0:T(8,128)(2,1)}, u32[]{:S(2)}) copy-start(bf16[4,128,384]{1,2,0:T(8,128)(2,1)} %copy.101) | copy-start | bytes 1179652 | tf_op jit(solution)/shard_map/while
  1079.5 17.9 %copy-start.2 = (bf16[2,12,128,384]{3,2,1,0:T(8,128)(2,1)S(1)}, bf16[2,12,128,384]{3,2,1,0:T(8,128)(2,1)}, u32[]{:S(2)}) copy-start(bf16[2,12,128,384]{3,2,1,0:T(8,128)(2,1)} %pad_maximum_fusion.10) | copy-start | bytes 7077892 | tf_op jit(solution)/shard_map/while
  (19 other events, 88.0 us)
Sparse Core Ops, SparseCore 0:
  1098.7 49.5 all-reduce.2
where the time goes:
time: 1160 us
  local copies, waits for them, and re-layouts  399 us (34%)
  other arithmetic  331 us (29%)
  waiting for transfers between devices  233 us (20%)
  starting transfers between devices  111 us (10%)
  matrix products  68.8 us (6%)
  between operations  13.6 us (1%)
    all_to_all x12, waiting for transfers between devices, turn(): lax.all_to_all(outgoing, 'dom', split_axis=0, concat_axis=0, tiled=True)  163 us
    concatenate x12, other arithmetic, turn(): table = jnp.concatenate([own_table, stale_table], 0)  129 us
    another operation x12, other arithmetic, turn(): return (inbox, jnp.stack(owned_next), jnp.stack(imported_next), results)  120 us
    slice x6, local copies, waits for them, and re-layouts, turn(): stale_table = imported[sublayer]  117 us
    all_to_all x12, starting transfers between devices, turn(): lax.all_to_all(outgoing, 'dom', split_axis=0, concat_axis=0, tiled=True)  80.7 us
    gather x6, local copies, waits for them, and re-layouts, gather_rows(): picked = table[columns]  71.8 us
    dynamic_update_slice x12, other arithmetic, turn(): lax.dynamic_update_slice_in_dim(stale_table, jnp.where(active, received,...  57.4 us
    psum x1, waiting for transfers between devices, broadcast(): return lax.psum(kept, axis)  49.7 us
  transfers between devices with their start and end apart: 19, of which 13 were waited for; matrix products, arithmetic and copies ran while one was open for 31% of the time, Pallas kernels for 0%

commit v1 on v0

v1 whole, which is shorter than its diff:
```python
import jax
import jax.numpy as jnp
import numpy as np
from jax import lax
from jax.experimental import pallas as pl
from jax.experimental.pallas import tpu as pltpu
from jax.sharding import PartitionSpec as P

alpha_mix = 0.1
lambda_decay = 0.5

VMEM_LIMIT = 56 * 1024 * 1024


def stale_kernel(count_ref, tile_ref, col_ref, adj_ref, stale_ref, out_ref, acc_ref):
    row = pl.program_id(0)
    count = count_ref[row]
    acc_ref[...] = jnp.zeros_like(acc_ref)

    def body(step, carry):
        first, second = 2 * step, 2 * step + 1
        t0, t1 = tile_ref[row, first], tile_ref[row, second]
        c0, c1 = col_ref[row, first], col_ref[row, second]
        keep = second < count
        right = jnp.where(keep, adj_ref[0, t1], jnp.zeros_like(adj_ref[0, t1]))
        left = jnp.concatenate([adj_ref[0, t0], right], 1)
        for layer in range(2):
            rows = jnp.concatenate([stale_ref[layer, c0], stale_ref[layer, c1]], 0)
            acc_ref[layer] += jnp.dot(left, rows, preferred_element_type=jnp.float32)
        return carry

    lax.fori_loop(0, (count + 1) // 2, body, 0)
    out_ref[:, 0] = acc_ref[...]


def stale_sums(tile_columns, adjacency, stale, groups, group_blocks, part_count):
    blocks, fanout = tile_columns.shape
    block, width = stale.shape[2], stale.shape[3]
    own = blocks
    rows = (groups - 1) * group_blocks
    cols = tile_columns[:rows]
    row_group = (jnp.arange(rows, dtype=jnp.int32) // group_blocks)[:, None]
    is_stale = cols >= own + part_count * (row_group + 1)
    rank = jnp.cumsum(is_stale.astype(jnp.int32), 1)
    places = jnp.arange(fanout, dtype=jnp.int32)[None, None, :]
    hit = is_stale[:, :, None] & (rank[:, :, None] - 1 == places)
    tile_list = jnp.sum(jnp.where(hit, jnp.arange(fanout, dtype=jnp.int32)[None, :, None], 0), 1)
    col_list = jnp.sum(jnp.where(hit, (cols - own - part_count)[:, :, None], 0), 1)
    counts = rank[:, -1]
    return pl.pallas_call(
        stale_kernel,
        out_shape=jax.ShapeDtypeStruct((2, rows, block, width), jnp.float32),
        grid_spec=pltpu.PrefetchScalarGridSpec(
            num_scalar_prefetch=3,
            grid=(rows,),
            in_specs=[
                pl.BlockSpec((1, fanout, block, block), lambda r, *_: (r, 0, 0, 0)),
                pl.BlockSpec(memory_space=pltpu.VMEM),
            ],
            out_specs=pl.BlockSpec((2, 1, block, width), lambda r, *_: (0, r, 0, 0)),
            scratch_shapes=[pltpu.VMEM((2, block, width), jnp.float32)],
        ),
        compiler_params=pltpu.CompilerParams(vmem_limit_bytes=VMEM_LIMIT),
        name="stale_sums",
    )(counts, tile_list, col_list, adjacency, stale)


def gather_sums(layer, idx, flag, own, recv, adj, stale):
    blocks, piece, width = own.shape
    slots = recv.shape[0]
    block = adj.shape[1]
    pieces = block // piece
    stale_rows = stale.shape[1]

    def kernel(idx_ref, flag_ref, own_ref, recv_ref, adj_ref, stale_ref, out_ref, table, rhs, sems):
        row = pl.program_id(0)
        fanout = idx_ref.shape[1]

        @pl.when(row == 0)
        def _():
            first = pltpu.make_async_copy(own_ref, table.at[pl.ds(0, blocks)], sems.at[0])
            second = pltpu.make_async_copy(recv_ref, table.at[pl.ds(blocks, slots)], sems.at[1])
            first.start()
            second.start()
            table[blocks + slots] = jnp.zeros((piece, width), table.dtype)
            first.wait()
            second.wait()

        for t in range(fanout):
            rhs[pl.ds(t * piece, piece), :] = table[idx_ref[row, t]]
        total = jnp.dot(adj_ref[0], rhs[...], preferred_element_type=jnp.float32)
        use = (flag_ref[0] == layer // 2) & (row < stale_rows)
        total = total + jnp.where(use, stale_ref[0, 0], 0.0)
        out_ref[:, 0] = total.reshape(pieces, piece, width).astype(out_ref.dtype)

    return pl.pallas_call(
        kernel,
        out_shape=jax.ShapeDtypeStruct((pieces, blocks, piece, width), jnp.bfloat16),
        grid_spec=pltpu.PrefetchScalarGridSpec(
            num_scalar_prefetch=2,
            grid=(blocks,),
            in_specs=[
                pl.BlockSpec(memory_space=pl.ANY),
                pl.BlockSpec(memory_space=pl.ANY),
                pl.BlockSpec((1, block, adj.shape[2]), lambda r, *_: (r, 0, 0)),
                pl.BlockSpec(
                    (1, 1, block, width),
                    lambda r, *_: (layer % 2, jnp.minimum(r, stale_rows - 1), 0, 0),
                ),
            ],
            out_specs=pl.BlockSpec((pieces, 1, piece, width), lambda r, *_: (0, r, 0, 0)),
            scratch_shapes=[
                pltpu.VMEM((blocks + slots + 1, piece, width), jnp.bfloat16),
                pltpu.VMEM((adj.shape[2], width), jnp.bfloat16),
                pltpu.SemaphoreType.DMA((2,)),
            ],
        ),
        compiler_params=pltpu.CompilerParams(vmem_limit_bytes=VMEM_LIMIT),
        name="gather_sums",
    )(idx, flag, own, recv, adj, stale)


def pack(picks_ref, features_ref, out_ref, groups, group_blocks):
    dests = out_ref.shape[0]

    def body(dest, carry):
        for h in range(groups):
            out_ref[dest, h] = features_ref[h * group_blocks + picks_ref[h, dest]]
        return carry

    lax.fori_loop(0, dests, body, 0)


def pack_first(picks, features, groups, group_blocks):
    blocks, piece, width = features.shape
    dests = picks.shape[1]

    def kernel(picks_ref, features_ref, out_ref):
        pack(picks_ref, features_ref, out_ref, groups, group_blocks)

    return pl.pallas_call(
        kernel,
        out_shape=jax.ShapeDtypeStruct((dests, groups, piece, width), jnp.bfloat16),
        in_specs=[pl.BlockSpec(memory_space=pltpu.SMEM), pl.BlockSpec(memory_space=pltpu.VMEM)],
        out_specs=pl.BlockSpec(memory_space=pltpu.VMEM),
        compiler_params=pltpu.CompilerParams(vmem_limit_bytes=VMEM_LIMIT),
        name="pack_first",
    )(picks, features)


def combine(layer, last, beta, picks, parts, initial, weight, groups, group_blocks):
    pieces, blocks, piece, width = parts.shape
    dests = picks.shape[1]

    def kernel(picks_ref, parts_ref, initial_ref, weight_ref, next_ref, *outs):
        for block in range(blocks):
            summed = parts_ref[0, block].astype(jnp.float32)
            for part in range(1, pieces):
                summed = summed + parts_ref[part, block].astype(jnp.float32)
            mixed = ((1.0 - alpha_mix) * summed + alpha_mix * initial_ref[block].astype(jnp.float32))
            mixed = mixed.astype(jnp.bfloat16)
            product = jnp.dot(mixed, weight_ref[...], preferred_element_type=jnp.float32)
            value = (1.0 - beta) * mixed.astype(jnp.float32) + beta * product
            next_ref[block] = jnp.maximum(value, 0.0).astype(jnp.bfloat16)
        if outs:
            pack(picks_ref, next_ref, outs[0], groups, group_blocks)

    shapes = [jax.ShapeDtypeStruct((blocks, piece, width), jnp.bfloat16)]
    if not last:
        shapes.append(jax.ShapeDtypeStruct((dests, groups, piece, width), jnp.bfloat16))
    return pl.pallas_call(
        kernel,
        out_shape=shapes,
        in_specs=[pl.BlockSpec(memory_space=pltpu.SMEM)] + [pl.BlockSpec(memory_space=pltpu.VMEM)] * 3,
        out_specs=[pl.BlockSpec(memory_space=pltpu.VMEM)] * len(shapes),
        compiler_params=pltpu.CompilerParams(vmem_limit_bytes=VMEM_LIMIT),
        name="combine",
    )(picks, parts, initial, weight)


def per_device(
    initial_features, layer_weights, adjacency_tiles, tile_columns, send_blocks, stale_imports
):
    section = lax.axis_index("section")
    sections = lax.axis_size("section")
    part_count = lax.axis_size("dom")
    blocks, fanout, block = adjacency_tiles.shape[:3]
    width = initial_features.shape[1]
    groups = send_blocks.shape[1]
    group_blocks = blocks // groups
    depth = layer_weights.shape[0]
    layers = depth * sections
    piece = block // sections
    slots = groups * part_count

    weights = lax.all_gather(layer_weights, "section", axis=0, tiled=True)
    adj = lax.dynamic_slice_in_dim(adjacency_tiles, section * piece, piece, 3)
    adj = adj.transpose(0, 2, 1, 3).reshape(blocks, block, fanout * piece)
    initial = lax.dynamic_slice_in_dim(
        initial_features.reshape(blocks, block, width), section * piece, piece, 1
    )
    picks = jnp.maximum(send_blocks[0], 0)
    row_group = (jnp.arange(blocks, dtype=jnp.int32) // group_blocks)[:, None]
    slot = jnp.maximum(tile_columns - blocks, 0)
    slot_group, slot_part = slot // part_count, slot % part_count
    idx = jnp.where(
        tile_columns < blocks,
        tile_columns,
        jnp.where(slot_group <= row_group, blocks + slot_part * groups + slot_group, blocks + slots),
    )
    stale = stale_sums(
        tile_columns, adjacency_tiles, stale_imports[:, 0], groups, group_blocks, part_count
    )
    flag = section[None].astype(jnp.int32)

    features = initial
    outgoing = pack_first(picks, initial, groups, group_blocks)
    for layer in range(layers):
        received = lax.all_to_all(outgoing, "dom", split_axis=0, concat_axis=0, tiled=True)
        received = received.reshape(slots, piece, width)
        parts = gather_sums(layer, idx, flag, features, received, adj, stale)
        parts = lax.all_to_all(parts, "section", split_axis=0, concat_axis=0, tiled=True)
        beta = float(np.log(np.float32(lambda_decay) / np.float32(layer + 1) + np.float32(1.0)))
        last = layer == layers - 1
        outs = combine(layer, last, beta, picks, parts, initial, weights[layer], groups, group_blocks)
        features = outs[0]
        if not last:
            outgoing = outs[1]

    columns = width // sections
    split = features.reshape(blocks, piece, sections, columns).transpose(2, 0, 1, 3)
    joined = lax.all_to_all(split, "section", split_axis=0, concat_axis=0, tiled=True)
    return joined.transpose(1, 0, 2, 3).reshape(blocks * block, columns)


def solution(mesh):
    return jax.shard_map(
        per_device,
        mesh=mesh,
        in_specs=(
            P("dom", None),
            P("section", None, None),
            P("dom", None, None, None),
            P("dom", None),
            P("dom", None, None),
            P("section", "dom", None, None, None),
        ),
        out_specs=P("dom", "section"),
        check_vma=False,
    )
```

time: 1160 us -> 652 us (0.56)
  blocking collectives: 0 us -> 423 us
  local copies, waits for them, and re-layouts: 399 us -> 34.1 us
  other arithmetic: 331 us -> 2.36 us
  waiting for transfers between devices: 233 us -> 13.9 us
  Pallas kernels: 0 us -> 147 us
  starting transfers between devices: 111 us -> 14.8 us
  matrix products: 68.8 us -> 0 us
    all_to_all x0 -> x15, blocking collectives: none -> 423 us  [the longest x7 254 us: per_device(): lax.all_to_all(outgoing, 'dom', split_axis=0, concat_axis=0, tiled=True)]
    all_to_all x12 -> x2, waiting for transfers between devices: 163 us -> 13.2 us  [the longest x1 13.2 us: per_device(): lax.all_to_all(parts, 'section', split_axis=0, concat_axis=0, tiled=True)]
    pallas_call x0 -> x18, Pallas kernels: none -> 147 us  [the longest x8 94.6 us: gather_sums(): pl.pallas_call(kernel, out_shape=jax.ShapeDtypeStruct((pieces, blocks, pi...]
    slice x12 -> x1, local copies, waits for them, and re-layouts: 130 us -> 0.7 us  [stale_sums(): counts = rank[:, -1]]
    concatenate x12 -> x0, other arithmetic: 129 us -> none  [turn(): table = jnp.concatenate([own_table, stale_table], 0)]
    another operation x12 -> x1, other arithmetic: 120 us -> 0.18 us  [stale_sums(): rank = jnp.cumsum(is_stale.astype(jnp.int32), 1)]
    gather x6 -> x0, local copies, waits for them, and re-layouts: 71.8 us -> none  [gather_rows(): picked = table[columns]]
    dynamic_slice x56 -> x2, local copies, waits for them, and re-layouts: 82.4 us -> 12.2 us  [the longest x1 11.4 us: per_device(): adj = lax.dynamic_slice_in_dim(adjacency_tiles, section * piece, piece, 3)]
  transfers between devices with their start and end apart: 19 -> 3, of which waited for: 13 -> 1; matrix products, arithmetic and copies ran while one was open for 31% -> 5% of each run, Pallas kernels for 0% -> 5%
where the time goes in v1:
time: 652 us; the launch traced here: 649 us
  blocking collectives  423 us (65%)
  Pallas kernels  147 us (23%)
  local copies, waits for them, and re-layouts  34.1 us (5%)
  starting transfers between devices  14.8 us (2%)
  waiting for transfers between devices  13.9 us (2%)
  between operations  13.5 us (2%)
    all_to_all x7, blocking collectives, per_device(): lax.all_to_all(outgoing, 'dom', split_axis=0, concat_axis=0, tiled=True)  254 us
    all_to_all x7, blocking collectives, per_device(): lax.all_to_all(parts, 'section', split_axis=0, concat_axis=0, tiled=True)  158 us
    pallas_call x8, Pallas kernels, gather_sums(): pl.pallas_call(kernel, out_shape=jax.ShapeDtypeStruct((pieces, blocks, pi...  94.6 us
    pallas_call x8, Pallas kernels, combine(): pl.pallas_call(kernel, out_shape=shapes, in_specs=[pl.BlockSpec(memory_sp...  31.3 us
    pallas_call x1, Pallas kernels, stale_sums(): pl.pallas_call(stale_kernel, out_shape=jax.ShapeDtypeStruct((2, rows, blo...  18.6 us
    all_to_all x1, waiting for transfers between devices, per_device(): lax.all_to_all(parts, 'section', split_axis=0, concat_axis=0, tiled=True)  13.2 us
  transfers between devices with their start and end apart: 3, of which 1 were waited for; matrix products, arithmetic and copies ran while one was open for 5% of the time, Pallas kernels for 5%

profile of v1, /device:TPU:1, one launch (start us, length us, event | category | flops | bytes accessed | tf_op | source)
XLA Modules:
  0.0 648.8 jit_solution(3737456893131321578)
XLA Ops:
  6.5 0.7 all-gather.2.cloned.1.call-update
  8.5 0.7 constant_dynamic-slice_fusion.1.features_ref.own_ref.initial_ref
  9.3 2.9 pack_first.1
  12.2 9.8 %all-to-all-start = ((bf16[32,3,32,384]{3,2,1,0:T(8,128)(2,1)}), bf16[32,3,32,384]{3,2,1,0:T(8,128)(2,1)S(1)}, u32[]{:S(2)}, u32[]{:S(2)}) async-start(bf16[32,3,32,384]{3,2,1,0:T(8,128)(2,1)} %pack_first.1), calls=%async_computation | async-start | bytes 4718592 | tf_op jit(solution)/shard_map/all_to_all | solution.py:219
  22.0 11.4 %constant_dynamic-slice_fusion = bf16[12,24,128,32]{3,2,1,0:T(8,128)(2,1)} fusion(bf16[12,24,128,128]{3,2,1,0:T(8,128)(2,1)} %adj_ref.1, s32[]{:T(128)S(6)} %select_n.54), kind=kLoop, calls=%fused_computation.40 | loop fusion | bytes 4718596 | tf_op jit(solution)/shard_map/dynamic_slice | solution.py:197
  33.5 8.5 %copy.45 = bf16[12,24,128,32]{2,3,1,0:T(8,128)(2,1)} copy(bf16[12,24,128,32]{3,2,1,0:T(8,128)(2,1)} %constant_dynamic-slice_fusion) | data formatting | bytes 4718592
  41.9 4.3 copy.33.adj_ref
  46.5 0.7 slice_reduce_fusion.count_ref
  47.2 0.7 select_reduce_fusion
  48.0 18.6 %stale_sums.1.stale_ref = f32[2,8,128,384]{3,2,1,0:T(8,128)} custom-call(s32[8]{0:T(128)} %slice_reduce_fusion.count_ref, s32[8,24]{1,0:T(8,128)} %get-tuple-element.34.tile_ref, s32[8,24]{1,0:T(8,128)} %get-tuple-element.33.col_ref, bf16[12,24,128,128]{3,2,1,0:T(8,128)(2,1)} %adj_ref.1, bf16[2,64,128,384]{3,2,1,0:T(8,128)(2,1)} %bitcast.39), custom_call_target="tpu_custom_call" | custom-call | tf_op jit(solution)/shard_map/stale_sums/pallas_call | solution.py:50
  67.2 1.4 copy-done.2
  68.6 11.8 %gather_sums.8 = bf16[4,12,32,384]{3,2,1,0:T(8,128)(2,1)} custom-call(s32[12,24]{1,0:T(8,128)} %compare_select_fusion.idx_ref, s32[1]{0:T(128)} %bitcast.flag_ref, bf16[12,32,384]{2,1,0:T(8,128)(2,1)} %constant_dynamic-slice_fusion.1.features_ref.own_ref.initial_ref, bf16[96,32,384]{2,1,0:T(8,128)(2,1)} %bitcast.40, bf16[12,128,768]{2,1,0:T(8,128)(2,1)} %copy.33.adj_ref, ...), custom_call_target="tpu_custom_call" | custom-call | tf_op jit(solution)/shard_map/gather_sums/pallas_call | solution.py:96
  80.4 5.0 all-to-all-start.1
  85.4 3.1 slice_bitcast_fusion
  88.5 13.2 %all-to-all-done.1.parts_ref = bf16[4,12,32,384]{3,2,1,0:T(8,128)(2,1)S(1)} async-done(((bf16[4,12,32,384]{3,2,1,0:T(8,128)(2,1)}), bf16[4,12,32,384]{3,2,1,0:T(8,128)(2,1)S(1)}, u32[]{:S(2)}, u32[]{:S(2)}) %all-to-all-start.1) | async-done | bytes 1179680 | tf_op jit(solution)/shard_map/all_to_all | solution.py:222
  101.8 1.1 copy-done.3
  102.9 4.0 combine.8
  106.9 38.8 %all_to_all.85 = bf16[32,3,32,384]{3,2,1,0:T(8,128)(2,1)} all-to-all(bf16[32,3,32,384]{3,2,1,0:T(8,128)(2,1)} %get-tuple-element.20), channel_id=1, replica_groups=mesh['section'=4,'dom'=32] {'dom'}, dimensions={0} | all-to-all | bytes 4718592 | tf_op jit(solution)/shard_map/all_to_all | solution.py:219
  145.7 11.8 %gather_sums.9 = bf16[4,12,32,384]{3,2,1,0:T(8,128)(2,1)} custom-call(s32[12,24]{1,0:T(8,128)} %compare_select_fusion.idx_ref, s32[1]{0:T(128)} %bitcast.flag_ref, bf16[12,32,384]{2,1,0:T(8,128)(2,1)} %get-tuple-element.19.own_ref, bf16[96,32,384]{2,1,0:T(8,128)(2,1)} %bitcast.42, bf16[12,128,768]{2,1,0:T(8,128)(2,1)} %copy.33.adj_ref, ...), custom_call_target="tpu_custom_call" | custom-call | tf_op jit(solution)/shard_map/gather_sums/pallas_call | solution.py:96
  157.5 22.7 %all_to_all.86.parts_ref = bf16[4,12,32,384]{3,2,1,0:T(8,128)(2,1)} all-to-all(bf16[4,12,32,384]{3,2,1,0:T(8,128)(2,1)} %gather_sums.9), channel_id=1, replica_groups=mesh['section'=4,'dom'=32] {'section'}, dimensions={0} | all-to-all | bytes 2359296 | tf_op jit(solution)/shard_map/all_to_all | solution.py:222
  180.3 4.0 combine.9
  184.3 35.8 %all_to_all.87 = bf16[32,3,32,384]{3,2,1,0:T(8,128)(2,1)} all-to-all(bf16[32,3,32,384]{3,2,1,0:T(8,128)(2,1)} %get-tuple-element.22), channel_id=1, replica_groups=mesh['section'=4,'dom'=32] {'dom'}, dimensions={0} | all-to-all | bytes 4718592 | tf_op jit(solution)/shard_map/all_to_all | solution.py:219
  220.1 11.8 %gather_sums.10 = bf16[4,12,32,384]{3,2,1,0:T(8,128)(2,1)} custom-call(s32[12,24]{1,0:T(8,128)} %compare_select_fusion.idx_ref, s32[1]{0:T(128)} %bitcast.flag_ref, bf16[12,32,384]{2,1,0:T(8,128)(2,1)} %get-tuple-element.21.own_ref, bf16[96,32,384]{2,1,0:T(8,128)(2,1)} %bitcast.43, bf16[12,128,768]{2,1,0:T(8,128)(2,1)} %copy.33.adj_ref, ...), custom_call_target="tpu_custom_call" | custom-call | tf_op jit(solution)/shard_map/gather_sums/pallas_call | solution.py:96
  231.9 22.5 %all_to_all.88.parts_ref = bf16[4,12,32,384]{3,2,1,0:T(8,128)(2,1)} all-to-all(bf16[4,12,32,384]{3,2,1,0:T(8,128)(2,1)} %gather_sums.10), channel_id=1, replica_groups=mesh['section'=4,'dom'=32] {'section'}, dimensions={0} | all-to-all | bytes 2359296 | tf_op jit(solution)/shard_map/all_to_all | solution.py:222
  254.5 4.0 combine.10
  258.5 35.8 %all_to_all.89 = bf16[32,3,32,384]{3,2,1,0:T(8,128)(2,1)} all-to-all(bf16[32,3,32,384]{3,2,1,0:T(8,128)(2,1)} %get-tuple-element.24), channel_id=1, replica_groups=mesh['section'=4,'dom'=32] {'dom'}, dimensions={0} | all-to-all | bytes 4718592 | tf_op jit(solution)/shard_map/all_to_all | solution.py:219
  294.3 11.8 %gather_sums.11 = bf16[4,12,32,384]{3,2,1,0:T(8,128)(2,1)} custom-call(s32[12,24]{1,0:T(8,128)} %compare_select_fusion.idx_ref, s32[1]{0:T(128)} %bitcast.flag_ref, bf16[12,32,384]{2,1,0:T(8,128)(2,1)} %get-tuple-element.23.own_ref, bf16[96,32,384]{2,1,0:T(8,128)(2,1)} %bitcast.44, bf16[12,128,768]{2,1,0:T(8,128)(2,1)} %copy.33.adj_ref, ...), custom_call_target="tpu_custom_call" | custom-call | tf_op jit(solution)/shard_map/gather_sums/pallas_call | solution.py:96
  306.2 22.5 %all_to_all.90.parts_ref = bf16[4,12,32,384]{3,2,1,0:T(8,128)(2,1)} all-to-all(bf16[4,12,32,384]{3,2,1,0:T(8,128)(2,1)} %gather_sums.11), channel_id=1, replica_groups=mesh['section'=4,'dom'=32] {'section'}, dimensions={0} | all-to-all | bytes 2359296 | tf_op jit(solution)/shard_map/all_to_all | solution.py:222
  328.7 4.0 combine.11
  332.7 35.8 %all_to_all.91 = bf16[32,3,32,384]{3,2,1,0:T(8,128)(2,1)} all-to-all(bf16[32,3,32,384]{3,2,1,0:T(8,128)(2,1)} %get-tuple-element.26), channel_id=1, replica_groups=mesh['section'=4,'dom'=32] {'dom'}, dimensions={0} | all-to-all | bytes 4718592 | tf_op jit(solution)/shard_map/all_to_all | solution.py:219
  368.5 11.8 %gather_sums.12 = bf16[4,12,32,384]{3,2,1,0:T(8,128)(2,1)} custom-call(s32[12,24]{1,0:T(8,128)} %compare_select_fusion.idx_ref, s32[1]{0:T(128)} %bitcast.flag_ref, bf16[12,32,384]{2,1,0:T(8,128)(2,1)} %get-tuple-element.25.own_ref, bf16[96,32,384]{2,1,0:T(8,128)(2,1)} %bitcast.45, bf16[12,128,768]{2,1,0:T(8,128)(2,1)} %copy.33.adj_ref, ...), custom_call_target="tpu_custom_call" | custom-call | tf_op jit(solution)/shard_map/gather_sums/pallas_call | solution.py:96
  380.3 22.5 %all_to_all.92.parts_ref = bf16[4,12,32,384]{3,2,1,0:T(8,128)(2,1)} all-to-all(bf16[4,12,32,384]{3,2,1,0:T(8,128)(2,1)} %gather_sums.12), channel_id=1, replica_groups=mesh['section'=4,'dom'=32] {'section'}, dimensions={0} | all-to-all | bytes 2359296 | tf_op jit(solution)/shard_map/all_to_all | solution.py:222
  402.9 4.0 combine.12
  406.9 35.8 %all_to_all.93 = bf16[32,3,32,384]{3,2,1,0:T(8,128)(2,1)} all-to-all(bf16[32,3,32,384]{3,2,1,0:T(8,128)(2,1)} %get-tuple-element.28), channel_id=1, replica_groups=mesh['section'=4,'dom'=32] {'dom'}, dimensions={0} | all-to-all | bytes 4718592 | tf_op jit(solution)/shard_map/all_to_all | solution.py:219
  442.7 11.8 %gather_sums.13 = bf16[4,12,32,384]{3,2,1,0:T(8,128)(2,1)} custom-call(s32[12,24]{1,0:T(8,128)} %compare_select_fusion.idx_ref, s32[1]{0:T(128)} %bitcast.flag_ref, bf16[12,32,384]{2,1,0:T(8,128)(2,1)} %get-tuple-element.27.own_ref, bf16[96,32,384]{2,1,0:T(8,128)(2,1)} %bitcast.46, bf16[12,128,768]{2,1,0:T(8,128)(2,1)} %copy.33.adj_ref, ...), custom_call_target="tpu_custom_call" | custom-call | tf_op jit(solution)/shard_map/gather_sums/pallas_call | solution.py:96
  454.6 22.5 %all_to_all.94.parts_ref = bf16[4,12,32,384]{3,2,1,0:T(8,128)(2,1)} all-to-all(bf16[4,12,32,384]{3,2,1,0:T(8,128)(2,1)} %gather_sums.13), channel_id=1, replica_groups=mesh['section'=4,'dom'=32] {'section'}, dimensions={0} | all-to-all | bytes 2359296 | tf_op jit(solution)/shard_map/all_to_all | solution.py:222
  477.1 4.0 combine.13
  481.1 35.8 %all_to_all.95 = bf16[32,3,32,384]{3,2,1,0:T(8,128)(2,1)} all-to-all(bf16[32,3,32,384]{3,2,1,0:T(8,128)(2,1)} %get-tuple-element.30), channel_id=1, replica_groups=mesh['section'=4,'dom'=32] {'dom'}, dimensions={0} | all-to-all | bytes 4718592 | tf_op jit(solution)/shard_map/all_to_all | solution.py:219
  516.9 11.8 %gather_sums.14 = bf16[4,12,32,384]{3,2,1,0:T(8,128)(2,1)} custom-call(s32[12,24]{1,0:T(8,128)} %compare_select_fusion.idx_ref, s32[1]{0:T(128)} %bitcast.flag_ref, bf16[12,32,384]{2,1,0:T(8,128)(2,1)} %get-tuple-element.29.own_ref, bf16[96,32,384]{2,1,0:T(8,128)(2,1)} %bitcast.47, bf16[12,128,768]{2,1,0:T(8,128)(2,1)} %copy.33.adj_ref, ...), custom_call_target="tpu_custom_call" | custom-call | tf_op jit(solution)/shard_map/gather_sums/pallas_call | solution.py:96
  528.8 22.5 %all_to_all.96.parts_ref = bf16[4,12,32,384]{3,2,1,0:T(8,128)(2,1)} all-to-all(bf16[4,12,32,384]{3,2,1,0:T(8,128)(2,1)} %gather_sums.14), channel_id=1, replica_groups=mesh['section'=4,'dom'=32] {'section'}, dimensions={0} | all-to-all | bytes 2359296 | tf_op jit(solution)/shard_map/all_to_all | solution.py:222
  551.3 4.1 combine.14
  555.4 35.8 %all_to_all.97 = bf16[32,3,32,384]{3,2,1,0:T(8,128)(2,1)} all-to-all(bf16[32,3,32,384]{3,2,1,0:T(8,128)(2,1)} %get-tuple-element.32), channel_id=1, replica_groups=mesh['section'=4,'dom'=32] {'dom'}, dimensions={0} | all-to-all | bytes 4718592 | tf_op jit(solution)/shard_map/all_to_all | solution.py:219
  591.2 11.8 %gather_sums.15 = bf16[4,12,32,384]{3,2,1,0:T(8,128)(2,1)} custom-call(s32[12,24]{1,0:T(8,128)} %compare_select_fusion.idx_ref, s32[1]{0:T(128)} %bitcast.flag_ref, bf16[12,32,384]{2,1,0:T(8,128)(2,1)} %get-tuple-element.31.own_ref, bf16[96,32,384]{2,1,0:T(8,128)(2,1)} %bitcast.41, bf16[12,128,768]{2,1,0:T(8,128)(2,1)} %copy.33.adj_ref, ...), custom_call_target="tpu_custom_call" | custom-call | tf_op jit(solution)/shard_map/gather_sums/pallas_call | solution.py:96
  603.1 22.5 %all_to_all.98.parts_ref = bf16[4,12,32,384]{3,2,1,0:T(8,128)(2,1)} all-to-all(bf16[4,12,32,384]{3,2,1,0:T(8,128)(2,1)} %gather_sums.15), channel_id=1, replica_groups=mesh['section'=4,'dom'=32] {'section'}, dimensions={0} | all-to-all | bytes 2359296 | tf_op jit(solution)/shard_map/all_to_all | solution.py:222
  625.5 2.9 combine.15
  628.4 1.2 reshape.86
  629.7 11.3 %all_to_all.99 = bf16[4,12,32,96]{3,2,1,0:T(8,128)(2,1)S(1)} all-to-all(bf16[4,12,32,96]{3,2,1,0:T(8,128)(2,1)S(1)} %bitcast.49), channel_id=1, replica_groups=mesh['section'=4,'dom'=32] {'section'}, dimensions={0} | all-to-all | bytes 589824 | tf_op jit(solution)/shard_map/all_to_all | solution.py:232
  641.1 0.9 copy.43
  (21 shorter events, 2.3 us)
Async XLA Ops:
  6.5 2.0 copy-start
  6.5 78.9 %all-gather.2.cloned.1.call-start = ((), (), s32[]{:S(2)}) async-start(), calls=%async_computation.17 | async-start | bytes 2949120 | tf_op jit(solution)/shard_map/all_gather | solution.py:196
  12.2 55.0 %all-to-all-start = ((bf16[32,3,32,384]{3,2,1,0:T(8,128)(2,1)}), bf16[32,3,32,384]{3,2,1,0:T(8,128)(2,1)S(1)}, u32[]{:S(2)}, u32[]{:S(2)}) async-start(bf16[32,3,32,384]{3,2,1,0:T(8,128)(2,1)} %pack_first.1), calls=%async_computation | async-start | bytes 4718592 | tf_op jit(solution)/shard_map/all_to_all | solution.py:219
  41.9 4.3 copy-start.4
  67.2 1.4 copy-start.2
  80.4 21.3 %all-to-all-start.1 = ((bf16[4,12,32,384]{3,2,1,0:T(8,128)(2,1)}), bf16[4,12,32,384]{3,2,1,0:T(8,128)(2,1)S(1)}, u32[]{:S(2)}, u32[]{:S(2)}) async-start(bf16[4,12,32,384]{3,2,1,0:T(8,128)(2,1)} %gather_sums.8), calls=%async_computation.1 | async-start | bytes 2359296 | tf_op jit(solution)/shard_map/all_to_all | solution.py:222
  101.8 1.1 copy-start.3
  625.5 16.4 %copy-start.1 = (bf16[1536,384]{1,0:T(8,128)(2,1)S(1)}, bf16[1536,384]{1,0:T(8,128)(2,1)}, u32[]{:S(2)}) copy-start(bf16[1536,384]{1,0:T(8,128)(2,1)} %param.6) | copy-start | bytes 3538948
Sparse Core Ops, SparseCore 0:
  9.0 44.4 all-gather.1

commit v2 on v1

v2 whole, which is shorter than its diff:
```python
import jax
import jax.numpy as jnp
import numpy as np
from jax import lax
from jax.experimental import pallas as pl
from jax.experimental.pallas import tpu as pltpu
from jax.sharding import PartitionSpec as P

alpha_mix = 0.1
lambda_decay = 0.5

VMEM_LIMIT = 56 * 1024 * 1024


def stale_kernel(count_ref, tile_ref, col_ref, adj_ref, stale_ref, out_ref, acc_ref):
    row = pl.program_id(0)
    count = count_ref[row]
    acc_ref[...] = jnp.zeros_like(acc_ref)

    def body(step, carry):
        first, second = 2 * step, 2 * step + 1
        t0, t1 = tile_ref[row, first], tile_ref[row, second]
        c0, c1 = col_ref[row, first], col_ref[row, second]
        keep = second < count
        right = jnp.where(keep, adj_ref[0, t1], jnp.zeros_like(adj_ref[0, t1]))
        left = jnp.concatenate([adj_ref[0, t0], right], 1)
        for layer in range(2):
            rows = jnp.concatenate([stale_ref[layer, c0], stale_ref[layer, c1]], 0)
            acc_ref[layer] += jnp.dot(left, rows, preferred_element_type=jnp.float32)
        return carry

    lax.fori_loop(0, (count + 1) // 2, body, 0)
    out_ref[:, 0] = acc_ref[...]


def stale_sums(tile_columns, adjacency, stale, groups, group_blocks, part_count):
    blocks, fanout = tile_columns.shape
    block, width = stale.shape[2], stale.shape[3]
    own = blocks
    rows = (groups - 1) * group_blocks
    cols = tile_columns[:rows]
    row_group = (jnp.arange(rows, dtype=jnp.int32) // group_blocks)[:, None]
    is_stale = cols >= own + part_count * (row_group + 1)
    rank = jnp.cumsum(is_stale.astype(jnp.int32), 1)
    places = jnp.arange(fanout, dtype=jnp.int32)[None, None, :]
    hit = is_stale[:, :, None] & (rank[:, :, None] - 1 == places)
    tile_list = jnp.sum(jnp.where(hit, jnp.arange(fanout, dtype=jnp.int32)[None, :, None], 0), 1)
    col_list = jnp.sum(jnp.where(hit, (cols - own - part_count)[:, :, None], 0), 1)
    counts = rank[:, -1]
    return pl.pallas_call(
        stale_kernel,
        out_shape=jax.ShapeDtypeStruct((2, rows, block, width), jnp.float32),
        grid_spec=pltpu.PrefetchScalarGridSpec(
            num_scalar_prefetch=3,
            grid=(rows,),
            in_specs=[
                pl.BlockSpec((1, fanout, block, block), lambda r, *_: (r, 0, 0, 0)),
                pl.BlockSpec(memory_space=pltpu.VMEM),
            ],
            out_specs=pl.BlockSpec((2, 1, block, width), lambda r, *_: (0, r, 0, 0)),
            scratch_shapes=[pltpu.VMEM((2, block, width), jnp.float32)],
        ),
        compiler_params=pltpu.CompilerParams(vmem_limit_bytes=VMEM_LIMIT),
        name="stale_sums",
    )(counts, tile_list, col_list, adjacency, stale)


MESH = pl.DeviceIdType.MESH
GROUPS = 3
STAGES = 7


def slice_kernel(adj_ref, own_sel_ref, other_sel_ref, own_ref, other_ref):
    per = own_sel_ref.shape[0] // adj_ref.shape[2]
    for m in range(adj_ref.shape[1] // per):
        left = jnp.concatenate([adj_ref[0, m * per + u] for u in range(per)], 1)
        lanes = pl.ds(m * 128, 128)
        own_ref[0, :, lanes] = jnp.dot(
            left, own_sel_ref[...], preferred_element_type=jnp.float32
        ).astype(jnp.bfloat16)
        other_ref[0, :, lanes] = jnp.dot(
            left, other_sel_ref[...], preferred_element_type=jnp.float32
        ).astype(jnp.bfloat16)


def slice_tiles(adjacency, own_slice, other_slice, piece):
    blocks, fanout, block, _ = adjacency.shape
    per = block // piece
    source = jnp.arange(per * block, dtype=jnp.int32)[:, None]
    lane = jnp.arange(block, dtype=jnp.int32)[None, :]

    def selector(j):
        wanted = (lane // piece) * block + j * piece + lane % piece
        return (source == wanted).astype(jnp.bfloat16)

    shape = jax.ShapeDtypeStruct((blocks, block, fanout * piece), jnp.bfloat16)
    spec = pl.BlockSpec((1, block, fanout * piece), lambda r: (r, 0, 0))
    whole = pl.BlockSpec((per * block, block), lambda r: (0, 0))
    return pl.pallas_call(
        slice_kernel,
        out_shape=[shape, shape],
        grid=(blocks,),
        in_specs=[pl.BlockSpec((1, fanout, block, block), lambda r: (r, 0, 0, 0)), whole, whole],
        out_specs=[spec, spec],
        compiler_params=pltpu.CompilerParams(vmem_limit_bytes=VMEM_LIMIT),
        name="slice_tiles",
    )(adjacency, selector(own_slice), selector(other_slice))


def place():
    section, dom = lax.axis_index("section"), lax.axis_index("dom")
    x_hi, core = section // 2, section % 2
    z, y, x_lo = dom // 8, (dom // 2) % 4, dom % 2
    return section, dom, x_hi, core, z, y, x_lo


def piece_of(x_hi, x_lo, core):
    first = (1 - core) * ((x_lo + x_hi) % 2) + core * x_hi
    second = (1 - core) * x_hi + core * x_lo
    return first, second


def main_kernel(
    idx_ref, pick_ref, beta_ref, adj_ref, weight_ref, initial_ref, stale_ref, out_ref,
    table, part, *rest,
):
    rest = list(rest)

    def take(count):
        got = rest[:count]
        del rest[:count]
        return got

    xown, seltab, agbuf, out2, rel2, land2 = (take(GROUPS) for _ in range(6))
    send0, recv0, send1, recv1, send2, recv2, keep1, keep2 = (take(GROUPS) for _ in range(8))
    ag1_s, ag1_r, ag2_s, ag2_r, rel_s, rel_r, main_s, main_r, fwd_s, fwd_r, rs_s, rs_r = rest

    layers = weight_ref.shape[0]
    fanout = idx_ref.shape[0] // (2 * 4 * GROUPS)
    width = weight_ref.shape[1]
    section, dom, x_hi, core, z, y, x_lo = place()
    first, second = piece_of(x_hi, x_lo, core)
    a = (1 - core) * z + core * y
    b = (1 - core) * y + core * z
    zero_core, one_core = 1 - core, core

    def at(zz, yy, lo):
        return zz * 8 + yy * 2 + lo

    def on_a(step):
        return (section, at((z + zero_core * step) % 4, (y + one_core * step) % 4, x_lo))

    def on_b(step):
        return (section, at((z + one_core * step) % 4, (y + zero_core * step) % 4, x_lo))

    a_next = (on_a(1), on_a(3))
    b_next = (on_b(1), on_b(3))
    partner = (x_hi * 2 + 1 - core, dom)
    flip1 = (section, at(z, y, 1 - x_lo))
    flip3 = ((1 - x_hi) * 2 + core, at(z, y, 1 - x_lo))
    hi1 = zero_core * x_hi + one_core * (1 - x_hi)
    line1 = (hi1 * 2 + core, at(z, y, 1 - x_lo))
    hi2 = zero_core * (1 - x_hi) + one_core * x_hi
    line2 = (hi2 * 2 + core, at(z, y, 1 - x_lo))

    barrier = pltpu.get_barrier_semaphore()
    friends = (*a_next, *b_next, partner, flip1, flip3)
    for friend in friends:
        pl.semaphore_signal(barrier, inc=1, device_id=friend, device_id_type=MESH)
    pl.semaphore_wait(barrier, len(friends))

    def remote(src, dst, ssem, rsem, device):
        return pltpu.make_async_remote_copy(
            src_ref=src, dst_ref=dst, send_sem=ssem, recv_sem=rsem,
            device_id=device, device_id_type=MESH,
        )

    def ag1(g, par, d):
        return remote(xown[g], agbuf[g].at[par, d], ag1_s.at[g * 2 + d],
                      ag1_r.at[g * 4 + par * 2 + d], a_next[d])

    def ag2(g, par, d):
        return remote(agbuf[g].at[par, d, d], agbuf[g].at[par, 2, d], ag2_s.at[g * 2 + d],
                      ag2_r.at[g * 4 + par * 2 + d], a_next[d])

    def relay(g, par, d):
        return remote(out2[g].at[2, d], rel2[g].at[par, d], rel_s.at[g * 2 + d],
                      rel_r.at[g * 4 + par * 2 + d], b_next[d])

    def main(g, par, d):
        return remote(out2[g].at[d], land2[g].at[par, d], main_s.at[g * 2 + d],
                      main_r.at[g * 4 + par * 2 + d], b_next[d])

    def fwd(g, par, d):
        return remote(rel2[g].at[par, d], land2[g].at[par, 2, d], fwd_s.at[g * 2 + d],
                      fwd_r.at[g * 4 + par * 2 + d], b_next[d])

    def rs(stage, g, par):
        send, recv = ((send0, recv0), (send1, recv1), (send2, recv2))[stage]
        device = (partner, line1, line2)[stage]
        return remote(send[g], recv[g].at[par], rs_s.at[stage * GROUPS + g],
                      rs_r.at[(stage * GROUPS + g) * 2 + par], device)

    def stage_a(g, layer):
        par = layer % 2
        for d in range(2):
            ag1(g, par, d).wait_recv()
        for d in range(2):
            ag2(g, par, d).start()

    def stage_b(g, layer):
        par = layer % 2
        for d in range(2):
            seltab[g][(a + (3, 1)[d]) % 4] = agbuf[g][par, d]
        for d in range(2):
            ag1(g, par, d).wait_send()
            ag2(g, par, d).wait_recv()
        seltab[g][(a + 2) % 4] = agbuf[g][par, 2]

        def chosen(dest, half, line, lo):
            place_in = (((g * 4 + dest) * 2 + half) * 4 + line) * 2 + lo
            return seltab[g][line, lo, pick_ref[place_in]]

        for d in (2, 0, 1):
            dest = (b + (1, 3, 2)[d]) % 4
            for half in range(2):
                for line in range(4):
                    for lo in range(2):
                        out2[g][d, half, line, lo] = chosen(dest, half, line, lo)
            if d == 2:
                for e in range(2):
                    relay(g, par, e).start()
            else:
                main(g, par, d).start()
        for half in range(2):
            for line in range(4):
                for lo in range(2):
                    slot = 4 * GROUPS + g * 32 + b * 8 + line * 2 + lo
                    table[half, slot] = chosen(b, half, line, lo)

    def stage_c(g, layer):
        par = layer % 2
        for d in range(2):
            relay(g, par, d).wait_recv()
            fwd(g, par, d).start()
        for d in range(2):
            ag2(g, par, d).wait_send()

    def stage_d(g, layer):
        par = layer % 2

        def fill(rel, where):
            for half in range(2):
                slots = pl.ds(4 * GROUPS + g * 32 + where * 8, 8)
                table[half, slots] = land2[g][par, rel, half].reshape(8, 16, width)

        for half in range(2):
            table[half, pl.ds(4 * g, 4)] = xown[g][half]
        for d in range(2):
            main(g, par, d).wait_recv()
            fill(d, (b + (3, 1)[d]) % 4)
        for d in range(2):
            fwd(g, par, d).wait_recv()
        fill(2, (b + 2) % 4)

        for half in range(2):
            def row_block(j, carry, half=half):
                row = g * 4 + j
                base = (half * 4 * GROUPS + row) * fanout
                rows = jnp.concatenate([table[half, idx_ref[base + t]] for t in range(fanout)], 0)
                total = jnp.dot(adj_ref[half, row], rows, preferred_element_type=jnp.float32)
                part[half * 4 + j] = total.reshape(8, 16, width)
                return carry

            lax.fori_loop(0, 4, row_block, 0, unroll=True)

        if g < GROUPS - 1:
            @pl.when(section == layer // 2)
            def _():
                for j in range(4):
                    part[x_lo * 4 + j] += stale_ref[layer % 2, g * 4 + j]

        for j in range(8):
            send0[g][j] = part[j, pl.ds((1 - core) * 4, 4)].astype(jnp.bfloat16)
        rs(0, g, par).start()
        for d in range(2):
            relay(g, par, d).wait_send()
            main(g, par, d).wait_send()

    def stage_e(g, layer):
        par = layer % 2
        rs(0, g, par).wait_recv()
        for j in range(8):
            gone = part[j, pl.ds(core * 4 + (1 - first) * 2, 2)]
            gone = gone + recv0[g][par, j, pl.ds((1 - first) * 2, 2)].astype(jnp.float32)
            send1[g][j] = gone.astype(jnp.bfloat16)
        rs(1, g, par).start()
        for j in range(8):
            kept = part[j, pl.ds(core * 4 + first * 2, 2)]
            keep1[g][j] = kept + recv0[g][par, j, pl.ds(first * 2, 2)].astype(jnp.float32)
        rs(0, g, par).wait_send()
        for d in range(2):
            fwd(g, par, d).wait_send()

    def stage_f(g, layer):
        par = layer % 2
        rs(1, g, par).wait_recv()
        for j in range(8):
            gone = keep1[g][j, 1 - second] + recv1[g][par, j, 1 - second].astype(jnp.float32)
            send2[g][j] = gone.astype(jnp.bfloat16)
        rs(2, g, par).start()
        for j in range(8):
            keep2[g][j] = keep1[g][j, second] + recv1[g][par, j, second].astype(jnp.float32)
        rs(1, g, par).wait_send()

    def stage_h(g, layer):
        par = layer % 2
        rs(2, g, par).wait_recv()
        summed = keep2[g][...] + recv2[g][par].astype(jnp.float32)
        start = jnp.concatenate([initial_ref[half, pl.ds(4 * g, 4)] for half in range(2)], 0)
        mixed = (1.0 - alpha_mix) * summed + alpha_mix * start.astype(jnp.float32)
        mixed = mixed.astype(jnp.bfloat16).reshape(8 * 16, width)
        beta = beta_ref[layer]
        product = jnp.dot(mixed, weight_ref[layer], preferred_element_type=jnp.float32)
        value = (1.0 - beta) * mixed.astype(jnp.float32) + beta * product
        value = jnp.maximum(value, 0.0).astype(jnp.bfloat16).reshape(2, 4, 16, width)
        rs(2, g, par).wait_send()

        @pl.when(layer < layers - 1)
        def _():
            xown[g][...] = value
            for d in range(2):
                ag1(g, 1 - par, d).start()
            seltab[g][a] = value

        @pl.when(layer == layers - 1)
        def _():
            for half in range(2):
                out_ref[half, pl.ds(4 * g, 4)] = value[half]

    for half in range(2):
        table[half, 4 * GROUPS + 96] = jnp.zeros((16, width), jnp.bfloat16)
    for g in range(GROUPS):
        for half in range(2):
            xown[g][half] = initial_ref[half, pl.ds(4 * g, 4)]
        for d in range(2):
            ag1(g, 0, d).start()
        for half in range(2):
            seltab[g][a, half] = initial_ref[half, pl.ds(4 * g, 4)]

    stages = (stage_a, stage_b, stage_c, stage_d, stage_e, stage_f, stage_h)
    offsets = (0, 2, 4)

    def body(layer, carry):
        for tick in range(STAGES):
            now = [(g, tick - offsets[g]) for g in range(GROUPS)]
            late = [(g, s + STAGES) for g, s in now if s < 0]
            due = [(g, s) for g, s in now if s >= 0]
            if late:
                @pl.when(layer > 0)
                def _(late=late):
                    for g, s in late:
                        stages[s](g, layer - 1)
            if due:
                @pl.when(layer < layers)
                def _(due=due):
                    for g, s in due:
                        stages[s](g, layer)
        return carry

    lax.fori_loop(0, layers + 1, body, 0)


def run_layers(idx, picks, betas, adj, weights, initial, stale):
    width = weights.shape[1]
    piece = initial.shape[2]
    dt = jnp.bfloat16
    slab = (piece, width)

    def each(shape, dtype=dt):
        return [pltpu.VMEM((*shape, *slab), dtype) for _ in range(GROUPS)]

    sems = pltpu.SemaphoreType.DMA
    scratch = [
        pltpu.VMEM((2, 4 * GROUPS + 97, *slab), dt),
        pltpu.VMEM((8, 8, *slab), jnp.float32),
        *each((2, 4)), *each((4, 2, 4)), *each((2, 3, 2, 4)),
        *each((3, 2, 4, 2)), *each((2, 2, 4, 2)), *each((2, 3, 2, 4, 2)),
        *each((8, 4)), *each((2, 8, 4)),
        *each((8, 2)), *each((2, 8, 2)),
        *each((8,)), *each((2, 8)),
        *each((8, 2), jnp.float32), *each((8,), jnp.float32),
        *[sems((count,)) for _ in range(5) for count in (2 * GROUPS, 4 * GROUPS)],
        sems((3 * GROUPS,)), sems((6 * GROUPS,)),
    ]
    smem = pl.BlockSpec(memory_space=pltpu.SMEM)
    vmem = pl.BlockSpec(memory_space=pltpu.VMEM)
    return pl.pallas_call(
        main_kernel,
        out_shape=jax.ShapeDtypeStruct(initial.shape, dt),
        in_specs=[smem] * 3 + [vmem] * 4,
        out_specs=vmem,
        scratch_shapes=scratch,
        compiler_params=pltpu.CompilerParams(
            vmem_limit_bytes=VMEM_LIMIT, collective_id=0, has_side_effects=True
        ),
        name="run_layers",
    )(idx, picks, betas, adj, weights, initial, stale)


def per_device(
    initial_features, layer_weights, adjacency_tiles, tile_columns, send_blocks, stale_imports
):
    section, dom, x_hi, core, z, y, x_lo = place()
    sections = lax.axis_size("section")
    part_count = lax.axis_size("dom")
    blocks, fanout, block = adjacency_tiles.shape[:3]
    width = initial_features.shape[1]
    groups = send_blocks.shape[1]
    group_blocks = blocks // groups
    depth = layer_weights.shape[0]
    layers = depth * sections
    piece = block // 8

    def number(hi, lo):
        first, second = piece_of(hi, lo, core)
        return core * 4 + first * 2 + second

    mine, theirs = number(x_hi, x_lo), number(x_hi, 1 - x_lo)
    swap = [(p, p + 1 - 2 * (p % 2)) for p in range(part_count)]

    def by_half(own, other):
        pair = jnp.stack([own, other])
        return jnp.where(x_lo == 0, pair, pair[::-1])

    weights = lax.all_gather(layer_weights, "section", axis=0, tiled=True)
    own_adj, other_adj = slice_tiles(adjacency_tiles, mine, theirs, piece)
    adj = by_half(own_adj, lax.ppermute(other_adj, "dom", swap))

    init_blocks = initial_features.reshape(blocks, 8, piece, width)
    own_init = lax.dynamic_index_in_dim(init_blocks, mine, 1, keepdims=False)
    other_init = lax.dynamic_index_in_dim(init_blocks, theirs, 1, keepdims=False)
    initial = by_half(own_init, lax.ppermute(other_init, "dom", swap))

    sends = lax.all_gather(send_blocks[0], "dom", axis=0, tiled=False)
    sends = jnp.maximum(sends, 0).reshape(4, 4, 2, groups, 4, 4, 2)
    zy = lax.dynamic_index_in_dim(sends, y, 1, keepdims=False)
    zy = lax.dynamic_index_in_dim(zy, z, 3, keepdims=False)
    yz = lax.dynamic_index_in_dim(sends, z, 0, keepdims=False)
    yz = lax.dynamic_index_in_dim(yz, y, 4, keepdims=False)
    picks = jnp.where(core == 0, zy, yz)
    picks = picks.transpose(2, 3, 4, 0, 1).reshape(-1).astype(jnp.int32)

    columns = by_half(tile_columns, lax.ppermute(tile_columns, "dom", swap))
    row_group = (jnp.arange(blocks, dtype=jnp.int32) // group_blocks)[None, :, None]
    slot = jnp.maximum(columns - blocks, 0)
    slot_group, source = slot // part_count, slot % part_count
    zs, ys, los = source // 8, (source // 2) % 4, source % 2
    where = jnp.where(core == 0, ys * 8 + zs * 2, zs * 8 + ys * 2) + los
    idx = jnp.where(
        columns < blocks,
        columns,
        jnp.where(
            slot_group <= row_group,
            blocks + slot_group * part_count + where,
            blocks + groups * part_count,
        ),
    ).reshape(-1).astype(jnp.int32)

    stale = stale_sums(
        tile_columns, adjacency_tiles, stale_imports[:, 0], groups, group_blocks, part_count
    )
    stale = stale.reshape(2, (groups - 1) * group_blocks, 8, piece, width)
    betas = jnp.log(lambda_decay / (jnp.arange(layers, dtype=jnp.float32) + 1.0) + 1.0)

    done = run_layers(idx, picks, betas, adj, weights, initial, stale)

    keep = jnp.where(x_lo == 0, done[0], done[1])
    give = jnp.where(x_lo == 0, done[1], done[0])
    pair = by_half(keep, lax.ppermute(give, "dom", swap))
    cols = width // sections
    split = pair.reshape(2, blocks, piece, sections, cols).transpose(3, 0, 1, 2, 4)
    joined = lax.all_to_all(split, "section", split_axis=0, concat_axis=0, tiled=True)
    order = [0] * 8
    for hi in range(2):
        for c in range(2):
            for lo in range(2):
                first, second = piece_of(hi, lo, c)
                order[c * 4 + first * 2 + second] = (hi * 2 + c) * 2 + lo
    joined = joined.reshape(8, blocks, piece, cols)
    joined = jnp.stack([joined[k] for k in order], 1)
    return joined.reshape(blocks * block, cols)


def solution(mesh):
    return jax.shard_map(
        per_device,
        mesh=mesh,
        in_specs=(
            P("dom", None),
            P("section", None, None),
            P("dom", None, None, None),
            P("dom", None),
            P("dom", None, None),
            P("section", "dom", None, None, None),
        ),
        out_specs=P("dom", "section"),
        check_vma=False,
    )
```

time: 652 us -> 469 us (0.72)
  blocking collectives: 423 us -> 110 us
  Pallas kernels: 147 us -> 324 us
  local copies, waits for them, and re-layouts: 34.1 us -> 6.29 us
  waiting for transfers between devices: 13.9 us -> 3.53 us
  starting transfers between devices: 14.8 us -> 4.92 us
    all_to_all x14 -> x0, blocking collectives: 411 us -> none  [the longest x7 254 us: per_device(): lax.all_to_all(outgoing, 'dom', split_axis=0, concat_axis=0, tiled=True)]
    pallas_call x17 -> x2, Pallas kernels: 129 us -> 305 us  [the longest x1 293 us: run_layers(): pl.pallas_call(main_kernel, out_shape=jax.ShapeDtypeStruct(initial.shape,...]
    all_gather x0 -> x1, blocking collectives: none -> 96.1 us  [per_device(): sends = lax.all_gather(send_blocks[0], 'dom', axis=0, tiled=False)]
    all_to_all x2 -> x0, starting transfers between devices: 14.8 us -> none  [the longest x1 9.8 us: per_device(): lax.all_to_all(outgoing, 'dom', split_axis=0, concat_axis=0, tiled=True)]
    all_to_all x2 -> x0, waiting for transfers between devices: 13.2 us -> none  [the longest x1 13.2 us: per_device(): lax.all_to_all(parts, 'section', split_axis=0, concat_axis=0, tiled=True)]
    dynamic_slice x2 -> x4, local copies, waits for them, and re-layouts: 12.2 us -> 0.58 us  [the longest x2 0.31 us: per_device(): yz = lax.dynamic_index_in_dim(yz, y, 4, keepdims=False)]
    unnamed x12 -> x14, local copies, waits for them, and re-layouts: 11.6 us -> 0.08 us
  transfers between devices with their start and end apart: 3 -> 5, of which waited for: 1 -> 1; matrix products, arithmetic and copies ran while one was open for 5% -> 2% of each run, Pallas kernels for 5% -> 7%
where the time goes in v2:
time: 469 us
  Pallas kernels  324 us (69%)
  blocking collectives  110 us (23%)
  between operations  13.6 us (3%)
  other arithmetic  7.49 us (2%)
  local copies, waits for them, and re-layouts  6.29 us (1%)
  starting transfers between devices  4.92 us (1%)
    pallas_call x1, Pallas kernels, run_layers(): pl.pallas_call(main_kernel, out_shape=jax.ShapeDtypeStruct(initial.shape,...  293 us
    all_gather x1, blocking collectives, per_device(): sends = lax.all_gather(send_blocks[0], 'dom', axis=0, tiled=False)  96.1 us
    pallas_call x1, Pallas kernels, stale_sums(): pl.pallas_call(stale_kernel, out_shape=jax.ShapeDtypeStruct((2, rows, blo...  18.8 us
    all_to_all x1, blocking collectives, per_device(): lax.all_to_all(split, 'section', split_axis=0, concat_axis=0, tiled=True)  13.5 us
    pallas_call x1, Pallas kernels, slice_tiles(): pl.pallas_call(slice_kernel, out_shape=[shape, shape], grid=(blocks,), in...  12.2 us
  transfers between devices with their start and end apart: 5, of which 1 were waited for; matrix products, arithmetic and copies ran while one was open for 2% of the time, Pallas kernels for 7%

profile of v2, /device:TPU:1, one launch (start us, length us, event | category | flops | bytes accessed | tf_op | source)
XLA Modules:
  0.0 469.1 jit_solution(8916290811541604948)
XLA Ops:
  6.5 0.0 all-gather.2.cloned.1.call-start
  6.5 0.7 all-gather.2.cloned.1.call-update
  7.3 2.1 collective-permute-start
  9.4 1.0 dynamic-slice_bitcast_fusion.1
  10.4 0.2 collective-permute-start.2
  10.6 0.8 fusion.1.other_sel_ref
  11.3 0.8 fusion.own_sel_ref
  12.1 0.0 copy-start.2
  12.1 0.0 copy-start.1
  12.1 12.2 %slice_tiles.1 = (bf16[12,128,384]{2,1,0:T(8,128)(2,1)}, bf16[12,128,384]{2,1,0:T(8,128)(2,1)}) custom-call(bf16[12,24,128,128]{3,2,1,0:T(8,128)(2,1)} %adj_ref.3, bf16[1024,128]{1,0:T(8,128)(2,1)} %fusion.own_sel_ref, bf16[1024,128]{1,0:T(8,128)(2,1)} %fusion.1.other_sel_ref), custom_call_target="tpu_custom_call" | custom-call | tf_op jit(solution)/shard_map/slice_tiles/pallas_call | solution.py:99
  24.3 1.4 collective-permute-start.1
  25.7 0.0 copy-done.2
  25.7 0.0 copy-done.1
  25.7 0.1 fusion.26
  25.8 0.2 reduce_window_sum.11
  25.9 96.1 %all_gather.6 = s32[32,3,32]{2,1,0:T(4,128)S(1)} all-gather(s32[1,3,32]{2,1,0:T(4,128)S(1)} %copy.49), channel_id=1, replica_groups=mesh['section'=4,'dom'=32] {'dom'}, dimensions={0}, use_global_device_ids=true | all-gather | bytes 12672 | tf_op jit(solution)/shard_map/all_gather | solution.py:445
  122.0 0.9 reshape.132
  123.0 0.8 slice_reduce_fusion.count_ref
  123.7 0.1 constant_dynamic-slice_fusion
  123.9 0.6 add_log_fusion.beta_ref
  124.5 0.3 copy.51
  124.7 0.3 copy.52
  125.0 0.7 select_reduce_fusion
  125.7 0.3 copy.53
  126.0 0.7 reshape.133.pick_ref
  126.7 0.0 copy-start
  126.7 18.8 %stale_sums.1 = f32[2,8,128,384]{3,2,1,0:T(8,128)} custom-call(s32[8]{0:T(128)} %slice_reduce_fusion.count_ref, s32[8,24]{1,0:T(8,128)} %get-tuple-element.10.tile_ref, s32[8,24]{1,0:T(8,128)} %get-tuple-element.9.col_ref, bf16[12,24,128,128]{3,2,1,0:T(8,128)(2,1)} %adj_ref.3, bf16[2,64,128,384]{3,2,1,0:T(8,128)(2,1)} %bitcast.69), custom_call_target="tpu_custom_call" | custom-call | tf_op jit(solution)/shard_map/stale_sums/pallas_call | solution.py:50
  145.6 0.0 collective-permute-done
  145.6 0.1 compare_select_fusion
  145.7 0.7 reshape.131.idx_ref
  146.3 0.0 collective-permute-done.2
  146.4 0.8 reverse_select_fusion.2.initial_ref
  147.1 0.0 collective-permute-done.1
  147.2 0.0 copy-done
  147.2 0.3 pad_maximum_fusion
  147.4 2.0 reverse_select_fusion.adj_ref
  149.5 0.0 all-gather.2.cloned.1.call-done.weight_ref
  149.5 292.8 %run_layers.1 = bf16[2,12,16,384]{3,2,1,0:T(8,128)(2,1)} custom-call(s32[576]{0:T(1024)} %reshape.131.idx_ref, s32[192]{0:T(256)} %reshape.133.pick_ref, f32[8]{0:T(128)} %add_log_fusion.beta_ref, bf16[2,12,128,384]{3,2,1,0:T(8,128)(2,1)} %reverse_select_fusion.adj_ref, bf16[8,384,384]{2,1,0:T(8,128)(2,1)} %all-gather.2.cloned.1.call-done.weight_ref, ...), custom_call_target="tpu_custom_call" | custom-call | tf_op jit(solution)/shard_map/run_layers/pallas_call | solution.py:398
  442.3 1.0 broadcast_select_fusion
  443.3 1.3 collective-permute-start.3
  444.5 2.8 collective-permute-done.3
  447.4 0.1 reverse_select_fusion.1
  447.5 0.3 reshape.136
  447.7 0.1 copy.63
  447.8 13.5 %all_to_all.5 = bf16[4,2,12,16,96]{4,3,2,1,0:T(8,128)(2,1)S(1)} all-to-all(bf16[4,2,12,16,96]{4,3,2,1,0:T(8,128)(2,1)S(1)} %bitcast.78), channel_id=1, replica_groups=mesh['section'=4,'dom'=32] {'section'}, dimensions={0} | all-to-all | bytes 589824 | tf_op jit(solution)/shard_map/all_to_all | solution.py:483
  461.4 0.9 copy.58
  (21 shorter events, 0.3 us)
Async XLA Ops:
  6.5 142.9 %all-gather.2.cloned.1.call-start = ((), (), s32[]{:S(2)}) async-start(), calls=%async_computation.1 | async-start | bytes 2949120 | tf_op jit(solution)/shard_map/all_gather | solution.py:436
  7.3 138.3 %collective-permute-start = (s32[12,24]{1,0:T(8,128)}, s32[12,24]{1,0:T(8,128)S(1)}, u32[]{:S(2)}, u32[]{:S(2)}) collective-permute-start(s32[12,24]{1,0:T(8,128)} %param.9), channel_id=1, source_target_pairs={{0,1},{1,0},{2,3},{3,2},{4,5},{5,4},{6,7},{7,6},{8,9},{9,8},{10,11... | collective-permute-start | bytes 3464 | tf_op jit(solution)/shard_map/ppermute | solution.py:454
  10.4 136.0 %collective-permute-start.2 = (bf16[12,16,384]{2,1,0:T(8,128)(2,1)S(1)}, bf16[12,16,384]{2,1,0:T(8,128)(2,1)S(1)}, u32[]{:S(2)}, u32[]{:S(2)}) collective-permute-start(bf16[12,16,384]{2,1,0:T(8,128)(2,1)S(1)} %get-tuple-element.14), channel_id=1, source_target_pairs={{0,1},{1,0},{2,3},{3,2},{4,5},{5,4},{6,7},{7,6},{8,9},{9,8},{10,11... | collective-permute-start | bytes 442376 | tf_op jit(solution)/shard_map/ppermute | solution.py:443
  12.1 13.5 %copy-start.2 = (s32[1,3,32]{2,0,1:T(1,128)S(1)}, s32[1,3,32]{2,0,1:T(1,128)}, u32[]{:S(2)}) copy-start(s32[1,3,32]{2,0,1:T(1,128)} %param.10) | copy-start | bytes 1156
  12.1 13.6 %copy-start.1 = (s32[12,24]{1,0:T(8,128)S(1)}, s32[12,24]{1,0:T(8,128)}, u32[]{:S(2)}) copy-start(s32[12,24]{1,0:T(8,128)} %param.9) | copy-start | bytes 3460
  24.3 122.8 %collective-permute-start.1 = (bf16[12,128,384]{2,1,0:T(8,128)(2,1)}, bf16[12,128,384]{2,1,0:T(8,128)(2,1)S(1)}, u32[]{:S(2)}, u32[]{:S(2)}) collective-permute-start(bf16[12,128,384]{2,1,0:T(8,128)(2,1)} %get-tuple-element.8), channel_id=1, source_target_pairs={{0,1},{1,0},{2,3},{3,2},{4,5},{5,4},{6,7},{7,6},{8,9},{9,8},{10,11... | collective-permute-start | bytes 3538952 | tf_op jit(solution)/shard_map/ppermute | solution.py:438
  126.7 20.4 %copy-start = (bf16[12,128,384]{2,1,0:T(8,128)(2,1)S(1)}, bf16[12,128,384]{2,1,0:T(8,128)(2,1)}, u32[]{:S(2)}) copy-start(bf16[12,128,384]{2,1,0:T(8,128)(2,1)} %get-tuple-element.7) | copy-start | bytes 3538948
  443.3 4.1 collective-permute-start.3
Sparse Core Ops, SparseCore 0:
  9.0 40.7 all-gather.1

commit v3 on v2

v3 whole, which is shorter than its diff:
```python
import jax
import jax.numpy as jnp
import numpy as np
from jax import lax
from jax.experimental import pallas as pl
from jax.experimental.pallas import tpu as pltpu
from jax.sharding import PartitionSpec as P

alpha_mix = 0.1
lambda_decay = 0.5

VMEM_LIMIT = 56 * 1024 * 1024


def stale_kernel(count_ref, tile_ref, col_ref, adj_ref, stale_ref, out_ref, acc_ref):
    row = pl.program_id(0)
    count = count_ref[row]
    acc_ref[...] = jnp.zeros_like(acc_ref)

    def body(step, carry):
        first, second = 2 * step, 2 * step + 1
        t0, t1 = tile_ref[row, first], tile_ref[row, second]
        c0, c1 = col_ref[row, first], col_ref[row, second]
        keep = second < count
        right = jnp.where(keep, adj_ref[0, t1], jnp.zeros_like(adj_ref[0, t1]))
        left = jnp.concatenate([adj_ref[0, t0], right], 1)
        for layer in range(2):
            rows = jnp.concatenate([stale_ref[layer, c0], stale_ref[layer, c1]], 0)
            acc_ref[layer] += jnp.dot(left, rows, preferred_element_type=jnp.float32)
        return carry

    lax.fori_loop(0, (count + 1) // 2, body, 0)
    out_ref[:, 0] = acc_ref[...]


def stale_sums(tile_columns, adjacency, stale, groups, group_blocks, part_count):
    blocks, fanout = tile_columns.shape
    block, width = stale.shape[2], stale.shape[3]
    own = blocks
    rows = (groups - 1) * group_blocks
    cols = tile_columns[:rows]
    row_group = (jnp.arange(rows, dtype=jnp.int32) // group_blocks)[:, None]
    is_stale = cols >= own + part_count * (row_group + 1)
    rank = jnp.cumsum(is_stale.astype(jnp.int32), 1)
    places = jnp.arange(fanout, dtype=jnp.int32)[None, None, :]
    hit = is_stale[:, :, None] & (rank[:, :, None] - 1 == places)
    tile_list = jnp.sum(jnp.where(hit, jnp.arange(fanout, dtype=jnp.int32)[None, :, None], 0), 1)
    col_list = jnp.sum(jnp.where(hit, (cols - own - part_count)[:, :, None], 0), 1)
    counts = rank[:, -1]
    return pl.pallas_call(
        stale_kernel,
        out_shape=jax.ShapeDtypeStruct((2, rows, block, width), jnp.float32),
        grid_spec=pltpu.PrefetchScalarGridSpec(
            num_scalar_prefetch=3,
            grid=(rows,),
            in_specs=[
                pl.BlockSpec((1, fanout, block, block), lambda r, *_: (r, 0, 0, 0)),
                pl.BlockSpec(memory_space=pltpu.VMEM),
            ],
            out_specs=pl.BlockSpec((2, 1, block, width), lambda r, *_: (0, r, 0, 0)),
            scratch_shapes=[pltpu.VMEM((2, block, width), jnp.float32)],
        ),
        compiler_params=pltpu.CompilerParams(vmem_limit_bytes=VMEM_LIMIT),
        name="stale_sums",
    )(counts, tile_list, col_list, adjacency, stale)


MESH = pl.DeviceIdType.MESH
GROUPS = 3


def slice_kernel(adj_ref, own_sel_ref, give_sel_ref, own_ref, give_ref):
    per = own_sel_ref.shape[0] // adj_ref.shape[2]
    for m in range(adj_ref.shape[1] // per):
        left = jnp.concatenate([adj_ref[0, m * per + u] for u in range(per)], 1)
        lanes = pl.ds(m * 128, 128)
        own_ref[0, :, lanes] = jnp.dot(
            left, own_sel_ref[...], preferred_element_type=jnp.float32
        ).astype(jnp.bfloat16)
        give_ref[0, :, lanes] = jnp.dot(
            left, give_sel_ref[0], preferred_element_type=jnp.float32
        ).astype(jnp.bfloat16)


def slice_tiles(adjacency, own_slice, near_slice, far_slice, piece):
    blocks, fanout, block, _ = adjacency.shape
    per = block // piece
    source = jnp.arange(per * block, dtype=jnp.int32)[:, None]
    lane = jnp.arange(block, dtype=jnp.int32)[None, :]

    def selector(j):
        wanted = (lane // piece) * block + j * piece + lane % piece
        return (source == wanted).astype(jnp.bfloat16)

    shape = jax.ShapeDtypeStruct((blocks, block, fanout * piece), jnp.bfloat16)
    spec = pl.BlockSpec((1, block, fanout * piece), lambda r: (r, 0, 0))
    whole = pl.BlockSpec((per * block, block), lambda r: (0, 0))
    given = pl.BlockSpec((1, per * block, block), lambda r: ((r % 4) // 3, 0, 0))
    return pl.pallas_call(
        slice_kernel,
        out_shape=[shape, shape],
        grid=(blocks,),
        in_specs=[pl.BlockSpec((1, fanout, block, block), lambda r: (r, 0, 0, 0)), whole, given],
        out_specs=[spec, spec],
        compiler_params=pltpu.CompilerParams(vmem_limit_bytes=VMEM_LIMIT),
        name="slice_tiles",
    )(adjacency, selector(own_slice), jnp.stack([selector(near_slice), selector(far_slice)]))


def place():
    section, dom = lax.axis_index("section"), lax.axis_index("dom")
    x_hi, core = section // 2, section % 2
    z, y, x_lo = dom // 8, (dom // 2) % 4, dom % 2
    return section, dom, x_hi, core, z, y, x_lo


def main_kernel(
    idx_ref, pick_ref, beta_ref, adj_ref, give_ref, weight_ref, initial_ref, stale_ref,
    spread_ref, out_ref, table, part, weights, other, *rest,
):
    rest = list(rest)

    def take(count):
        got = rest[:count]
        del rest[:count]
        return got

    xown, seltab, agbuf, out2, land2 = (take(GROUPS) for _ in range(5))
    send0, recv0, sendx, recvx, keep, fin, finland = (take(GROUPS) for _ in range(7))
    (ag_s, ag_r, sel_s, sel_r, core_s, core_r, x_s, x_r, fin_s, fin_r,
     tile_s, tile_r, w_s, w_r, w_local) = rest

    layers = beta_ref.shape[0]
    fanout = idx_ref.shape[0] // (2 * 4 * GROUPS)
    width = weight_ref.shape[1]
    section, dom, x_hi, core, z, y, x_lo = place()
    x = x_hi * 2 + x_lo
    a = (1 - core) * z + core * y
    b = (1 - core) * y + core * z

    def on_a(step):
        zz, yy = (z + (1 - core) * step) % 4, (y + core * step) % 4
        return (section, zz * 8 + yy * 2 + x_lo)

    def on_b(step):
        zz, yy = (z + core * step) % 4, (y + (1 - core) * step) % 4
        return (section, zz * 8 + yy * 2 + x_lo)

    def on_x(step, other_core=0):
        xx = (x + step) % 4
        cc = (core + other_core) % 2
        return ((xx // 2) * 2 + cc, z * 8 + y * 2 + xx % 2)

    steps = (1, 3, 2)
    partner = on_x(0, 1)
    near = (section, z * 8 + y * 2 + 1 - x_lo)
    far = ((1 - x_hi) * 2 + core, z * 8 + y * 2 + 1 - x_lo)

    barrier = pltpu.get_barrier_semaphore()
    friends = [on_a(s) for s in steps] + [on_b(s) for s in steps] + [partner]
    friends += [on_x(s, c) for s in steps for c in range(2)]
    for friend in friends:
        pl.semaphore_signal(barrier, inc=1, device_id=friend, device_id_type=MESH)
    pl.semaphore_wait(barrier, len(friends))

    def remote(src, dst, ssem, rsem, device):
        return pltpu.make_async_remote_copy(
            src_ref=src, dst_ref=dst, send_sem=ssem, recv_sem=rsem,
            device_id=device, device_id_type=MESH,
        )

    def gather(g, par, d):
        return remote(xown[g], agbuf[g].at[par, d], ag_s.at[g * 3 + d],
                      ag_r.at[(g * 2 + par) * 3 + d], on_a(steps[d]))

    def choose(g, par, d):
        return remote(out2[g].at[d], land2[g].at[par, d], sel_s.at[g * 3 + d],
                      sel_r.at[(g * 2 + par) * 3 + d], on_b(steps[d]))

    def to_core(g, par):
        return remote(send0[g], recv0[g].at[par], core_s.at[g], core_r.at[g * 2 + par], partner)

    def to_x(g, par, d):
        return remote(sendx[g].at[d], recvx[g].at[par, d], x_s.at[g * 3 + d],
                      x_r.at[(g * 2 + par) * 3 + d], on_x(steps[d]))

    hops = [(s, c) for s in (1, 3, 2, 0) for c in range(2) if (s, c) != (0, 0)]

    def to_out(g, n):
        s, c = hops[n]
        target = (x + s) % 4
        return remote(fin[g].at[(target // 2) * 2 + (core + c) % 2, target % 2], finland[g].at[n],
                      fin_s.at[g * 7 + n], fin_r.at[g * 7 + n], on_x(s, c))

    def give_near(g):
        rows = pl.ds(4 * g, 3)
        return remote(give_ref.at[rows], other.at[rows], tile_s.at[g * 2], tile_r.at[g * 2], near)

    def give_far(g):
        rows = pl.ds(4 * g + 3, 1)
        return remote(give_ref.at[rows], other.at[rows], tile_s.at[g * 2 + 1],
                      tile_r.at[g * 2 + 1], far)

    far_section = (1 - x_hi) * 2 + core
    weight_keep = pltpu.make_async_copy(weight_ref, weights.at[section], w_local)
    weight_core = remote(weight_ref, weights.at[section], w_s.at[0], w_r.at[0], partner)
    weight_far = remote(weight_ref, weights.at[section], w_s.at[1], w_r.at[1], far)
    weight_pass = remote(weights.at[far_section], weights.at[far_section], w_s.at[2], w_r.at[2],
                         partner)

    def stage_a(g, layer):
        par = layer % 2
        for d in range(3):
            gather(g, par, d).wait_recv()
            seltab[g][(a + 4 - steps[d]) % 4] = agbuf[g][par, d]
        for d in (2, 0, 1):
            for half in range(2):
                for line in range(4):
                    for lo in range(2):
                        out2[g][d, half, line, lo] = chosen(
                            g, (b + steps[d]) % 4, half, line, lo
                        )
            choose(g, par, d).start()

    def chosen(g, dest, half, line, lo):
        which = (((g * 4 + dest) * 2 + half) * 4 + line) * 2 + lo
        return seltab[g][line, lo, pick_ref[which]]

    def stage_d(g, layer):
        par = layer % 2
        for half in range(2):
            table[half, pl.ds(4 * g, 4)] = xown[g][half]
            for line in range(4):
                for lo in range(2):
                    slot = 4 * GROUPS + g * 32 + b * 8 + line * 2 + lo
                    table[half, slot] = chosen(g, b, half, line, lo)
        for d in range(3):
            choose(g, par, d).wait_recv()
            slots = pl.ds(4 * GROUPS + g * 32 + ((b + 4 - steps[d]) % 4) * 8, 8)
            for half in range(2):
                table[half, slots] = land2[g][par, d, half].reshape(8, 16, width)

        @pl.when(layer == 0)
        def _():
            give_near(g).wait_recv()
            give_far(g).wait_recv()

        for tiles, half in ((adj_ref, x_lo), (other, 1 - x_lo)):
            def row_block(j, carry, tiles=tiles, half=half):
                row = g * 4 + j
                base = (half * 4 * GROUPS + row) * fanout
                rows = jnp.concatenate([table[half, idx_ref[base + t]] for t in range(fanout)], 0)
                total = jnp.dot(tiles[row], rows, preferred_element_type=jnp.float32)
                part[half * 4 + j] = total.reshape(8, 16, width)
                return carry

            lax.fori_loop(0, 4, row_block, 0, unroll=True)

        if g < GROUPS - 1:
            @pl.when(section == layer // 2)
            def _():
                for j in range(4):
                    part[x_lo * 4 + j] += stale_ref[layer % 2, g * 4 + j]

        for j in range(8):
            send0[g][j] = part[j, pl.ds((1 - core) * 4, 4)].astype(jnp.bfloat16)
        to_core(g, par).start()
        for d in range(3):
            gather(g, par, d).wait_send()

    def stage_e(g, layer):
        par = layer % 2
        to_core(g, par).wait_recv()

        def summed(j, piece):
            return part[j, core * 4 + piece] + recv0[g][par, j, piece].astype(jnp.float32)

        for d in (2, 0, 1):
            piece = (x + steps[d]) % 4
            for j in range(8):
                sendx[g][d, j] = summed(j, piece).astype(jnp.bfloat16)
            to_x(g, par, d).start()
        for j in range(8):
            keep[g][j] = summed(j, x)
        for d in range(3):
            choose(g, par, d).wait_send()

    def stage_h(g, layer):
        par = layer % 2
        total = keep[g][...]
        for d in range(3):
            to_x(g, par, d).wait_recv()
            total = total + recvx[g][par, d].astype(jnp.float32)
        start = jnp.concatenate([initial_ref[half, pl.ds(4 * g, 4)] for half in range(2)], 0)
        mixed = (1.0 - alpha_mix) * total + alpha_mix * start.astype(jnp.float32)
        mixed = mixed.astype(jnp.bfloat16).reshape(8 * 16, width)
        beta = beta_ref[layer]
        weight = weights[layer // 2, layer % 2]
        product = jnp.dot(mixed, weight, preferred_element_type=jnp.float32)
        value = (1.0 - beta) * mixed.astype(jnp.float32) + beta * product
        value = jnp.maximum(value, 0.0).astype(jnp.bfloat16)

        @pl.when(layer < layers - 1)
        def _():
            shaped = value.reshape(2, 4, 16, width)
            xown[g][...] = shaped
            for d in (2, 0, 1):
                gather(g, 1 - par, d).start()
            seltab[g][a] = shaped

        @pl.when(layer == layers - 1)
        def _():
            wide = jnp.dot(value, spread_ref[...], preferred_element_type=jnp.float32)
            wide = wide.astype(jnp.bfloat16)
            for target in range(4):
                lanes = wide[:, target * 128:(target + 1) * 128]
                fin[g][target] = lanes.reshape(2, 4, 16, 128)
            for n in range(len(hops)):
                to_out(g, n).start()

        to_core(g, par).wait_send()
        for d in range(3):
            to_x(g, par, d).wait_send()

    for half in range(2):
        table[half, 4 * GROUPS + 96] = jnp.zeros((16, width), jnp.bfloat16)
    for g in range(GROUPS):
        for half in range(2):
            xown[g][half] = initial_ref[half, pl.ds(4 * g, 4)]
        for d in (2, 0, 1):
            gather(g, 0, d).start()
        for half in range(2):
            seltab[g][a, half] = initial_ref[half, pl.ds(4 * g, 4)]
    weight_keep.start()
    weight_core.start()
    give_near(0).start()
    give_far(0).start()
    weight_far.start()
    for g in range(1, GROUPS):
        give_near(g).start()
        give_far(g).start()

    def body(layer, carry):
        for g in range(GROUPS):
            if g == 2:
                @pl.when(layer == 0)
                def _():
                    weight_pass.wait_recv()

            for stage, back in ORDER:
                turn = g - back
                if turn >= 0:
                    @pl.when(layer < layers)
                    def _(stage=stage, turn=turn):
                        run[stage](turn, layer)
                else:
                    @pl.when(layer > 0)
                    def _(stage=stage, turn=turn):
                        run[stage](turn + GROUPS, layer - 1)

            if g == 0:
                @pl.when(layer == 0)
                def _():
                    weight_far.wait_recv()
                    weight_pass.start()
                    weight_keep.wait()
                    weight_core.wait_recv()
        return carry

    run = {"a": stage_a, "d": stage_d, "e": stage_e, "h": stage_h}
    lax.fori_loop(0, layers + 1, body, 0)

    for g in range(GROUPS):
        rows = pl.ds(4 * g, 4)
        mine = fin[g][section, x_lo]
        out_ref[rows, core * 4 + x] = mine
        for n, (s, c) in enumerate(hops):
            to_out(g, n).wait_recv()
            piece = ((core + c) % 2) * 4 + (x + 4 - s) % 4
            out_ref[rows, piece] = finland[g][n]
        for n in range(len(hops)):
            to_out(g, n).wait_send()
        give_near(g).wait_send()
        give_far(g).wait_send()
    weight_core.wait_send()
    weight_far.wait_send()
    weight_pass.wait_send()


ORDER = (("a", 0), ("d", 1), ("h", 2), ("e", 1))


def run_layers(idx, picks, betas, adj, give, weights, initial, stale, spread):
    depth, width = weights.shape[:2]
    blocks, piece = initial.shape[1:3]
    dt = jnp.bfloat16
    slab = (piece, width)

    def each(shape, dtype=dt, tail=slab):
        return [pltpu.VMEM((*shape, *tail), dtype) for _ in range(GROUPS)]

    sems = pltpu.SemaphoreType.DMA
    scratch = [
        pltpu.VMEM((2, 4 * GROUPS + 97, *slab), dt),
        pltpu.VMEM((8, 8, *slab), jnp.float32),
        pltpu.VMEM((4, *weights.shape), dt),
        pltpu.VMEM(adj.shape, dt),
        *each((2, 4)), *each((4, 2, 4)), *each((2, 3, 2, 4)),
        *each((3, 2, 4, 2)), *each((2, 3, 2, 4, 2)),
        *each((8, 4)), *each((2, 8, 4)),
        *each((3, 8)), *each((2, 3, 8)), *each((8,), jnp.float32),
        *each((4, 2, 4), dt, (piece, 128)), *each((7, 4), dt, (piece, 128)),
        sems((9,)), sems((18,)), sems((9,)), sems((18,)), sems((3,)), sems((6,)),
        sems((9,)), sems((18,)), sems((21,)), sems((21,)), sems((6,)), sems((6,)),
        sems((3,)), sems((3,)), sems,
    ]
    smem = pl.BlockSpec(memory_space=pltpu.SMEM)
    vmem = pl.BlockSpec(memory_space=pltpu.VMEM)
    return pl.pallas_call(
        main_kernel,
        out_shape=jax.ShapeDtypeStruct((blocks, 8, piece, 128), dt),
        in_specs=[smem] * 3 + [vmem] * 6,
        out_specs=vmem,
        scratch_shapes=scratch,
        compiler_params=pltpu.CompilerParams(
            vmem_limit_bytes=VMEM_LIMIT, collective_id=0, has_side_effects=True
        ),
        name="run_layers",
    )(idx, picks, betas, adj, give, weights, initial, stale, spread)


def per_device(
    initial_features, layer_weights, adjacency_tiles, tile_columns, send_blocks, stale_imports
):
    section, dom, x_hi, core, z, y, x_lo = place()
    sections = lax.axis_size("section")
    part_count = lax.axis_size("dom")
    blocks, fanout, block = adjacency_tiles.shape[:3]
    width = initial_features.shape[1]
    groups = send_blocks.shape[1]
    group_blocks = blocks // groups
    layers = layer_weights.shape[0] * sections
    piece = block // 8

    def number(hi, lo):
        return core * 4 + hi * 2 + lo

    mine = number(x_hi, x_lo)
    near, far = number(x_hi, 1 - x_lo), number(1 - x_hi, 1 - x_lo)
    swap = [(p, p + 1 - 2 * (p % 2)) for p in range(part_count)]

    def by_half(own, other):
        pair = jnp.stack([own, other])
        return jnp.where(x_lo == 0, pair, pair[::-1])

    init_blocks = initial_features.reshape(blocks, 8, piece, width)
    own_init = lax.dynamic_index_in_dim(init_blocks, mine, 1, keepdims=False)
    other_init = lax.dynamic_index_in_dim(init_blocks, near, 1, keepdims=False)
    other_init = lax.ppermute(other_init, "dom", swap)

    numbers = jnp.concatenate([send_blocks.reshape(-1), tile_columns.reshape(-1)])
    numbers = by_half(numbers, lax.ppermute(numbers, "dom", swap))
    sends = jnp.maximum(numbers[:, : groups * part_count], 0)
    columns = numbers[:, groups * part_count :].reshape(2, blocks, fanout)

    def along(step):
        moves = []
        for s in range(sections):
            for p in range(part_count):
                pz, py, lo = p // 8, (p // 2) % 4, p % 2
                q = (
                    ((pz + step) % 4) * 8 + py * 2 + lo
                    if s % 2 == 0
                    else pz * 8 + ((py + step) % 4) * 2 + lo
                )
                moves.append((s * part_count + p, s * part_count + q))
        return moves

    lines = jnp.stack(
        [sends] + [lax.ppermute(sends, ("section", "dom"), along(step)) for step in (1, 2, 3)]
    )
    a = jnp.where(core == 0, z, y)
    lines = lines[(a - jnp.arange(4, dtype=jnp.int32)) % 4]
    lines = lines.reshape(4, 2, groups, 4, 4, 2)
    to_y = lax.dynamic_index_in_dim(lines, z, 3, keepdims=False)
    to_z = lax.dynamic_index_in_dim(lines, y, 4, keepdims=False)
    picks = jnp.where(core == 0, to_y, to_z)
    picks = picks.transpose(2, 3, 4, 0, 1).reshape(-1).astype(jnp.int32)

    row_group = (jnp.arange(blocks, dtype=jnp.int32) // group_blocks)[None, :, None]
    slot = jnp.maximum(columns - blocks, 0)
    slot_group, source = slot // part_count, slot % part_count
    zs, ys, los = source // 8, (source // 2) % 4, source % 2
    where = jnp.where(core == 0, ys * 8 + zs * 2, zs * 8 + ys * 2) + los
    idx = jnp.where(
        columns < blocks,
        columns,
        jnp.where(
            slot_group <= row_group,
            blocks + slot_group * part_count + where,
            blocks + groups * part_count,
        ),
    ).reshape(-1).astype(jnp.int32)

    own_adj, give_adj = slice_tiles(adjacency_tiles, mine, near, far, piece)
    stale = stale_sums(
        tile_columns, adjacency_tiles, stale_imports[:, 0], groups, group_blocks, part_count
    )
    stale = stale.reshape(2, (groups - 1) * group_blocks, 8, piece, width)
    betas = jnp.log(lambda_decay / (jnp.arange(layers, dtype=jnp.float32) + 1.0) + 1.0)
    initial = by_half(own_init, other_init)
    cols = width // sections
    source = jnp.arange(width, dtype=jnp.int32)[:, None]
    lane = jnp.arange(sections * 128, dtype=jnp.int32)[None, :]
    spread = (source == (lane // 128) * cols + lane % 128) & (lane % 128 < cols)

    done = run_layers(
        idx, picks, betas, own_adj, give_adj, layer_weights, initial, stale,
        spread.astype(jnp.bfloat16),
    )
    return done.reshape(blocks * block, 128)[:, :cols]


def solution(mesh):
    return jax.shard_map(
        per_device,
        mesh=mesh,
        in_specs=(
            P("dom", None),
            P("section", None, None),
            P("dom", None, None, None),
            P("dom", None),
            P("dom", None, None),
            P("section", "dom", None, None, None),
        ),
        out_specs=P("dom", "section"),
        check_vma=False,
    )
```

time: 469 us -> 294 us (0.63)
  blocking collectives: 110 us -> 0 us
  Pallas kernels: 324 us -> 269 us
  between operations: 13.6 us -> 0.14 us
    all_gather x1 -> x0, blocking collectives: 96.1 us -> none  [per_device(): sends = lax.all_gather(send_blocks[0], 'dom', axis=0, tiled=False)]
    pallas_call x1, Pallas kernels: 293 us -> 240 us  [run_layers(): pl.pallas_call(main_kernel, out_shape=jax.ShapeDtypeStruct((blocks, 8, pi...]
    all_to_all x1 -> x0, blocking collectives: 13.5 us -> none  [per_device(): lax.all_to_all(split, 'section', split_axis=0, concat_axis=0, tiled=True)]
  transfers between devices with their start and end apart: 5 -> 5, of which waited for: 1 -> 1; matrix products, arithmetic and copies ran while one was open for 2% -> 4% of each run, Pallas kernels for 7% -> 10%
where the time goes in v3:
time: 294 us; the launch traced here: 293 us
  Pallas kernels  269 us (91%)
  starting transfers between devices  8.67 us (3%)
  other arithmetic  8.04 us (3%)
  local copies, waits for them, and re-layouts  6.89 us (2%)
    pallas_call x1, Pallas kernels, run_layers(): pl.pallas_call(main_kernel, out_shape=jax.ShapeDtypeStruct((blocks, 8, pi...  240 us
    pallas_call x1, Pallas kernels, stale_sums(): pl.pallas_call(stale_kernel, out_shape=jax.ShapeDtypeStruct((2, rows, blo...  16.6 us
    pallas_call x1, Pallas kernels, slice_tiles(): pl.pallas_call(slice_kernel, out_shape=[shape, shape], grid=(blocks,), in...  12.4 us
    ppermute x3, starting transfers between devices, per_device(): lax.ppermute(sends, ('section', 'dom'), along(step))  6.47 us
  transfers between devices with their start and end apart: 5, of which 1 were waited for; matrix products, arithmetic and copies ran while one was open for 4% of the time, Pallas kernels for 10%

profile of v3, /device:TPU:1, one launch (start us, length us, event | category | flops | bytes accessed | tf_op | source)
XLA Modules:
  0.0 292.7 jit_solution(18267779748087500058)
XLA Ops:
  0.0 0.7 reduce
  0.7 0.1 reshape.306
  0.8 0.8 reshape.307
  1.6 0.1 pad_add_fusion.2
  1.6 2.0 collective-permute-start
  3.7 1.0 dynamic-slice_bitcast_fusion.1
  4.7 0.1 collective-permute-start.4
  4.9 0.6 add_log_fusion.beta_ref
  5.5 0.7 slice_add_fusion
  6.2 0.8 fusion.32
  6.9 0.2 reduce_window_sum.11
  7.1 0.7 slice_reduce_fusion.count_ref
  7.9 0.1 iota_compare_fusion.2
  8.0 0.1 iota_compare_fusion.1
  8.0 0.8 fusion.2.own_sel_ref
  8.8 0.9 add_convert_fusion.give_sel_ref
  9.7 0.9 fusion.1.spread_ref
  10.6 0.7 select_reduce_fusion
  11.4 0.1 le.11
  11.5 0.1 le.12
  11.6 12.4 %slice_tiles.1 = (bf16[12,128,384]{2,1,0:T(8,128)(2,1)}, bf16[12,128,384]{2,1,0:T(8,128)(2,1)}) custom-call(bf16[12,24,128,128]{3,2,1,0:T(8,128)(2,1)} %adj_ref.3, bf16[1024,128]{1,0:T(8,128)(2,1)} %fusion.2.own_sel_ref, bf16[2,1024,128]{2,1,0:T(8,128)(2,1)} %add_convert_fusion.give_sel_ref), custom_call_target="tpu_custom_call" | custom-call | tf_op jit(solution)/shard_map/slice_tiles/pallas_call | solution.py:99
  23.9 16.6 %stale_sums.1 = f32[2,8,128,384]{3,2,1,0:T(8,128)} custom-call(s32[8]{0:T(128)} %slice_reduce_fusion.count_ref, s32[8,24]{1,0:T(8,128)} %get-tuple-element.10.tile_ref, s32[8,24]{1,0:T(8,128)} %get-tuple-element.9.col_ref, bf16[12,24,128,128]{3,2,1,0:T(8,128)(2,1)} %adj_ref.3, bf16[2,64,128,384]{3,2,1,0:T(8,128)(2,1)} %bitcast.31), custom_call_target="tpu_custom_call" | custom-call | tf_op jit(solution)/shard_map/stale_sums/pallas_call | solution.py:50
  40.5 0.0 collective-permute-done
  40.5 0.1 rev.6
  40.7 0.1 slice.22
  40.8 3.8 %collective-permute-start.2 = (s32[2,96]{1,0:T(2,128)S(1)}, s32[2,96]{1,0:T(2,128)S(1)}, u32[]{:S(2)}, u32[]{:S(2)}) collective-permute-start(s32[2,96]{1,0:T(2,128)S(1)} %get-tuple-element.16), channel_id=1, source_target_pairs={{0,16},{1,17},{2,18},{3,19},{4,20},{5,21},{6,22},{7,23},{8,24},{9,... | collective-permute-start | bytes 2312 | tf_op jit(solution)/shard_map/ppermute | solution.py:480
  44.6 0.0 collective-permute-start.1
  44.6 2.7 collective-permute-start.3
  47.2 0.1 reshape.308
  47.3 0.6 compare_select_fusion.idx_ref
  47.9 0.0 collective-permute-done.2
  47.9 0.4 collective-permute-done.1
  48.3 0.0 collective-permute-done.3
  48.3 0.6 gather_fusion
  48.9 0.1 copy.20
  49.1 0.2 copy.21
  49.2 0.2 copy.22
  49.4 0.3 copy.23
  49.7 0.7 reshape.310.pick_ref
  50.4 0.0 collective-permute-done.4
  50.4 0.8 reverse_select_fusion.initial_ref
  51.2 239.6 %run_layers.1 = bf16[12,8,16,128]{3,2,1,0:T(8,128)(2,1)} custom-call(s32[576]{0:T(1024)} %compare_select_fusion.idx_ref, s32[192]{0:T(256)} %reshape.310.pick_ref, f32[8]{0:T(128)} %add_log_fusion.beta_ref, bf16[12,128,384]{2,1,0:T(8,128)(2,1)} %get-tuple-element.7.adj_ref, bf16[12,128,384]{2,1,0:T(8,128)(2,1)} %get-tuple-element.8.give_ref, ...), custom_call_target="tpu_custom_call" | custom-call | tf_op jit(solution)/shard_map/run_layers/pallas_call | solution.py:419
  290.8 1.9 copy.29
  (19 shorter events, 0.2 us)
Async XLA Ops:
  1.6 38.9 %collective-permute-start = (s32[384]{0:T(512)S(1)}, s32[384]{0:T(512)S(1)}, u32[]{:S(2)}, u32[]{:S(2)}) collective-permute-start(s32[384]{0:T(512)S(1)} %pad_add_fusion.2), channel_id=1, source_target_pairs={{0,1},{1,0},{2,3},{3,2},{4,5},{5,4},{6,7},{7,6},{8,9},{9,8},{10,11... | collective-permute-start | bytes 4616 | tf_op jit(solution)/shard_map/ppermute | solution.py:462
  4.7 45.7 %collective-permute-start.4 = (bf16[12,16,384]{2,1,0:T(8,128)(2,1)S(1)}, bf16[12,16,384]{2,1,0:T(8,128)(2,1)S(1)}, u32[]{:S(2)}, u32[]{:S(2)}) collective-permute-start(bf16[12,16,384]{2,1,0:T(8,128)(2,1)S(1)} %get-tuple-element.14), channel_id=1, source_target_pairs={{0,1},{1,0},{2,3},{3,2},{4,5},{5,4},{6,7},{7,6},{8,9},{9,8},{10,11... | collective-permute-start | bytes 442376 | tf_op jit(solution)/shard_map/ppermute | solution.py:459
  40.8 7.2 %collective-permute-start.2 = (s32[2,96]{1,0:T(2,128)S(1)}, s32[2,96]{1,0:T(2,128)S(1)}, u32[]{:S(2)}, u32[]{:S(2)}) collective-permute-start(s32[2,96]{1,0:T(2,128)S(1)} %get-tuple-element.16), channel_id=1, source_target_pairs={{0,16},{1,17},{2,18},{3,19},{4,20},{5,21},{6,22},{7,23},{8,24},{9,... | collective-permute-start | bytes 2312 | tf_op jit(solution)/shard_map/ppermute | solution.py:480
  44.6 3.7 %collective-permute-start.1 = (s32[2,96]{1,0:T(2,128)S(1)}, s32[2,96]{1,0:T(2,128)S(1)}, u32[]{:S(2)}, u32[]{:S(2)}) collective-permute-start(s32[2,96]{1,0:T(2,128)S(1)} %get-tuple-element.16), channel_id=1, source_target_pairs={{0,8},{1,9},{2,10},{3,11},{4,12},{5,13},{6,14},{7,15},{8,16},{9,17... | collective-permute-start | bytes 2312 | tf_op jit(solution)/shard_map/ppermute | solution.py:480
  44.6 3.7 %collective-permute-start.3 = (s32[2,96]{1,0:T(2,128)S(1)}, s32[2,96]{1,0:T(2,128)S(1)}, u32[]{:S(2)}, u32[]{:S(2)}) collective-permute-start(s32[2,96]{1,0:T(2,128)S(1)} %get-tuple-element.16), channel_id=1, source_target_pairs={{0,24},{1,25},{2,26},{3,27},{4,28},{5,29},{6,30},{7,31},{8,0},{9,1... | collective-permute-start | bytes 2312 | tf_op jit(solution)/shard_map/ppermute | solution.py:480

commit v4 on v3

--- a/solution.py
+++ b/solution.py
@@ -12,99 +12,8 @@
 VMEM_LIMIT = 56 * 1024 * 1024
 
 
-def stale_kernel(count_ref, tile_ref, col_ref, adj_ref, stale_ref, out_ref, acc_ref):
-    row = pl.program_id(0)
-    count = count_ref[row]
-    acc_ref[...] = jnp.zeros_like(acc_ref)
-
-    def body(step, carry):
-        first, second = 2 * step, 2 * step + 1
-        t0, t1 = tile_ref[row, first], tile_ref[row, second]
-        c0, c1 = col_ref[row, first], col_ref[row, second]
-        keep = second < count
-        right = jnp.where(keep, adj_ref[0, t1], jnp.zeros_like(adj_ref[0, t1]))
-        left = jnp.concatenate([adj_ref[0, t0], right], 1)
-        for layer in range(2):
-            rows = jnp.concatenate([stale_ref[layer, c0], stale_ref[layer, c1]], 0)
-            acc_ref[layer] += jnp.dot(left, rows, preferred_element_type=jnp.float32)
-        return carry
-
-    lax.fori_loop(0, (count + 1) // 2, body, 0)
-    out_ref[:, 0] = acc_ref[...]
-
-
-def stale_sums(tile_columns, adjacency, stale, groups, group_blocks, part_count):
-    blocks, fanout = tile_columns.shape
-    block, width = stale.shape[2], stale.shape[3]
-    own = blocks
-    rows = (groups - 1) * group_blocks
-    cols = tile_columns[:rows]
-    row_group = (jnp.arange(rows, dtype=jnp.int32) // group_blocks)[:, None]
-    is_stale = cols >= own + part_count * (row_group + 1)
-    rank = jnp.cumsum(is_stale.astype(jnp.int32), 1)
-    places = jnp.arange(fanout, dtype=jnp.int32)[None, None, :]
-    hit = is_stale[:, :, None] & (rank[:, :, None] - 1 == places)
-    tile_list = jnp.sum(jnp.where(hit, jnp.arange(fanout, dtype=jnp.int32)[None, :, None], 0), 1)
-    col_list = jnp.sum(jnp.where(hit, (cols - own - part_count)[:, :, None], 0), 1)
-    counts = rank[:, -1]
-    return pl.pallas_call(
-        stale_kernel,
-        out_shape=jax.ShapeDtypeStruct((2, rows, block, width), jnp.float32),
-        grid_spec=pltpu.PrefetchScalarGridSpec(
-            num_scalar_prefetch=3,
-            grid=(rows,),
-            in_specs=[
-                pl.BlockSpec((1, fanout, block, block), lambda r, *_: (r, 0, 0, 0)),
-                pl.BlockSpec(memory_space=pltpu.VMEM),
-            ],
-            out_specs=pl.BlockSpec((2, 1, block, width), lambda r, *_: (0, r, 0, 0)),
-            scratch_shapes=[pltpu.VMEM((2, block, width), jnp.float32)],
-        ),
-        compiler_params=pltpu.CompilerParams(vmem_limit_bytes=VMEM_LIMIT),
-        name="stale_sums",
-    )(counts, tile_list, col_list, adjacency, stale)
-
-
 MESH = pl.DeviceIdType.MESH
 GROUPS = 3
-
-
-def slice_kernel(adj_ref, own_sel_ref, give_sel_ref, own_ref, give_ref):
-    per = own_sel_ref.shape[0] // adj_ref.shape[2]
-    for m in range(adj_ref.shape[1] // per):
-        left = jnp.concatenate([adj_ref[0, m * per + u] for u in range(per)], 1)
-        lanes = pl.ds(m * 128, 128)
-        own_ref[0, :, lanes] = jnp.dot(
-            left, own_sel_ref[...], preferred_element_type=jnp.float32
-        ).astype(jnp.bfloat16)
-        give_ref[0, :, lanes] = jnp.dot(
-            left, give_sel_ref[0], preferred_element_type=jnp.float32
-        ).astype(jnp.bfloat16)
-
-
-def slice_tiles(adjacency, own_slice, near_slice, far_slice, piece):
-    blocks, fanout, block, _ = adjacency.shape
-    per = block // piece
-    source = jnp.arange(per * block, dtype=jnp.int32)[:, None]
-    lane = jnp.arange(block, dtype=jnp.int32)[None, :]
-
-    def selector(j):
-        wanted = (lane // piece) * block + j * piece + lane % piece
-        return (source == wanted).astype(jnp.bfloat16)
-
-    shape = jax.ShapeDtypeStruct((blocks, block, fanout * piece), jnp.bfloat16)
-    spec = pl.BlockSpec((1, block, fanout * piece), lambda r: (r, 0, 0))
-    whole = pl.BlockSpec((per * block, block), lambda r: (0, 0))
-    given = pl.BlockSpec((1, per * block, block), lambda r: ((r % 4) // 3, 0, 0))
-    return pl.pallas_call(
-        slice_kernel,
-        out_shape=[shape, shape],
-        grid=(blocks,),
-        in_specs=[pl.BlockSpec((1, fanout, block, block), lambda r: (r, 0, 0, 0)), whole, given],
-        out_specs=[spec, spec],
-        compiler_params=pltpu.CompilerParams(vmem_limit_bytes=VMEM_LIMIT),
-        name="slice_tiles",
-    )(adjacency, selector(own_slice), jnp.stack([selector(near_slice), selector(far_slice)]))
 
 
 def place():
@@ -115,8 +24,8 @@
 
 
 def main_kernel(
-    idx_ref, pick_ref, beta_ref, adj_ref, give_ref, weight_ref, initial_ref, stale_ref,
-    spread_ref, out_ref, table, part, weights, other, *rest,
+    idx_ref, pick_ref, old_ref, beta_ref, tiles_ref, stale_ref, weight_ref, initial_ref,
+    cut_ref, spread_ref, out_ref, table, part, weights, mine, give, other, tiles, stale, old, *rest,
 ):
     rest = list(rest)
 
@@ -128,7 +37,7 @@
     xown, seltab, agbuf, out2, land2 = (take(GROUPS) for _ in range(5))
     send0, recv0, sendx, recvx, keep, fin, finland = (take(GROUPS) for _ in range(7))
     (ag_s, ag_r, sel_s, sel_r, core_s, core_r, x_s, x_r, fin_s, fin_r,
-     tile_s, tile_r, w_s, w_r, w_local) = rest
+     tile_s, tile_r, w_s, w_r, w_local, load) = rest
 
     layers = beta_ref.shape[0]
     fanout = idx_ref.shape[0] // (2 * 4 * GROUPS)
@@ -173,9 +82,9 @@
         return remote(xown[g], agbuf[g].at[par, d], ag_s.at[g * 3 + d],
                       ag_r.at[(g * 2 + par) * 3 + d], on_a(steps[d]))
 
-    def choose(g, par, d):
-        return remote(out2[g].at[d], land2[g].at[par, d], sel_s.at[g * 3 + d],
-                      sel_r.at[(g * 2 + par) * 3 + d], on_b(steps[d]))
+    def choose(g, par, d, n):
+        return remote(out2[g].at[d, n], land2[g].at[par, d, n], sel_s.at[(g * 3 + d) * 4 + n],
+                      sel_r.at[((g * 2 + par) * 3 + d) * 4 + n], on_b(steps[d]))
 
     def to_core(g, par):
         return remote(send0[g], recv0[g].at[par], core_s.at[g], core_r.at[g * 2 + par], partner)
@@ -194,11 +103,11 @@
 
     def give_near(g):
         rows = pl.ds(4 * g, 3)
-        return remote(give_ref.at[rows], other.at[rows], tile_s.at[g * 2], tile_r.at[g * 2], near)
+        return remote(give.at[rows], other.at[rows], tile_s.at[g * 2], tile_r.at[g * 2], near)
 
     def give_far(g):
         rows = pl.ds(4 * g + 3, 1)
-        return remote(give_ref.at[rows], other.at[rows], tile_s.at[g * 2 + 1],
+        return remote(give.at[rows], other.at[rows], tile_s.at[g * 2 + 1],
                       tile_r.at[g * 2 + 1], far)
 
     far_section = (1 - x_hi) * 2 + core
@@ -208,49 +117,54 @@
     weight_pass = remote(weights.at[far_section], weights.at[far_section], w_s.at[2], w_r.at[2],
                          partner)
 
+    lines = [a] + [(a + 4 - step) % 4 for step in steps]
+
+    def chosen(g, dest, half, n, lo):
+        which = (((g * 4 + dest) * 2 + half) * 4 + lines[n]) * 2 + lo
+        return seltab[g][n, lo, pick_ref[which]]
+
+    def send_chosen(g, par, n):
+        for d in (2, 0, 1):
+            for half in range(2):
+                for lo in range(2):
+                    out2[g][d, n, half, lo] = chosen(g, (b + steps[d]) % 4, half, n, lo)
+            choose(g, par, d, n).start()
+
     def stage_a(g, layer):
         par = layer % 2
         for d in range(3):
             gather(g, par, d).wait_recv()
-            seltab[g][(a + 4 - steps[d]) % 4] = agbuf[g][par, d]
-        for d in (2, 0, 1):
-            for half in range(2):
-                for line in range(4):
-                    for lo in range(2):
-                        out2[g][d, half, line, lo] = chosen(
-                            g, (b + steps[d]) % 4, half, line, lo
-                        )
-            choose(g, par, d).start()
-
-    def chosen(g, dest, half, line, lo):
-        which = (((g * 4 + dest) * 2 + half) * 4 + line) * 2 + lo
-        return seltab[g][line, lo, pick_ref[which]]
+            seltab[g][d + 1] = agbuf[g][par, d]
+            send_chosen(g, par, d + 1)
+
+    def slot_of(g, place_b, n):
+        return 4 * GROUPS + g * 32 + place_b * 8 + lines[n] * 2
 
     def stage_d(g, layer):
         par = layer % 2
         for half in range(2):
             table[half, pl.ds(4 * g, 4)] = xown[g][half]
-            for line in range(4):
+            for n in range(4):
                 for lo in range(2):
-                    slot = 4 * GROUPS + g * 32 + b * 8 + line * 2 + lo
-                    table[half, slot] = chosen(g, b, half, line, lo)
-        for d in range(3):
-            choose(g, par, d).wait_recv()
-            slots = pl.ds(4 * GROUPS + g * 32 + ((b + 4 - steps[d]) % 4) * 8, 8)
-            for half in range(2):
-                table[half, slots] = land2[g][par, d, half].reshape(8, 16, width)
+                    table[half, slot_of(g, b, n) + lo] = chosen(g, b, half, n, lo)
+        for n in range(4):
+            for d in range(3):
+                choose(g, par, d, n).wait_recv()
+                slots = pl.ds(slot_of(g, (b + 4 - steps[d]) % 4, n), 2)
+                for half in range(2):
+                    table[half, slots] = land2[g][par, d, n, half]
 
         @pl.when(layer == 0)
         def _():
             give_near(g).wait_recv()
             give_far(g).wait_recv()
 
-        for tiles, half in ((adj_ref, x_lo), (other, 1 - x_lo)):
-            def row_block(j, carry, tiles=tiles, half=half):
+        for cut, half in ((mine, x_lo), (other, 1 - x_lo)):
+            def row_block(j, carry, cut=cut, half=half):
                 row = g * 4 + j
                 base = (half * 4 * GROUPS + row) * fanout
                 rows = jnp.concatenate([table[half, idx_ref[base + t]] for t in range(fanout)], 0)
-                total = jnp.dot(tiles[row], rows, preferred_element_type=jnp.float32)
+                total = jnp.dot(cut[row], rows, preferred_element_type=jnp.float32)
                 part[half * 4 + j] = total.reshape(8, 16, width)
                 return carry
 
@@ -260,7 +174,7 @@
             @pl.when(section == layer // 2)
             def _():
                 for j in range(4):
-                    part[x_lo * 4 + j] += stale_ref[layer % 2, g * 4 + j]
+                    part[x_lo * 4 + j] += old[j]
 
         for j in range(8):
             send0[g][j] = part[j, pl.ds((1 - core) * 4, 4)].astype(jnp.bfloat16)
@@ -283,7 +197,8 @@
         for j in range(8):
             keep[g][j] = summed(j, x)
         for d in range(3):
-            choose(g, par, d).wait_send()
+            for n in range(4):
+                choose(g, par, d, n).wait_send()
 
     def stage_h(g, layer):
         par = layer % 2
@@ -306,7 +221,8 @@
             xown[g][...] = shaped
             for d in (2, 0, 1):
                 gather(g, 1 - par, d).start()
-            seltab[g][a] = shaped
+            seltab[g][0] = shaped
+            send_chosen(g, 1 - par, 0)
 
         @pl.when(layer == layers - 1)
         def _():
@@ -322,23 +238,69 @@
         for d in range(3):
             to_x(g, par, d).wait_send()
 
-    for half in range(2):
-        table[half, 4 * GROUPS + 96] = jnp.zeros((16, width), jnp.bfloat16)
+    loads = []
+    for g in range(GROUPS):
+        rows = pl.ds(4 * g, 4)
+        loads.append(pltpu.make_async_copy(tiles_ref.at[rows], tiles.at[rows], load.at[g]))
+    for l in range(2):
+        loads.append(
+            pltpu.make_async_copy(stale_ref.at[l], stale.at[l, pl.ds(0, 64)], load.at[GROUPS + l])
+        )
+    for item in loads:
+        item.start()
     for g in range(GROUPS):
         for half in range(2):
             xown[g][half] = initial_ref[half, pl.ds(4 * g, 4)]
         for d in (2, 0, 1):
             gather(g, 0, d).start()
         for half in range(2):
-            seltab[g][a, half] = initial_ref[half, pl.ds(4 * g, 4)]
+            seltab[g][0, half] = initial_ref[half, pl.ds(4 * g, 4)]
+        send_chosen(g, 0, 0)
     weight_keep.start()
     weight_core.start()
-    give_near(0).start()
-    give_far(0).start()
-    weight_far.start()
-    for g in range(1, GROUPS):
+    for half in range(2):
+        table[half, 4 * GROUPS + 96] = jnp.zeros((16, width), jnp.bfloat16)
+    for l in range(2):
+        stale[l, 64] = jnp.zeros((128, width), jnp.bfloat16)
+
+    def slice_rows(row, far_one):
+        left = jnp.concatenate(
+            [
+                jnp.concatenate([tiles[row, m * 8 + u] for u in range(8)], 1)
+                for m in range(fanout // 8)
+            ],
+            0,
+        )
+        both = jnp.dot(left, cut_ref[far_one], preferred_element_type=jnp.float32)
+        both = both.astype(jnp.bfloat16)
+        for m in range(fanout // 8):
+            lanes = pl.ds(m * 128, 128)
+            mine[row, :, lanes] = both[m * 128:(m + 1) * 128, :128]
+            give[row, :, lanes] = both[m * 128:(m + 1) * 128, 128:]
+
+    for g in range(GROUPS):
+        loads[g].wait()
+        for j in range(4):
+            slice_rows(4 * g + j, j // 3)
         give_near(g).start()
         give_far(g).start()
+        if g == 0:
+            weight_far.start()
+
+    def stale_rows(g, depth):
+        def one(j, carry):
+            row = 4 * g + j
+            total = jnp.zeros((128, width), jnp.float32)
+            for m in range(fanout // 8):
+                left = jnp.concatenate([tiles[row, m * 8 + u] for u in range(8)], 1)
+                rows = jnp.concatenate(
+                    [stale[depth, old_ref[row * fanout + m * 8 + u]] for u in range(8)], 0
+                )
+                total = total + jnp.dot(left, rows, preferred_element_type=jnp.float32)
+            old[j] = total.reshape(8, 16, width)
+            return carry
+
+        lax.fori_loop(0, 4, one, 0)
 
     def body(layer, carry):
         for g in range(GROUPS):
@@ -365,6 +327,13 @@
                     weight_pass.start()
                     weight_keep.wait()
                     weight_core.wait_recv()
+                    for l in range(2):
+                        loads[GROUPS + l].wait()
+
+            if g < GROUPS - 1:
+                @pl.when((layer < layers) & (section == layer // 2))
+                def _(g=g):
+                    stale_rows(g, layer % 2)
         return carry
 
     run = {"a": stage_a, "d": stage_d, "e": stage_e, "h": stage_h}
@@ -372,8 +341,8 @@
 
     for g in range(GROUPS):
         rows = pl.ds(4 * g, 4)
-        mine = fin[g][section, x_lo]
-        out_ref[rows, core * 4 + x] = mine
+        kept = fin[g][section, x_lo]
+        out_ref[rows, core * 4 + x] = kept
         for n, (s, c) in enumerate(hops):
             to_out(g, n).wait_recv()
             piece = ((core + c) % 2) * 4 + (x + 4 - s) % 4
@@ -390,9 +359,10 @@
 ORDER = (("a", 0), ("d", 1), ("h", 2), ("e", 1))
 
 
-def run_layers(idx, picks, betas, adj, give, weights, initial, stale, spread):
+def run_layers(idx, picks, old, betas, tiles, stale, weights, initial, cuts, spread):
     depth, width = weights.shape[:2]
     blocks, piece = initial.shape[1:3]
+    fanout, block = tiles.shape[1:3]
     dt = jnp.bfloat16
     slab = (piece, width)
 
@@ -404,29 +374,33 @@
         pltpu.VMEM((2, 4 * GROUPS + 97, *slab), dt),
         pltpu.VMEM((8, 8, *slab), jnp.float32),
         pltpu.VMEM((4, *weights.shape), dt),
-        pltpu.VMEM(adj.shape, dt),
+        *[pltpu.VMEM((blocks, block, fanout * piece), dt) for _ in range(3)],
+        pltpu.VMEM(tiles.shape, dt),
+        pltpu.VMEM((depth, stale.shape[1] + 1, block, width), dt),
+        pltpu.VMEM((4, 8, *slab), jnp.float32),
         *each((2, 4)), *each((4, 2, 4)), *each((2, 3, 2, 4)),
-        *each((3, 2, 4, 2)), *each((2, 3, 2, 4, 2)),
+        *each((3, 4, 2, 2)), *each((2, 3, 4, 2, 2)),
         *each((8, 4)), *each((2, 8, 4)),
         *each((3, 8)), *each((2, 3, 8)), *each((8,), jnp.float32),
         *each((4, 2, 4), dt, (piece, 128)), *each((7, 4), dt, (piece, 128)),
-        sems((9,)), sems((18,)), sems((9,)), sems((18,)), sems((3,)), sems((6,)),
+        sems((9,)), sems((18,)), sems((36,)), sems((72,)), sems((3,)), sems((6,)),
         sems((9,)), sems((18,)), sems((21,)), sems((21,)), sems((6,)), sems((6,)),
-        sems((3,)), sems((3,)), sems,
+        sems((3,)), sems((3,)), sems, sems((5,)),
     ]
     smem = pl.BlockSpec(memory_space=pltpu.SMEM)
     vmem = pl.BlockSpec(memory_space=pltpu.VMEM)
+    hbm = pl.BlockSpec(memory_space=pltpu.MemorySpace.HBM)
     return pl.pallas_call(
         main_kernel,
         out_shape=jax.ShapeDtypeStruct((blocks, 8, piece, 128), dt),
-        in_specs=[smem] * 3 + [vmem] * 6,
+        in_specs=[smem] * 4 + [hbm] * 2 + [vmem] * 4,
         out_specs=vmem,
         scratch_shapes=scratch,
         compiler_params=pltpu.CompilerParams(
             vmem_limit_bytes=VMEM_LIMIT, collective_id=0, has_side_effects=True
         ),
         name="run_layers",
-    )(idx, picks, betas, adj, give, weights, initial, stale, spread)
+    )(idx, picks, old, betas, tiles, stale, weights, initial, cuts, spread)
 
 
 def per_device(
@@ -502,11 +476,17 @@
         ),
     ).reshape(-1).astype(jnp.int32)
 
-    own_adj, give_adj = slice_tiles(adjacency_tiles, mine, near, far, piece)
-    stale = stale_sums(
-        tile_columns, adjacency_tiles, stale_imports[:, 0], groups, group_blocks, part_count
-    )
-    stale = stale.reshape(2, (groups - 1) * group_blocks, 8, piece, width)
+    old_rows = (groups - 1) * group_blocks
+    own_columns = tile_columns[:old_rows]
+    is_old = own_columns >= blocks + part_count * (row_group[0, :old_rows] + 1)
+    stale_slots = stale_imports.shape[2]
+    old = jnp.where(is_old, own_columns - blocks - part_count, stale_slots).reshape(-1)
+
+    lane = jnp.arange(2 * block, dtype=jnp.int32)
+    targets = jnp.where(lane[None] < block, mine, jnp.stack([near, far])[:, None])
+    wanted = ((lane % block) // piece) * block + targets * piece + lane % piece
+    cuts = jnp.arange(8 * block, dtype=jnp.int32)[None, :, None] == wanted[:, None, :]
+
     betas = jnp.log(lambda_decay / (jnp.arange(layers, dtype=jnp.float32) + 1.0) + 1.0)
     initial = by_half(own_init, other_init)
     cols = width // sections
@@ -515,8 +495,8 @@
     spread = (source == (lane // 128) * cols + lane % 128) & (lane % 128 < cols)
 
     done = run_layers(
-        idx, picks, betas, own_adj, give_adj, layer_weights, initial, stale,
-        spread.astype(jnp.bfloat16),
+        idx, picks, old, betas, adjacency_tiles, stale_imports[:, 0], layer_weights, initial,
+        cuts.astype(jnp.bfloat16), spread.astype(jnp.bfloat16),
     )
     return done.reshape(blocks * block, 128)[:, :cols]
 

time: 294 us -> 259 us (0.88)
  Pallas kernels: 269 us -> 237 us
    pallas_call x2 -> x0, Pallas kernels: 29 us -> none  [the longest x1 16.6 us: stale_sums(): pl.pallas_call(stale_kernel, out_shape=jax.ShapeDtypeStruct((2, rows, blo...]
  transfers between devices with their start and end apart: 5 -> 5, of which waited for: 1 -> 1; matrix products, arithmetic and copies ran while one was open for 4% -> 3% of each run, Pallas kernels for 10% -> 0%
where the time goes in v4:
time: 259 us; the launch traced here: 258 us
  Pallas kernels  237 us (92%)
  starting transfers between devices  8 us (3%)
  local copies, waits for them, and re-layouts  6.86 us (3%)
  other arithmetic  6.04 us (2%)
    pallas_call x1, Pallas kernels, run_layers(): pl.pallas_call(main_kernel, out_shape=jax.ShapeDtypeStruct((blocks, 8, pi...  237 us
    ppermute x3, starting transfers between devices, per_device(): lax.ppermute(sends, ('section', 'dom'), along(step))  5.8 us
  transfers between devices with their start and end apart: 5, of which 1 were waited for; matrix products, arithmetic and copies ran while one was open for 3% of the time, Pallas kernels for 0%

profile of v4, /device:TPU:1, one launch (start us, length us, event | category | flops | bytes accessed | tf_op | source)
XLA Modules:
  0.0 258.4 jit_solution(18230928303295444227)
XLA Ops:
  0.0 0.7 reduce
  0.7 0.1 reshape.274
  0.8 0.8 reshape.275
  1.6 0.1 pad_add_fusion.2
  1.6 2.0 collective-permute-start
  3.7 1.0 dynamic-slice_bitcast_fusion.1
  4.7 0.1 collective-permute-start.4
  4.9 0.6 add_log_fusion.beta_ref
  5.6 0.8 add_select_fusion.6
  6.3 0.1 pad_add_fusion.3
  6.4 0.1 add_add_fusion
  6.5 1.3 fusion.cut_ref
  7.8 0.9 fusion.2.spread_ref
  8.7 0.7 reshape.279.old_ref
  9.4 0.1 le.11
  9.5 0.1 le.12
  9.6 0.0 collective-permute-done
  9.6 0.1 rev.6
  9.8 0.1 slice.22
  9.8 3.1 %collective-permute-start.2 = (s32[2,96]{1,0:T(2,128)S(1)}, s32[2,96]{1,0:T(2,128)S(1)}, u32[]{:S(2)}, u32[]{:S(2)}) collective-permute-start(s32[2,96]{1,0:T(2,128)S(1)} %get-tuple-element.8), channel_id=1, source_target_pairs={{0,16},{1,17},{2,18},{3,19},{4,20},{5,21},{6,22},{7,23},{8,24},{9,... | collective-permute-start | bytes 2312 | tf_op jit(solution)/shard_map/ppermute | solution.py:454
  13.0 0.4 collective-permute-start.1
  13.3 2.3 collective-permute-start.3
  15.6 0.1 reshape.276
  15.7 0.6 compare_select_fusion.idx_ref
  16.3 0.0 collective-permute-done.2
  16.3 0.3 collective-permute-done.1
  16.6 0.0 collective-permute-done.3
  16.6 0.6 gather_fusion
  17.2 0.1 copy.13
  17.3 0.2 copy.14
  17.5 0.2 copy.15
  17.7 0.3 copy.16
  17.9 0.7 reshape.278.pick_ref
  18.7 0.0 collective-permute-done.4
  18.7 0.8 reverse_select_fusion.initial_ref
  19.5 237.1 %run_layers.1 = bf16[12,8,16,128]{3,2,1,0:T(8,128)(2,1)} custom-call(s32[576]{0:T(1024)} %compare_select_fusion.idx_ref, s32[192]{0:T(256)} %reshape.278.pick_ref, s32[192]{0:T(256)} %reshape.279.old_ref, f32[8]{0:T(128)} %add_log_fusion.beta_ref, bf16[12,24,128,128]{3,2,1,0:T(8,128)(2,1)} %tiles_ref.1, bf16[2,64,128,384]{3,2,1,0:T(8,128)(2,1)} %bitcast.33, ...), custom_call_target="tpu_custom_call" | custom-call | tf_op jit(solution)/shard_map/run_layers/pallas_call | solution.py:393
  256.5 1.9 copy.22
  (19 shorter events, 0.2 us)
Async XLA Ops:
  1.6 7.9 %collective-permute-start = (s32[384]{0:T(512)S(1)}, s32[384]{0:T(512)S(1)}, u32[]{:S(2)}, u32[]{:S(2)}) collective-permute-start(s32[384]{0:T(512)S(1)} %pad_add_fusion.2), channel_id=1, source_target_pairs={{0,1},{1,0},{2,3},{3,2},{4,5},{5,4},{6,7},{7,6},{8,9},{9,8},{10,11... | collective-permute-start | bytes 4616 | tf_op jit(solution)/shard_map/ppermute | solution.py:436
  4.7 14.0 %collective-permute-start.4 = (bf16[12,16,384]{2,1,0:T(8,128)(2,1)S(1)}, bf16[12,16,384]{2,1,0:T(8,128)(2,1)S(1)}, u32[]{:S(2)}, u32[]{:S(2)}) collective-permute-start(bf16[12,16,384]{2,1,0:T(8,128)(2,1)S(1)} %get-tuple-element.6), channel_id=1, source_target_pairs={{0,1},{1,0},{2,3},{3,2},{4,5},{5,4},{6,7},{7,6},{8,9},{9,8},{10,11... | collective-permute-start | bytes 442376 | tf_op jit(solution)/shard_map/ppermute | solution.py:433
  9.8 6.5 %collective-permute-start.2 = (s32[2,96]{1,0:T(2,128)S(1)}, s32[2,96]{1,0:T(2,128)S(1)}, u32[]{:S(2)}, u32[]{:S(2)}) collective-permute-start(s32[2,96]{1,0:T(2,128)S(1)} %get-tuple-element.8), channel_id=1, source_target_pairs={{0,16},{1,17},{2,18},{3,19},{4,20},{5,21},{6,22},{7,23},{8,24},{9,... | collective-permute-start | bytes 2312 | tf_op jit(solution)/shard_map/ppermute | solution.py:454
  13.0 3.6 %collective-permute-start.1 = (s32[2,96]{1,0:T(2,128)S(1)}, s32[2,96]{1,0:T(2,128)S(1)}, u32[]{:S(2)}, u32[]{:S(2)}) collective-permute-start(s32[2,96]{1,0:T(2,128)S(1)} %get-tuple-element.8), channel_id=1, source_target_pairs={{0,8},{1,9},{2,10},{3,11},{4,12},{5,13},{6,14},{7,15},{8,16},{9,17... | collective-permute-start | bytes 2312 | tf_op jit(solution)/shard_map/ppermute | solution.py:454
  13.3 3.2 %collective-permute-start.3 = (s32[2,96]{1,0:T(2,128)S(1)}, s32[2,96]{1,0:T(2,128)S(1)}, u32[]{:S(2)}, u32[]{:S(2)}) collective-permute-start(s32[2,96]{1,0:T(2,128)S(1)} %get-tuple-element.8), channel_id=1, source_target_pairs={{0,24},{1,25},{2,26},{3,27},{4,28},{5,29},{6,30},{7,31},{8,0},{9,1... | collective-permute-start | bytes 2312 | tf_op jit(solution)/shard_map/ppermute | solution.py:454

commit v5 on v4

--- a/solution.py
+++ b/solution.py
@@ -24,8 +24,9 @@
 
 
 def main_kernel(
-    idx_ref, pick_ref, old_ref, beta_ref, tiles_ref, stale_ref, weight_ref, initial_ref,
-    cut_ref, spread_ref, out_ref, table, part, weights, mine, give, other, tiles, stale, old, *rest,
+    number_ref, start_ref, tiles_ref, stale_ref, weight_ref, out_ref,
+    table, part, weights, mine, give, other, tiles, stale, old,
+    landed, numbers, initial, cuts, spread, *rest,
 ):
     rest = list(rest)
 
@@ -37,19 +38,19 @@
     xown, seltab, agbuf, out2, land2 = (take(GROUPS) for _ in range(5))
     send0, recv0, sendx, recvx, keep, fin, finland = (take(GROUPS) for _ in range(7))
     (ag_s, ag_r, sel_s, sel_r, core_s, core_r, x_s, x_r, fin_s, fin_r,
-     tile_s, tile_r, w_s, w_r, w_local, load) = rest
-
-    layers = beta_ref.shape[0]
-    fanout = idx_ref.shape[0] // (2 * 4 * GROUPS)
+     tile_s, tile_r, w_s, w_r, w_local, load, num_s, num_r, num_local, start_s, start_r) = rest
+
+    layers = 4 * weight_ref.shape[0]
+    fanout = tiles_ref.shape[1]
     width = weight_ref.shape[1]
     section, dom, x_hi, core, z, y, x_lo = place()
     x = x_hi * 2 + x_lo
     a = (1 - core) * z + core * y
     b = (1 - core) * y + core * z
 
-    def on_a(step):
+    def on_a(step, other_lo=0):
         zz, yy = (z + (1 - core) * step) % 4, (y + core * step) % 4
-        return (section, zz * 8 + yy * 2 + x_lo)
+        return (section, zz * 8 + yy * 2 + (x_lo + other_lo) % 2)
 
     def on_b(step):
         zz, yy = (z + core * step) % 4, (y + (1 - core) * step) % 4
@@ -65,9 +66,26 @@
     near = (section, z * 8 + y * 2 + 1 - x_lo)
     far = ((1 - x_hi) * 2 + core, z * 8 + y * 2 + 1 - x_lo)
 
+    piece, near_piece = core * 4 + x, core * 4 + x_hi * 2 + 1 - x_lo
+    loads = []
+    for g in range(GROUPS):
+        rows = pl.ds(4 * g, 4)
+        loads.append(pltpu.make_async_copy(tiles_ref.at[rows], tiles.at[rows], load.at[g]))
+    for l in range(2):
+        loads.append(
+            pltpu.make_async_copy(stale_ref.at[l], stale.at[l, pl.ds(0, 64)], load.at[GROUPS + l])
+        )
+    start_own = pltpu.make_async_copy(start_ref.at[:, piece], initial.at[x_lo], load.at[5])
+    number_own = pltpu.make_async_copy(number_ref, numbers.at[0], num_local.at[0])
+    start_own.start()
+    number_own.start()
+    for item in loads:
+        item.start()
+
     barrier = pltpu.get_barrier_semaphore()
     friends = [on_a(s) for s in steps] + [on_b(s) for s in steps] + [partner]
     friends += [on_x(s, c) for s in steps for c in range(2)]
+    friends += [on_a(s, 1) for s in steps]
     for friend in friends:
         pl.semaphore_signal(barrier, inc=1, device_id=friend, device_id_type=MESH)
     pl.semaphore_wait(barrier, len(friends))
@@ -118,10 +136,22 @@
                          partner)
 
     lines = [a] + [(a + 4 - step) % 4 for step in steps]
+    line_stride, place_stride = 8 - 6 * core, 2 + 6 * core
+
+    def number_to(k):
+        n, flip = k // 2, k % 2
+        return remote(number_ref, landed.at[k], num_s.at[k], num_r.at[k],
+                      on_a(steps[n - 1] if n else 0, flip))
+
+    def start_to(g):
+        rows = pl.ds(4 * g, 4)
+        return remote(start_ref.at[rows, near_piece], initial.at[x_lo, rows], start_s.at[g],
+                      start_r.at[g], near)
 
     def chosen(g, dest, half, n, lo):
-        which = (((g * 4 + dest) * 2 + half) * 4 + lines[n]) * 2 + lo
-        return seltab[g][n, lo, pick_ref[which]]
+        target = a * line_stride + dest * place_stride + half
+        pick = numbers[n * 2 + (lo + x_lo) % 2, 0, g * 32 + target]
+        return seltab[g][n, lo, jnp.maximum(pick, 0)]
 
     def send_chosen(g, par, n):
         for d in (2, 0, 1):
@@ -138,7 +168,7 @@
             send_chosen(g, par, d + 1)
 
     def slot_of(g, place_b, n):
-        return 4 * GROUPS + g * 32 + place_b * 8 + lines[n] * 2
+        return 4 * GROUPS + g * 32 + place_b * place_stride + lines[n] * line_stride
 
     def stage_d(g, layer):
         par = layer % 2
@@ -159,11 +189,16 @@
             give_near(g).wait_recv()
             give_far(g).wait_recv()
 
-        for cut, half in ((mine, x_lo), (other, 1 - x_lo)):
-            def row_block(j, carry, cut=cut, half=half):
+        for rel, (cut, half) in enumerate(((mine, x_lo), (other, 1 - x_lo))):
+            def row_block(j, carry, rel=rel, cut=cut, half=half):
                 row = g * 4 + j
-                base = (half * 4 * GROUPS + row) * fanout
-                rows = jnp.concatenate([table[half, idx_ref[base + t]] for t in range(fanout)], 0)
+
+                def entry(t):
+                    column = numbers[rel, 1 + row, t]
+                    fresh = column < 4 * GROUPS + 32 * (g + 1)
+                    return table[half, jnp.where(fresh, column, 4 * GROUPS + 96)]
+
+                rows = jnp.concatenate([entry(t) for t in range(fanout)], 0)
                 total = jnp.dot(cut[row], rows, preferred_element_type=jnp.float32)
                 part[half * 4 + j] = total.reshape(8, 16, width)
                 return carry
@@ -206,10 +241,12 @@
         for d in range(3):
             to_x(g, par, d).wait_recv()
             total = total + recvx[g][par, d].astype(jnp.float32)
-        start = jnp.concatenate([initial_ref[half, pl.ds(4 * g, 4)] for half in range(2)], 0)
+        start = jnp.concatenate([initial[half, pl.ds(4 * g, 4)] for half in range(2)], 0)
         mixed = (1.0 - alpha_mix) * total + alpha_mix * start.astype(jnp.float32)
         mixed = mixed.astype(jnp.bfloat16).reshape(8 * 16, width)
-        beta = beta_ref[layer]
+        beta = jnp.float32(BETAS[0])
+        for l in range(1, layers):
+            beta = jnp.where(layer == l, jnp.float32(BETAS[l]), beta)
         weight = weights[layer // 2, layer % 2]
         product = jnp.dot(mixed, weight, preferred_element_type=jnp.float32)
         value = (1.0 - beta) * mixed.astype(jnp.float32) + beta * product
@@ -226,7 +263,7 @@
 
         @pl.when(layer == layers - 1)
         def _():
-            wide = jnp.dot(value, spread_ref[...], preferred_element_type=jnp.float32)
+            wide = jnp.dot(value, spread[...], preferred_element_type=jnp.float32)
             wide = wide.astype(jnp.bfloat16)
             for target in range(4):
                 lanes = wide[:, target * 128:(target + 1) * 128]
@@ -238,30 +275,53 @@
         for d in range(3):
             to_x(g, par, d).wait_send()
 
-    loads = []
     for g in range(GROUPS):
-        rows = pl.ds(4 * g, 4)
-        loads.append(pltpu.make_async_copy(tiles_ref.at[rows], tiles.at[rows], load.at[g]))
-    for l in range(2):
-        loads.append(
-            pltpu.make_async_copy(stale_ref.at[l], stale.at[l, pl.ds(0, 64)], load.at[GROUPS + l])
-        )
-    for item in loads:
-        item.start()
-    for g in range(GROUPS):
-        for half in range(2):
-            xown[g][half] = initial_ref[half, pl.ds(4 * g, 4)]
-        for d in (2, 0, 1):
-            gather(g, 0, d).start()
-        for half in range(2):
-            seltab[g][0, half] = initial_ref[half, pl.ds(4 * g, 4)]
-        send_chosen(g, 0, 0)
+        start_to(g).start()
+    for k in range(1, 8):
+        number_to(k).start()
     weight_keep.start()
     weight_core.start()
+
     for half in range(2):
         table[half, 4 * GROUPS + 96] = jnp.zeros((16, width), jnp.bfloat16)
     for l in range(2):
         stale[l, 64] = jnp.zeros((128, width), jnp.bfloat16)
+
+    row = lax.broadcasted_iota(jnp.int32, (128, 256), 0)
+    lane = lax.broadcasted_iota(jnp.int32, (128, 256), 1)
+    inner = lane & 127
+    for far_one in range(2):
+        given = near_piece if far_one == 0 else core * 4 + (1 - x_hi) * 2 + 1 - x_lo
+        wanted = jnp.where(lane < 128, piece, given) * 16 + (inner & 15)
+        for u in range(8):
+            hit = (inner >= u * 16) & (inner < u * 16 + 16) & (row == wanted)
+            cuts[far_one, pl.ds(u * 128, 128), :] = jnp.where(hit, 1.0, 0.0).astype(jnp.bfloat16)
+    cols = width // 4
+    row = lax.broadcasted_iota(jnp.int32, (width, 128), 0)
+    lane = lax.broadcasted_iota(jnp.int32, (width, 128), 1)
+    for target in range(4):
+        hit = (row == target * cols + lane) & (lane < cols)
+        spread[:, pl.ds(target * 128, 128)] = jnp.where(hit, 1.0, 0.0).astype(jnp.bfloat16)
+
+    start_own.wait()
+    for g in range(GROUPS):
+        start_to(g).wait_recv()
+        for half in range(2):
+            xown[g][half] = initial[half, pl.ds(4 * g, 4)]
+        for d in (2, 0, 1):
+            gather(g, 0, d).start()
+        for half in range(2):
+            seltab[g][0, half] = initial[half, pl.ds(4 * g, 4)]
+    for k in range(1, 8):
+        number_to(k).wait_recv()
+    number_rest = pltpu.make_async_copy(
+        landed.at[pl.ds(1, 7)], numbers.at[pl.ds(1, 7)], num_local.at[1]
+    )
+    number_rest.start()
+    number_own.wait()
+    number_rest.wait()
+    for g in range(GROUPS):
+        send_chosen(g, 0, 0)
 
     def slice_rows(row, far_one):
         left = jnp.concatenate(
@@ -271,7 +331,7 @@
             ],
             0,
         )
-        both = jnp.dot(left, cut_ref[far_one], preferred_element_type=jnp.float32)
+        both = jnp.dot(left, cuts[far_one], preferred_element_type=jnp.float32)
         both = both.astype(jnp.bfloat16)
         for m in range(fanout // 8):
             lanes = pl.ds(m * 128, 128)
@@ -286,6 +346,7 @@
         give_far(g).start()
         if g == 0:
             weight_far.start()
+        stage_a(g, 0)
 
     def stale_rows(g, depth):
         def one(j, carry):
@@ -293,9 +354,13 @@
             total = jnp.zeros((128, width), jnp.float32)
             for m in range(fanout // 8):
                 left = jnp.concatenate([tiles[row, m * 8 + u] for u in range(8)], 1)
-                rows = jnp.concatenate(
-                    [stale[depth, old_ref[row * fanout + m * 8 + u]] for u in range(8)], 0
-                )
+
+                def entry(t):
+                    column = numbers[0, 1 + row, t]
+                    past = column - (4 * GROUPS + 32)
+                    return stale[depth, jnp.where(past >= 32 * g, past, 64)]
+
+                rows = jnp.concatenate([entry(m * 8 + u) for u in range(8)], 0)
                 total = total + jnp.dot(left, rows, preferred_element_type=jnp.float32)
             old[j] = total.reshape(8, 16, width)
             return carry
@@ -312,7 +377,7 @@
             for stage, back in ORDER:
                 turn = g - back
                 if turn >= 0:
-                    @pl.when(layer < layers)
+                    @pl.when((layer < layers) & (layer > 0) if stage == "a" else layer < layers)
                     def _(stage=stage, turn=turn):
                         run[stage](turn, layer)
                 else:
@@ -351,17 +416,21 @@
             to_out(g, n).wait_send()
         give_near(g).wait_send()
         give_far(g).wait_send()
+        start_to(g).wait_send()
+    for k in range(1, 8):
+        number_to(k).wait_send()
     weight_core.wait_send()
     weight_far.wait_send()
     weight_pass.wait_send()
 
 
+BETAS = [float(np.log(np.float32(lambda_decay / (l + 1.0)) + np.float32(1.0))) for l in range(8)]
 ORDER = (("a", 0), ("d", 1), ("h", 2), ("e", 1))
 
 
-def run_layers(idx, picks, old, betas, tiles, stale, weights, initial, cuts, spread):
+def run_layers(numbers, start, tiles, stale, weights):
     depth, width = weights.shape[:2]
-    blocks, piece = initial.shape[1:3]
+    blocks, pieces, piece = start.shape[:3]
     fanout, block = tiles.shape[1:3]
     dt = jnp.bfloat16
     slab = (piece, width)
@@ -378,6 +447,11 @@
         pltpu.VMEM(tiles.shape, dt),
         pltpu.VMEM((depth, stale.shape[1] + 1, block, width), dt),
         pltpu.VMEM((4, 8, *slab), jnp.float32),
+        pltpu.VMEM((8, *numbers.shape), jnp.int32),
+        pltpu.SMEM((8, *numbers.shape), jnp.int32),
+        pltpu.VMEM((2, blocks, *slab), dt),
+        pltpu.VMEM((2, 8 * block, 2 * block), dt),
+        pltpu.VMEM((width, 4 * block), dt),
         *each((2, 4)), *each((4, 2, 4)), *each((2, 3, 2, 4)),
         *each((3, 4, 2, 2)), *each((2, 3, 4, 2, 2)),
         *each((8, 4)), *each((2, 8, 4)),
@@ -385,119 +459,37 @@
         *each((4, 2, 4), dt, (piece, 128)), *each((7, 4), dt, (piece, 128)),
         sems((9,)), sems((18,)), sems((36,)), sems((72,)), sems((3,)), sems((6,)),
         sems((9,)), sems((18,)), sems((21,)), sems((21,)), sems((6,)), sems((6,)),
-        sems((3,)), sems((3,)), sems, sems((5,)),
+        sems((3,)), sems((3,)), sems, sems((6,)),
+        sems((8,)), sems((8,)), sems((2,)), sems((3,)), sems((3,)),
     ]
-    smem = pl.BlockSpec(memory_space=pltpu.SMEM)
     vmem = pl.BlockSpec(memory_space=pltpu.VMEM)
     hbm = pl.BlockSpec(memory_space=pltpu.MemorySpace.HBM)
     return pl.pallas_call(
         main_kernel,
-        out_shape=jax.ShapeDtypeStruct((blocks, 8, piece, 128), dt),
-        in_specs=[smem] * 4 + [hbm] * 2 + [vmem] * 4,
+        out_shape=jax.ShapeDtypeStruct((blocks, pieces, piece, 128), dt),
+        in_specs=[hbm] * 4 + [vmem],
         out_specs=vmem,
         scratch_shapes=scratch,
         compiler_params=pltpu.CompilerParams(
             vmem_limit_bytes=VMEM_LIMIT, collective_id=0, has_side_effects=True
         ),
         name="run_layers",
-    )(idx, picks, old, betas, tiles, stale, weights, initial, cuts, spread)
+    )(numbers, start, tiles, stale, weights)
 
 
 def per_device(
     initial_features, layer_weights, adjacency_tiles, tile_columns, send_blocks, stale_imports
 ):
-    section, dom, x_hi, core, z, y, x_lo = place()
-    sections = lax.axis_size("section")
-    part_count = lax.axis_size("dom")
     blocks, fanout, block = adjacency_tiles.shape[:3]
     width = initial_features.shape[1]
-    groups = send_blocks.shape[1]
-    group_blocks = blocks // groups
-    layers = layer_weights.shape[0] * sections
+    groups, part_count = send_blocks.shape[1:]
     piece = block // 8
-
-    def number(hi, lo):
-        return core * 4 + hi * 2 + lo
-
-    mine = number(x_hi, x_lo)
-    near, far = number(x_hi, 1 - x_lo), number(1 - x_hi, 1 - x_lo)
-    swap = [(p, p + 1 - 2 * (p % 2)) for p in range(part_count)]
-
-    def by_half(own, other):
-        pair = jnp.stack([own, other])
-        return jnp.where(x_lo == 0, pair, pair[::-1])
-
-    init_blocks = initial_features.reshape(blocks, 8, piece, width)
-    own_init = lax.dynamic_index_in_dim(init_blocks, mine, 1, keepdims=False)
-    other_init = lax.dynamic_index_in_dim(init_blocks, near, 1, keepdims=False)
-    other_init = lax.ppermute(other_init, "dom", swap)
-
-    numbers = jnp.concatenate([send_blocks.reshape(-1), tile_columns.reshape(-1)])
-    numbers = by_half(numbers, lax.ppermute(numbers, "dom", swap))
-    sends = jnp.maximum(numbers[:, : groups * part_count], 0)
-    columns = numbers[:, groups * part_count :].reshape(2, blocks, fanout)
-
-    def along(step):
-        moves = []
-        for s in range(sections):
-            for p in range(part_count):
-                pz, py, lo = p // 8, (p // 2) % 4, p % 2
-                q = (
-                    ((pz + step) % 4) * 8 + py * 2 + lo
-                    if s % 2 == 0
-                    else pz * 8 + ((py + step) % 4) * 2 + lo
-                )
-                moves.append((s * part_count + p, s * part_count + q))
-        return moves
-
-    lines = jnp.stack(
-        [sends] + [lax.ppermute(sends, ("section", "dom"), along(step)) for step in (1, 2, 3)]
-    )
-    a = jnp.where(core == 0, z, y)
-    lines = lines[(a - jnp.arange(4, dtype=jnp.int32)) % 4]
-    lines = lines.reshape(4, 2, groups, 4, 4, 2)
-    to_y = lax.dynamic_index_in_dim(lines, z, 3, keepdims=False)
-    to_z = lax.dynamic_index_in_dim(lines, y, 4, keepdims=False)
-    picks = jnp.where(core == 0, to_y, to_z)
-    picks = picks.transpose(2, 3, 4, 0, 1).reshape(-1).astype(jnp.int32)
-
-    row_group = (jnp.arange(blocks, dtype=jnp.int32) // group_blocks)[None, :, None]
-    slot = jnp.maximum(columns - blocks, 0)
-    slot_group, source = slot // part_count, slot % part_count
-    zs, ys, los = source // 8, (source // 2) % 4, source % 2
-    where = jnp.where(core == 0, ys * 8 + zs * 2, zs * 8 + ys * 2) + los
-    idx = jnp.where(
-        columns < blocks,
-        columns,
-        jnp.where(
-            slot_group <= row_group,
-            blocks + slot_group * part_count + where,
-            blocks + groups * part_count,
-        ),
-    ).reshape(-1).astype(jnp.int32)
-
-    old_rows = (groups - 1) * group_blocks
-    own_columns = tile_columns[:old_rows]
-    is_old = own_columns >= blocks + part_count * (row_group[0, :old_rows] + 1)
-    stale_slots = stale_imports.shape[2]
-    old = jnp.where(is_old, own_columns - blocks - part_count, stale_slots).reshape(-1)
-
-    lane = jnp.arange(2 * block, dtype=jnp.int32)
-    targets = jnp.where(lane[None] < block, mine, jnp.stack([near, far])[:, None])
-    wanted = ((lane % block) // piece) * block + targets * piece + lane % piece
-    cuts = jnp.arange(8 * block, dtype=jnp.int32)[None, :, None] == wanted[:, None, :]
-
-    betas = jnp.log(lambda_decay / (jnp.arange(layers, dtype=jnp.float32) + 1.0) + 1.0)
-    initial = by_half(own_init, other_init)
-    cols = width // sections
-    source = jnp.arange(width, dtype=jnp.int32)[:, None]
-    lane = jnp.arange(sections * 128, dtype=jnp.int32)[None, :]
-    spread = (source == (lane // 128) * cols + lane % 128) & (lane % 128 < cols)
-
-    done = run_layers(
-        idx, picks, old, betas, adjacency_tiles, stale_imports[:, 0], layer_weights, initial,
-        cuts.astype(jnp.bfloat16), spread.astype(jnp.bfloat16),
-    )
+    cols = width // 4
+    sends = jnp.pad(send_blocks.reshape(1, -1), ((0, 0), (0, 128 - groups * part_count)))
+    columns = jnp.pad(tile_columns, ((0, 15 - blocks), (0, 128 - fanout)))
+    numbers = jnp.concatenate([sends, columns], 0)
+    start = initial_features.reshape(blocks, 8, piece, width)
+    done = run_layers(numbers, start, adjacency_tiles, stale_imports[:, 0], layer_weights)
     return done.reshape(blocks * block, 128)[:, :cols]
 
 

time: 259 us -> 247 us (0.954)
  starting transfers between devices: 8 us -> 0 us
  Pallas kernels: 237 us -> 243 us
  local copies, waits for them, and re-layouts: 6.86 us -> 1.96 us
  other arithmetic: 6.04 us -> 2 us
    ppermute x5 -> x0, starting transfers between devices: 8 us -> none  [the longest x3 5.8 us: per_device(): lax.ppermute(sends, ('section', 'dom'), along(step))]
    pallas_call x1, Pallas kernels: 237 us -> 243 us  [run_layers(): pl.pallas_call(main_kernel, out_shape=jax.ShapeDtypeStruct((blocks, piece...]
  transfers between devices with their start and end apart: 5 -> 0, of which waited for: 1 -> 0; matrix products, arithmetic and copies ran while one was open for 3% -> 0% of each run, Pallas kernels for 0% -> 0%
where the time goes in v5:
time: 247 us
  Pallas kernels  243 us (98%)
    pallas_call x1, Pallas kernels, run_layers(): pl.pallas_call(main_kernel, out_shape=jax.ShapeDtypeStruct((blocks, piece...  243 us

profile of v5, /device:TPU:1, one launch (start us, length us, event | category | flops | bytes accessed | tf_op | source)
XLA Modules:
  0.0 247.2 jit_solution(16631806798041544909)
XLA Ops:
  0.0 0.7 reduce
  0.7 0.1 reshape.9
  0.8 1.3 pad_add_fusion.number_ref
  2.1 243.2 %run_layers.1 = bf16[12,8,16,128]{3,2,1,0:T(8,128)(2,1)} custom-call(s32[16,128]{1,0:T(8,128)} %pad_add_fusion.number_ref, bf16[12,8,16,384]{3,2,1,0:T(8,128)(2,1)} %bitcast.6, bf16[12,24,128,128]{3,2,1,0:T(8,128)(2,1)} %tiles_ref.1, bf16[2,64,128,384]{3,2,1,0:T(8,128)(2,1)} %bitcast.4, bf16[2,384,384]{2,1,0:T(8,128)(2,1)} %weight_ref.1), custom_call_target="tpu_custom_call" | custom-call | tf_op jit(solution)/shard_map/run_layers/pallas_call | solution.py:467
  245.3 1.9 copy.8

commit v6 on v5

--- a/solution.py
+++ b/solution.py
@@ -131,9 +131,15 @@
     far_section = (1 - x_hi) * 2 + core
     weight_keep = pltpu.make_async_copy(weight_ref, weights.at[section], w_local)
     weight_core = remote(weight_ref, weights.at[section], w_s.at[0], w_r.at[0], partner)
-    weight_far = remote(weight_ref, weights.at[section], w_s.at[1], w_r.at[1], far)
-    weight_pass = remote(weights.at[far_section], weights.at[far_section], w_s.at[2], w_r.at[2],
-                         partner)
+    weight_far = [
+        remote(weight_ref.at[d], weights.at[section, d], w_s.at[1 + d], w_r.at[1 + d], far)
+        for d in range(2)
+    ]
+    weight_pass = [
+        remote(weights.at[far_section, d], weights.at[far_section, d], w_s.at[3 + d],
+               w_r.at[3 + d], partner)
+        for d in range(2)
+    ]
 
     lines = [a] + [(a + 4 - step) % 4 for step in steps]
     line_stride, place_stride = 8 - 6 * core, 2 + 6 * core
@@ -345,7 +351,7 @@
         give_near(g).start()
         give_far(g).start()
         if g == 0:
-            weight_far.start()
+            weight_far[0].start()
         stage_a(g, 0)
 
     def stale_rows(g, depth):
@@ -370,9 +376,10 @@
     def body(layer, carry):
         for g in range(GROUPS):
             if g == 2:
-                @pl.when(layer == 0)
-                def _():
-                    weight_pass.wait_recv()
+                for d in range(2):
+                    @pl.when(layer == d)
+                    def _(d=d):
+                        weight_pass[d].wait_recv()
 
             for stage, back in ORDER:
                 turn = g - back
@@ -388,12 +395,23 @@
             if g == 0:
                 @pl.when(layer == 0)
                 def _():
-                    weight_far.wait_recv()
-                    weight_pass.start()
+                    weight_far[0].wait_recv()
+                    weight_pass[0].start()
                     weight_keep.wait()
                     weight_core.wait_recv()
                     for l in range(2):
                         loads[GROUPS + l].wait()
+
+            if g == 0:
+                @pl.when(layer == 1)
+                def _():
+                    weight_far[1].wait_recv()
+                    weight_pass[1].start()
+
+            if g == GROUPS - 1:
+                @pl.when(layer == 0)
+                def _():
+                    weight_far[1].start()
 
             if g < GROUPS - 1:
                 @pl.when((layer < layers) & (section == layer // 2))
@@ -420,8 +438,9 @@
     for k in range(1, 8):
         number_to(k).wait_send()
     weight_core.wait_send()
-    weight_far.wait_send()
-    weight_pass.wait_send()
+    for d in range(2):
+        weight_far[d].wait_send()
+        weight_pass[d].wait_send()
 
 
 BETAS = [float(np.log(np.float32(lambda_decay / (l + 1.0)) + np.float32(1.0))) for l in range(8)]
@@ -459,7 +478,7 @@
         *each((4, 2, 4), dt, (piece, 128)), *each((7, 4), dt, (piece, 128)),
         sems((9,)), sems((18,)), sems((36,)), sems((72,)), sems((3,)), sems((6,)),
         sems((9,)), sems((18,)), sems((21,)), sems((21,)), sems((6,)), sems((6,)),
-        sems((3,)), sems((3,)), sems, sems((6,)),
+        sems((5,)), sems((5,)), sems, sems((6,)),
         sems((8,)), sems((8,)), sems((2,)), sems((3,)), sems((3,)),
     ]
     vmem = pl.BlockSpec(memory_space=pltpu.VMEM)

time: 247 us -> 246 us (level)
  no operation moved by 1% of the time
where the time goes in v6:
time: 246 us; the launch traced here: 245 us
  Pallas kernels  241 us (98%)
    pallas_call x1, Pallas kernels, run_layers(): pl.pallas_call(main_kernel, out_shape=jax.ShapeDtypeStruct((blocks, piece...  241 us

profile of v6, /device:TPU:1, one launch (start us, length us, event | category | flops | bytes accessed | tf_op | source)
XLA Modules:
  0.0 245.5 jit_solution(5158219601868784640)
XLA Ops:
  0.0 0.7 reduce
  0.7 0.1 reshape.9
  0.8 1.3 pad_add_fusion.number_ref
  2.1 241.5 %run_layers.1 = bf16[12,8,16,128]{3,2,1,0:T(8,128)(2,1)} custom-call(s32[16,128]{1,0:T(8,128)} %pad_add_fusion.number_ref, bf16[12,8,16,384]{3,2,1,0:T(8,128)(2,1)} %bitcast.6, bf16[12,24,128,128]{3,2,1,0:T(8,128)(2,1)} %tiles_ref.1, bf16[2,64,128,384]{3,2,1,0:T(8,128)(2,1)} %bitcast.4, bf16[2,384,384]{2,1,0:T(8,128)(2,1)} %weight_ref.1), custom_call_target="tpu_custom_call" | custom-call | tf_op jit(solution)/shard_map/run_layers/pallas_call | solution.py:486
  243.6 1.9 copy.8

commit v7 on v6

--- a/solution.py
+++ b/solution.py
@@ -168,6 +168,7 @@
 
     def stage_a(g, layer):
         par = layer % 2
+        send_chosen(g, par, 0)
         for d in range(3):
             gather(g, par, d).wait_recv()
             seltab[g][d + 1] = agbuf[g][par, d]
@@ -265,7 +266,6 @@
             for d in (2, 0, 1):
                 gather(g, 1 - par, d).start()
             seltab[g][0] = shaped
-            send_chosen(g, 1 - par, 0)
 
         @pl.when(layer == layers - 1)
         def _():
@@ -326,9 +326,6 @@
     number_rest.start()
     number_own.wait()
     number_rest.wait()
-    for g in range(GROUPS):
-        send_chosen(g, 0, 0)
-
     def slice_rows(row, far_one):
         left = jnp.concatenate(
             [

time: 246 us -> 245 us (level)
  no operation moved by 1% of the time
where the time goes in v7:
time: 245 us
  Pallas kernels  241 us (98%)
    pallas_call x1, Pallas kernels, run_layers(): pl.pallas_call(main_kernel, out_shape=jax.ShapeDtypeStruct((blocks, piece...  241 us

profile of v7, /device:TPU:1, one launch (start us, length us, event | category | flops | bytes accessed | tf_op | source)
XLA Modules:
  0.0 244.5 jit_solution(5918364573007611418)
XLA Ops:
  0.0 0.7 reduce
  0.7 0.1 reshape.9
  0.8 1.3 pad_add_fusion.number_ref
  2.1 240.5 %run_layers.1 = bf16[12,8,16,128]{3,2,1,0:T(8,128)(2,1)} custom-call(s32[16,128]{1,0:T(8,128)} %pad_add_fusion.number_ref, bf16[12,8,16,384]{3,2,1,0:T(8,128)(2,1)} %bitcast.6, bf16[12,24,128,128]{3,2,1,0:T(8,128)(2,1)} %tiles_ref.1, bf16[2,64,128,384]{3,2,1,0:T(8,128)(2,1)} %bitcast.4, bf16[2,384,384]{2,1,0:T(8,128)(2,1)} %weight_ref.1), custom_call_target="tpu_custom_call" | custom-call | tf_op jit(solution)/shard_map/run_layers/pallas_call | solution.py:483
  242.6 1.9 copy.8
